TPU v7x, 128 devices: a whole 4x4x4 slice. The times are simulated.
128 devices in a mesh: head: 4 (over x), ctx: 32 (over z, y, core).
Axes of the slice: x: 4, y: 4, z: 4, core: 2. Of those that a mesh axis runs over, the one named last changes fastest.
Arguments:
- queries: bfloat16 [16384, 4096], P('ctx', 'head'), may hold values from -4 to 4
- key_input: bfloat16 [16384, 4096], P('ctx', 'head'), may hold values from -4 to 4
- value_input: bfloat16 [16384, 4096], P('ctx', 'head'), may hold values from -32 to 32
- norm_gain: float32 [4096], P('head'), may hold values from 0.1 to 1.9
- out_grad: bfloat16 [16384, 4096], P('ctx', 'head'), may hold values from -6 to 6
- doc_lengths: int32 [8], replicated, may hold values from 1 to 64, 128 in all
Outputs:
- normed_out: bfloat16 [16384, 4096], P('ctx', 'head')
- query_grad: bfloat16 [16384, 4096], P('ctx', 'head')
- key_grad: bfloat16 [16384, 4096], P('ctx', 'head')
- value_grad: bfloat16 [16384, 4096], P('ctx', 'head')
Inputs may be any that keep to these rules, and one draw needn't show every extreme that they name: `doc_lengths`: the lengths of the slab's 8 documents in order, in units of 128 tokens; they sum to 128, and the longest has exactly 64.
All inputs are finite; a program needn't handle non-finite values.
Results may differ from a plain program's by a relative error of at most 0.0053.
Values sent between devices are 32-bit elements; how exact they have to be, the bound alone decides.
No kernel may reach another device: no remote copies, remote signals or barrier semaphores. Data moves between devices by JAX's collectives and lax.ppermute only.
A program may use at most 128 MiB of HBM per device.

v0:
```python
import jax
import jax.numpy as jnp
from jax import lax
from jax.sharding import PartitionSpec as P

HEADS = 32
HEAD_DIM = 128
BLOCK = 512
GRAIN = 128


EPSILON = 1e-06


def prefix(part, axis, combine, identity, reverse):
    count = lax.axis_size(axis)
    place = lax.axis_index(axis)
    ahead = count - 1 - place if reverse else place
    gathered = jax.tree.map(lambda a: lax.all_gather(a, axis), part)
    state = jax.tree.map(lambda a, e: jnp.zeros_like(a) + jnp.asarray(e, a.dtype), part, identity)

    def one(lap, state):
        source = count - 1 - lap if reverse else lap
        return combine(
            state, jax.tree.map(lambda a: lax.dynamic_index_in_dim(a, source, 0, False), gathered)
        )

    return lax.fori_loop(0, ahead, one, state)


def doc_index(starts_at, grain_ids, total_grains):
    counted = jnp.sum(
        (starts_at[None, :] <= grain_ids[:, None]).astype(jnp.int32), axis=1, dtype=jnp.int32
    )
    return counted - 1 + (grain_ids >= total_grains).astype(jnp.int32)


def join_reset(earlier, nearer):
    return (jnp.maximum(earlier[0], nearer[0]), nearer[1] + (1.0 - nearer[0]) * earlier[1])


def masked_round(values_in, allowed):
    return jnp.where(allowed[None], values_in, 0.0).astype(jnp.bfloat16)


def on_device(queries, key_input, value_input, norm_gain, out_grad, doc_lengths):
    highest = lax.Precision.HIGHEST
    rows_here = queries.shape[0]
    width_here = queries.shape[1]
    heads_here = width_here // HEAD_DIM
    width_all = HEADS * HEAD_DIM
    grains_here = rows_here // GRAIN
    blocks_here = rows_here // BLOCK
    ctx_count = lax.axis_size("ctx")
    total_grains = ctx_count * grains_here
    device = lax.axis_index("ctx")
    first_grain = device * grains_here
    starts_at = jnp.cumsum(doc_lengths, dtype=jnp.int32) - doc_lengths
    token_docs = doc_index(
        starts_at, first_grain + jnp.arange(rows_here, dtype=jnp.int32) // GRAIN, total_grains
    )
    edge_grains = jnp.stack([first_grain - 1, first_grain + grains_here])
    edge_docs = doc_index(starts_at, edge_grains, total_grains)
    before_doc = edge_docs[0]
    after_doc = edge_docs[1]
    query_heads = queries.reshape(rows_here, heads_here, HEAD_DIM)
    key_heads = key_input.reshape(rows_here, heads_here, HEAD_DIM)
    value_heads = value_input.reshape(rows_here, heads_here, HEAD_DIM)
    causal = jnp.arange(BLOCK)[:, None] >= jnp.arange(BLOCK)[None, :]
    state_sum = jnp.zeros((heads_here, HEAD_DIM, HEAD_DIM), jnp.float32)
    query_block = query_heads
    key_block = key_heads
    value_block = value_heads
    seg_docs = token_docs
    allowed = causal & (seg_docs[:, None] == seg_docs[None, :])
    scores = jnp.einsum("ihd,jhd->hij", query_block, key_block, preferred_element_type=jnp.float32)
    weights = masked_round(scores, allowed)
    local_parts = [
        jnp.einsum("hij,jhe->ihe", weights, value_block, preferred_element_type=jnp.float32)
    ]
    entry_states = [state_sum]
    entry_docs = [before_doc]
    weights_kept = [weights]
    masks_kept = [allowed]
    last_doc = seg_docs[-1]
    tail_keys = key_block * (seg_docs == last_doc).astype(jnp.bfloat16)[:, None, None]
    state_sum = jnp.where(last_doc == before_doc, state_sum, 0.0) + jnp.einsum(
        "jhd,jhe->hde", tail_keys, value_block, preferred_element_type=jnp.float32
    )
    forward_flag = (token_docs[-1] != before_doc).astype(jnp.float32).reshape(1)
    incoming = prefix(
        (forward_flag, state_sum),
        "ctx",
        join_reset,
        (jnp.zeros((1,), jnp.float32), jnp.zeros_like(state_sum)),
        False,
    )[1]
    segment = 0
    entry_total = (
        entry_states[segment] + jnp.where(entry_docs[segment] == before_doc, 1.0, 0.0) * incoming
    )
    entry_totals = [entry_total]
    follows = (token_docs == entry_docs[segment]).astype(jnp.float32)
    mixed_parts = local_parts[segment] + follows[:, None, None] * jnp.einsum(
        "ihd,hde->ihe", query_heads.astype(jnp.float32), entry_total, precision=highest
    )
    flat_mixed = mixed_parts.reshape(rows_here, width_here)
    scaled_grad = norm_gain[None, :] * out_grad.astype(jnp.float32)
    square_sum = lax.psum(jnp.sum(flat_mixed * flat_mixed, axis=1), "head")
    root_mean = jnp.sqrt(square_sum / width_all + EPSILON)
    normed = flat_mixed / root_mean[:, None]
    dot_mean = lax.psum(jnp.sum(normed * scaled_grad, axis=1), "head") / width_all
    normed_out = (normed * norm_gain[None, :]).astype(jnp.bfloat16)
    grad_mixed = ((scaled_grad - normed * dot_mean[:, None]) / root_mean[:, None]).astype(
        jnp.bfloat16
    )
    grad_heads = grad_mixed.reshape(rows_here, heads_here, HEAD_DIM)
    upper_sum = jnp.zeros((heads_here, HEAD_DIM, HEAD_DIM), jnp.float32)
    following = after_doc
    query_parts = [None] * blocks_here
    key_parts = [None] * blocks_here
    value_parts = [None] * blocks_here
    upper_states = [None] * blocks_here
    upper_docs = [None] * blocks_here
    for segment in reversed(range(blocks_here)):
        query_block = query_heads
        key_block = key_heads
        value_block = value_heads
        seg_docs = token_docs
        grad_scores = jnp.einsum(
            "ihe,jhe->hij", grad_heads, value_block, preferred_element_type=jnp.float32
        )
        grad_weights = masked_round(grad_scores, masks_kept[segment])
        follows = (seg_docs == entry_docs[segment]).astype(jnp.float32)[:, None, None]
        query_part = jnp.einsum(
            "hij,jhd->ihd", grad_weights, key_block, preferred_element_type=jnp.float32
        )
        query_parts[segment] = query_part + follows * jnp.einsum(
            "hde,ihe->ihd", entry_totals[segment], grad_heads.astype(jnp.float32), precision=highest
        )
        key_parts[segment] = jnp.einsum(
            "hij,ihd->jhd", grad_weights, query_block, preferred_element_type=jnp.float32
        )
        value_parts[segment] = jnp.einsum(
            "hij,ihe->jhe", weights_kept[segment], grad_heads, preferred_element_type=jnp.float32
        )
        upper_states[segment] = upper_sum
        upper_docs[segment] = following
        first_doc = seg_docs[0]
        head_queries = query_block * (seg_docs == first_doc).astype(jnp.bfloat16)[:, None, None]
        upper_sum = jnp.where(first_doc == following, upper_sum, 0.0) + jnp.einsum(
            "ihd,ihe->hde", head_queries, grad_heads, preferred_element_type=jnp.float32
        )
        following = first_doc
    backward_flag = (token_docs[0] != after_doc).astype(jnp.float32).reshape(1)
    suffix_in = prefix(
        (backward_flag, upper_sum),
        "ctx",
        join_reset,
        (jnp.zeros((1,), jnp.float32), jnp.zeros_like(upper_sum)),
        True,
    )[1]
    segment = 0
    upper_total = (
        upper_states[segment] + jnp.where(upper_docs[segment] == after_doc, 1.0, 0.0) * suffix_in
    )
    leads_into = (token_docs == upper_docs[segment]).astype(jnp.float32)[:, None, None]
    key_final = key_parts[segment] + leads_into * jnp.einsum(
        "hde,jhe->jhd", upper_total, value_heads.astype(jnp.float32), precision=highest
    )
    value_final = value_parts[segment] + leads_into * jnp.einsum(
        "hde,jhd->jhe", upper_total, key_heads.astype(jnp.float32), precision=highest
    )
    query_grad = query_parts[0].reshape(rows_here, width_here).astype(jnp.bfloat16)
    key_grad = key_final.reshape(rows_here, width_here).astype(jnp.bfloat16)
    value_grad = value_final.reshape(rows_here, width_here).astype(jnp.bfloat16)
    return (normed_out, query_grad, key_grad, value_grad)


def solution(mesh):
    in_specs = (
        P("ctx", "head"),
        P("ctx", "head"),
        P("ctx", "head"),
        P("head"),
        P("ctx", "head"),
        P(),
    )
    out_specs = (P("ctx", "head"), P("ctx", "head"), P("ctx", "head"), P("ctx", "head"))
    return jax.shard_map(
        on_device, mesh=mesh, in_specs=in_specs, out_specs=out_specs, check_vma=False
    )
```

profile of v0, /device:TPU:1, one launch (start us, length us, event | category | flops | bytes accessed | tf_op | source)
XLA Modules:
  0.0 370.6 jit_solution(8158638619154520649)
XLA Ops:
  13.3 1.9 compare_convert_fusion
  22.9 66.0 %all-reduce.2 = (f32[32]{0:T(128)S(1)}, f32[32]{0:T(128)S(1)}) all-reduce(f32[32]{0:T(128)S(1)} %dynamic-update-slice, f32[32]{0:T(128)S(1)} %dynamic-update-slice.1), channel_id=1, replica_groups=mesh['head'=4,'ctx'=32] {'ctx'}, use_global_device_ids=true, to_apply=%add | all-reduce | flops 64 | bytes 512
  90.5 2.0 copy-done.1
  92.4 2.9 fusion.1
  95.3 2.5 while.26
  97.9 4.1 %multiply_reduce_fusion.1 = (f32[512]{0:T(512)S(1)}, f32[512,8,128]{0,2,1:T(8,128)}) fusion(f32[8,128,128]{2,1,0:T(8,128)S(1)} %get-tuple-element.132, bf16[512,8,128]{0,2,1:T(8,128)(2,1)S(1)} %bitcast.103, f32[512]{0:T(512)S(1)} %get-tuple-element.174, f32[8,512,128]{1,2,0:T(8,128)} %fusion.1), kind=kOutput, calls=%fused_computation.15 | convolution fusion | flops 807403008 | bytes 5771264 | tf_op jit(solution)/shard_map/ihd,hde->ihe/dot_general | solution.py:104
  102.0 8.5 %psum.14 = f32[512]{0:T(512)S(1)} all-reduce(f32[512]{0:T(512)S(1)} %get-tuple-element.179), channel_id=1, replica_groups=mesh['head'=4,'ctx'=32] {'head'}, use_global_device_ids=true, to_apply=%region_6.7 | all-reduce | flops 512 | bytes 4096 | tf_op jit(solution)/shard_map/psum | solution.py:109
  110.5 2.9 copy.61
  113.4 2.4 multiply_reduce_fusion
  115.8 6.2 %psum.15 = f32[512]{0:T(512)S(1)} all-reduce(f32[512]{0:T(512)S(1)} %multiply_reduce_fusion), channel_id=1, replica_groups=mesh['head'=4,'ctx'=32] {'head'}, use_global_device_ids=true, to_apply=%region_8.9 | all-reduce | flops 512 | bytes 4096 | tf_op jit(solution)/shard_map/psum | solution.py:112
  122.0 3.8 %divide_convert_fusion = (bf16[512,1024]{1,0:T(8,128)(2,1)}, bf16[512,1024]{1,0:T(8,128)(2,1)}) fusion(bf16[512,1024]{1,0:T(8,128)(2,1)} %param.14, f32[512]{0:T(512)S(1)} %broadcast_multiply_fusion, f32[1024]{0:T(1024)S(1)} %copy-done.10, f32[512]{0:T(512)S(1)} %add_sqrt_fusion, f32[512,1024]{1,0:T(8,128)} %copy.61), kind=kLoop, calls=%fused_computation.11 | loop fusion | flops 4718592 | bytes 5251072 | tf_op jit(solution)/shard_map/convert_element_type | solution.py:114
  125.8 2.3 copy.79
  128.1 2.5 fusion.10
  130.6 2.7 select_convert_fusion
  135.4 2.2 add_convert_fusion.1
  137.5 2.4 copy.73
  139.9 4.3 %fusion.33 = f32[8,128,512]{2,1,0:T(8,128)} fusion(bf16[512,8,128]{0,2,1:T(8,128)(2,1)S(1)} %bitcast.109, bf16[8,512,512]{2,1,0:T(8,128)(2,1)} %copy-done.1), kind=kOutput, calls=%fused_computation.66 | convolution fusion | flops 536870912 | bytes 7340032 | tf_op jit(solution)/shard_map/hij,ihe->jhe/dot_general | solution.py:144
  144.1 133.0 %all-gather.7.cloned.1.call-done = f32[256,128,128]{2,1,0:T(8,128)} async-done(((f32[8,128,128]{2,1,0:T(8,128)}), f32[256,128,128]{2,1,0:T(8,128)}) %all-gather.7.cloned.1.call-update) | async-done | bytes 16777232 | tf_op jit(solution)/shard_map/all_gather | solution.py:19
  277.2 74.9 %while.27 = (s32[]{:T(128)}, f32[8,128,128]{2,1,0:T(8,128)S(1)}, s32[]{:T(128)}, f32[32,8,128,128]{3,2,1,0:T(8,128)}, f32[32,1]{0,1:T(1,128)S(1)}, /*index=5*/s32[]{:T(128)}, s32[]{:T(128)}, s32[]{:T(128)}, s32[]{:T(128)}) while((s32[]{:T(128)}, f32[8,128,128]{2,1,0:T(8,128)S(1)}, s32[]{:T(128)}, f32[32,8,128,128]{3,2,1,0:T(8,128)}, ...), condition=%wide.region_10.11_spmd, body=%wide.region_9.10_spmd.sunk | while | flops 262151 | bytes 1573031 | solution.py:28
  300.3 1.9 bitcast_add_fusion.7
  352.1 2.3 fusion.3
  354.4 2.1 add_convert_fusion
  356.6 2.3 copy.75
  358.8 3.6 fusion
  (116 shorter events, 90.8 us)
Async XLA Ops:
  7.2 8.1 %copy-start = (bf16[512,1024]{1,0:T(8,128)(2,1)S(1)}, bf16[512,1024]{1,0:T(8,128)(2,1)}, u32[]{:S(2)}) copy-start(bf16[512,1024]{1,0:T(8,128)(2,1)} %param.12) | copy-start | bytes 3145732
  7.2 88.1 %all-gather.5.cloned.1.call-start = ((), (), s32[]{:S(2)}) async-start(), calls=%async_computation | async-start | bytes 17301504 | tf_op jit(solution)/shard_map/all_gather | solution.py:19
  13.3 6.0 %copy-start.6 = (bf16[512,8,128]{0,2,1:T(8,128)(2,1)}, bf16[512,8,128]{0,2,1:T(8,128)(2,1)S(1)}, u32[]{:S(2)}) copy-start(bf16[512,8,128]{0,2,1:T(8,128)(2,1)S(1)} %copy.57) | copy-start | bytes 3145732
  15.3 5.5 %copy-start.11 = (u32[128]{0:T(128)S(1)}, u32[128]{0:T(128)}, u32[]{:S(2)}) copy-start(u32[128]{0:T(128)} %constant.125) | copy-start | bytes 1540
  16.5 72.5 %copy-start.8 = (bf16[512,1024]{1,0:T(8,128)(2,1)S(1)}, bf16[512,1024]{1,0:T(8,128)(2,1)}, u32[]{:S(2)}) copy-start(bf16[512,1024]{1,0:T(8,128)(2,1)} %param.11) | copy-start | bytes 3145732
  16.6 260.6 %all-gather.7.cloned.1.call-start = ((), (), s32[]{:S(2)}) async-start(), calls=%async_computation.1 | async-start | bytes 17301504 | tf_op jit(solution)/shard_map/all_gather | solution.py:19
  90.5 2.0 copy-start.1
  110.5 2.9 copy-start.10
  130.6 2.7 copy-start.7
  133.3 1.9 copy-start.2
  133.4 2.0 copy-start.3
  137.5 2.4 copy-start.4
  352.1 2.3 copy-start.5
  352.1 2.3 copy-start.9
Sparse Core Ops, SparseCore 0:
  16.7 76.7 all-gather.4
  130.7 146.4 all-gather.6
where the time goes:
time: 374 us; the launch traced here: 371 us
  waiting for transfers between devices  133 us (36%)
  other arithmetic  87.7 us (23%)
  blocking collectives  80.7 us (22%)
  matrix products  30.8 us (8%)
  local copies, waits for them, and re-layouts  20.7 us (6%)
  between operations  16.9 us (5%)
    all_gather x2, waiting for transfers between devices, prefix(): gathered = jax.tree.map(lambda a: lax.all_gather(a, axis), part)  133 us
    unnamed x1, blocking collectives  66 us
    add x31, other arithmetic, join_reset(): nearer[1] + (1.0 - nearer[0]) * earlier[1]  58.5 us
    sub x31, other arithmetic, join_reset(): 1.0 - nearer[0]  18.2 us
    unnamed x33, local copies, waits for them, and re-layouts  12 us
    psum x1, blocking collectives, on_device(): square_sum = lax.psum(jnp.sum(flat_mixed * flat_mixed, axis=1), 'head')  8.5 us
  transfers between devices with their start and end apart: 2, of which 1 were waited for; matrix products, arithmetic and copies ran while one was open for 6% of the time, Pallas kernels for 0%

commit v1 on v0

--- a/solution.py
+++ b/solution.py
@@ -55,7 +55,10 @@
     total_grains = ctx_count * grains_here
     device = lax.axis_index("ctx")
     first_grain = device * grains_here
-    starts_at = jnp.cumsum(doc_lengths, dtype=jnp.int32) - doc_lengths
+    slots = jnp.arange(doc_lengths.shape[0])
+    starts_at = jnp.sum(
+        jnp.where(slots[None, :] < slots[:, None], doc_lengths[None, :], 0), axis=1, dtype=jnp.int32
+    )
     token_docs = doc_index(
         starts_at, first_grain + jnp.arange(rows_here, dtype=jnp.int32) // GRAIN, total_grains
     )

time: 374 us -> 373 us (level)
  no operation moved by 1% of the time
where the time goes in v1:
time: 373 us; the launch traced here: 370 us
  waiting for transfers between devices  133 us (36%)
  other arithmetic  87 us (23%)
  blocking collectives  81 us (22%)
  matrix products  30.8 us (8%)
  local copies, waits for them, and re-layouts  20.6 us (6%)
  between operations  16.9 us (5%)
    all_gather x2, waiting for transfers between devices, prefix(): gathered = jax.tree.map(lambda a: lax.all_gather(a, axis), part)  133 us
    unnamed x1, blocking collectives  66 us
    add x31, other arithmetic, join_reset(): nearer[1] + (1.0 - nearer[0]) * earlier[1]  58.5 us
    sub x31, other arithmetic, join_reset(): 1.0 - nearer[0]  18.2 us
    unnamed x33, local copies, waits for them, and re-layouts  12 us
    psum x1, blocking collectives, on_device(): square_sum = lax.psum(jnp.sum(flat_mixed * flat_mixed, axis=1), 'head')  8.84 us
  transfers between devices with their start and end apart: 2, of which 1 were waited for; matrix products, arithmetic and copies ran while one was open for 6% of the time, Pallas kernels for 0%

profile of v1, /device:TPU:1, one launch (start us, length us, event | category | flops | bytes accessed | tf_op | source)
XLA Modules:
  0.0 369.7 jit_solution(13711919093524669658)
XLA Ops:
  22.0 66.0 %all-reduce.2 = (f32[32]{0:T(128)S(1)}, f32[32]{0:T(128)S(1)}) all-reduce(f32[32]{0:T(128)S(1)} %dynamic-update-slice, f32[32]{0:T(128)S(1)} %dynamic-update-slice.1), channel_id=1, replica_groups=mesh['head'=4,'ctx'=32] {'ctx'}, use_global_device_ids=true, to_apply=%add | all-reduce | flops 64 | bytes 512
  89.6 2.0 copy-done.1
  91.6 2.9 fusion.1
  94.5 2.5 while.26
  97.0 4.1 %multiply_reduce_fusion.1 = (f32[512]{0:T(512)S(1)}, f32[512,8,128]{0,2,1:T(8,128)}) fusion(f32[8,128,128]{2,1,0:T(8,128)S(1)} %get-tuple-element.132, bf16[512,8,128]{0,2,1:T(8,128)(2,1)S(1)} %bitcast.100, f32[512]{0:T(512)S(1)} %get-tuple-element.174, f32[8,512,128]{1,2,0:T(8,128)} %fusion.1), kind=kOutput, calls=%fused_computation.15 | convolution fusion | flops 807403008 | bytes 5771264 | tf_op jit(solution)/shard_map/ihd,hde->ihe/dot_general | solution.py:107
  101.1 8.8 %psum.14 = f32[512]{0:T(512)S(1)} all-reduce(f32[512]{0:T(512)S(1)} %get-tuple-element.179), channel_id=1, replica_groups=mesh['head'=4,'ctx'=32] {'head'}, use_global_device_ids=true, to_apply=%region_6.7 | all-reduce | flops 512 | bytes 4096 | tf_op jit(solution)/shard_map/psum | solution.py:112
  110.0 2.9 copy.61
  112.9 2.4 multiply_reduce_fusion
  115.3 6.2 %psum.15 = f32[512]{0:T(512)S(1)} all-reduce(f32[512]{0:T(512)S(1)} %multiply_reduce_fusion), channel_id=1, replica_groups=mesh['head'=4,'ctx'=32] {'head'}, use_global_device_ids=true, to_apply=%region_8.9 | all-reduce | flops 512 | bytes 4096 | tf_op jit(solution)/shard_map/psum | solution.py:115
  121.5 3.8 %divide_convert_fusion = (bf16[512,1024]{1,0:T(8,128)(2,1)}, bf16[512,1024]{1,0:T(8,128)(2,1)}) fusion(bf16[512,1024]{1,0:T(8,128)(2,1)} %param.14, f32[512]{0:T(512)S(1)} %broadcast_multiply_fusion, f32[1024]{0:T(1024)S(1)} %copy-done.10, f32[512]{0:T(512)S(1)} %add_sqrt_fusion, f32[512,1024]{1,0:T(8,128)} %copy.61), kind=kLoop, calls=%fused_computation.11 | loop fusion | flops 4718592 | bytes 5251072 | tf_op jit(solution)/shard_map/convert_element_type | solution.py:117
  125.3 2.3 copy.79
  127.6 2.5 fusion.10
  130.1 2.7 select_convert_fusion
  134.9 2.2 add_convert_fusion.1
  137.0 2.4 copy.73
  139.4 4.3 %fusion.33 = f32[8,128,512]{2,1,0:T(8,128)} fusion(bf16[512,8,128]{0,2,1:T(8,128)(2,1)S(1)} %bitcast.106, bf16[8,512,512]{2,1,0:T(8,128)(2,1)} %copy-done.1), kind=kOutput, calls=%fused_computation.67 | convolution fusion | flops 536870912 | bytes 7340032 | tf_op jit(solution)/shard_map/hij,ihe->jhe/dot_general | solution.py:147
  143.6 132.6 %all-gather.7.cloned.1.call-done = f32[256,128,128]{2,1,0:T(8,128)} async-done(((f32[8,128,128]{2,1,0:T(8,128)}), f32[256,128,128]{2,1,0:T(8,128)}) %all-gather.7.cloned.1.call-update) | async-done | bytes 16777232 | tf_op jit(solution)/shard_map/all_gather | solution.py:19
  276.3 74.9 %while.27 = (s32[]{:T(128)}, f32[8,128,128]{2,1,0:T(8,128)S(1)}, s32[]{:T(128)}, f32[32,8,128,128]{3,2,1,0:T(8,128)}, f32[32,1]{0,1:T(1,128)S(1)}, /*index=5*/s32[]{:T(128)}, s32[]{:T(128)}, s32[]{:T(128)}, s32[]{:T(128)}) while((s32[]{:T(128)}, f32[8,128,128]{2,1,0:T(8,128)S(1)}, s32[]{:T(128)}, f32[32,8,128,128]{3,2,1,0:T(8,128)}, ...), condition=%wide.region_10.11_spmd, body=%wide.region_9.10_spmd.sunk | while | flops 262151 | bytes 1573031 | solution.py:28
  309.3 1.9 bitcast_add_fusion.7
  319.3 1.9 bitcast_add_fusion.7
  351.2 2.3 fusion.3
  353.5 2.1 add_convert_fusion
  355.7 2.3 copy.75
  358.0 3.6 fusion
  (115 shorter events, 90.1 us)
Async XLA Ops:
  7.2 7.3 %copy-start = (bf16[512,1024]{1,0:T(8,128)(2,1)S(1)}, bf16[512,1024]{1,0:T(8,128)(2,1)}, u32[]{:S(2)}) copy-start(bf16[512,1024]{1,0:T(8,128)(2,1)} %param.12) | copy-start | bytes 3145732
  7.2 87.3 %all-gather.5.cloned.1.call-start = ((), (), s32[]{:S(2)}) async-start(), calls=%async_computation | async-start | bytes 17301504 | tf_op jit(solution)/shard_map/all_gather | solution.py:19
  12.6 5.9 %copy-start.6 = (bf16[512,8,128]{0,2,1:T(8,128)(2,1)}, bf16[512,8,128]{0,2,1:T(8,128)(2,1)S(1)}, u32[]{:S(2)}) copy-start(bf16[512,8,128]{0,2,1:T(8,128)(2,1)S(1)} %copy.57) | copy-start | bytes 3145732
  14.5 5.5 %copy-start.11 = (u32[128]{0:T(128)S(1)}, u32[128]{0:T(128)}, u32[]{:S(2)}) copy-start(u32[128]{0:T(128)} %constant.122) | copy-start | bytes 1540
  15.7 72.5 %copy-start.8 = (bf16[512,1024]{1,0:T(8,128)(2,1)S(1)}, bf16[512,1024]{1,0:T(8,128)(2,1)}, u32[]{:S(2)}) copy-start(bf16[512,1024]{1,0:T(8,128)(2,1)} %param.11) | copy-start | bytes 3145732
  15.8 260.5 %all-gather.7.cloned.1.call-start = ((), (), s32[]{:S(2)}) async-start(), calls=%async_computation.1 | async-start | bytes 17301504 | tf_op jit(solution)/shard_map/all_gather | solution.py:19
  89.6 2.0 copy-start.1
  110.0 2.9 copy-start.10
  130.1 2.7 copy-start.7
  132.8 1.9 copy-start.2
  132.8 2.0 copy-start.3
  137.0 2.4 copy-start.4
  351.2 2.3 copy-start.5
  351.2 2.3 copy-start.9
Sparse Core Ops, SparseCore 0:
  15.9 76.7 all-gather.4
  130.2 145.9 all-gather.6

commit v2 on v0

v2 whole, which is shorter than its diff:
```python
import jax
import jax.numpy as jnp
from jax import lax
from jax.experimental import pallas as pl
from jax.experimental.pallas import tpu as pltpu
from jax.sharding import PartitionSpec as P

HEADS = 32
HEAD_DIM = 128
BLOCK = 512
GRAIN = 128
NDOCS = 8
GRAINS = BLOCK // GRAIN
WIDTH = HEADS * HEAD_DIM
HALF = BLOCK // 2
EPSILON = 1e-06

F32 = jnp.float32
BF16 = jnp.bfloat16


def dot(a, b, dims):
    return lax.dot_general(a, b, (dims, ((), ())), preferred_element_type=F32)


NN = ((1,), (0,))
NT = ((1,), (1,))
TN = ((0,), (0,))


def grain_docs(lengths_ref):
    total = lax.axis_size("ctx") * GRAINS
    first = lax.axis_index("ctx") * GRAINS
    starts = [jnp.int32(0)]
    for i in range(NDOCS - 1):
        starts.append(starts[-1] + lengths_ref[i])
    docs = []
    for k in range(-1, GRAINS + 1):
        grain = first + k
        count = (grain >= total).astype(jnp.int32) - 1
        for s in starts:
            count = count + (s <= grain).astype(jnp.int32)
        docs.append(count)
    return docs


def rows_equal(docs, doc, cols, dtype):
    parts = [
        jnp.full((GRAIN, cols), (docs[1 + g] == doc).astype(F32), F32) for g in range(GRAINS)
    ]
    return jnp.concatenate(parts, axis=0).astype(dtype)


def pair_mask(docs):
    rows = lax.broadcasted_iota(jnp.int32, (GRAIN, GRAIN), 0)
    cols = lax.broadcasted_iota(jnp.int32, (GRAIN, GRAIN), 1)
    lower = jnp.where(rows >= cols, 1.0, 0.0).astype(F32)
    out = []
    for i in range(GRAINS):
        line = []
        for j in range(GRAINS):
            if j < i:
                same = (docs[1 + i] == docs[1 + j]).astype(F32)
                line.append(jnp.full((GRAIN, GRAIN), same, F32))
            elif j == i:
                line.append(lower)
            else:
                line.append(jnp.zeros((GRAIN, GRAIN), F32))
        out.append(jnp.concatenate(line, axis=1))
    return jnp.concatenate(out, axis=0).astype(BF16)


def split_rows(x):
    high = x.astype(BF16)
    low = (x - high.astype(F32)).astype(BF16)
    return jnp.concatenate([high, low], axis=0)


def split_cols(x):
    high = x.astype(BF16)
    low = (x - high.astype(F32)).astype(BF16)
    return jnp.concatenate([high, low], axis=1)


def twice(x):
    return jnp.concatenate([x, x], axis=1)


def head_cols(h):
    return slice(h * HEAD_DIM, (h + 1) * HEAD_DIM)


STEP_HEADS = 2
STEP_COLS = STEP_HEADS * HEAD_DIM


def state_kernel(lengths_ref, key_ref, value_ref, out_ref):
    docs = grain_docs(lengths_ref)
    mask = rows_equal(docs, docs[GRAINS], HEAD_DIM, BF16)
    for h in range(STEP_HEADS):
        keys = key_ref[:, head_cols(h)] * mask
        out_ref[h * HEAD_DIM : (h + 1) * HEAD_DIM, :] = dot(keys, value_ref[:, head_cols(h)], TN)


def local_kernel(lengths_ref, query_ref, key_ref, value_ref, out_ref, mask_ref):
    @pl.when(pl.program_id(0) == 0)
    def _():
        mask_ref[...] = pair_mask(grain_docs(lengths_ref))

    for h in range(STEP_HEADS):
        cols = head_cols(h)
        for r in range(2):
            rows = slice(r * HALF, (r + 1) * HALF)
            upto = (r + 1) * HALF
            weights = dot(query_ref[rows, cols], key_ref[:upto, cols], NT).astype(BF16)
            weights = weights * mask_ref[rows, :upto]
            out_ref[rows, cols] = dot(weights, value_ref[:upto, cols], NN)


def scan_kernel(lengths_ref, parts_ref, out_ref, keep_ref, *, backward):
    count = parts_ref.shape[0]
    for b in range(count):
        keep_ref[b] = jnp.int32(1)
    start = jnp.int32(0)
    for i in range(NDOCS - 1):
        start = start + lengths_ref[i]
        place = (start - 1) // GRAINS if backward else start // GRAINS
        keep_ref[place] = jnp.int32(0)
    running = jnp.zeros(parts_ref.shape[1:], F32)
    for b in reversed(range(count)) if backward else range(count):
        out_ref[b] = running
        running = parts_ref[b] + keep_ref[b].astype(F32) * running


def mixed_kernel(
    lengths_ref, query_ref, local_ref, state_ref, grad_ref, gain_ref, mixed_ref, sums_ref, acc_ref
):
    step = pl.program_id(0)
    docs = grain_docs(lengths_ref)
    mask = rows_equal(docs, docs[0], HEAD_DIM, BF16)
    squares = jnp.zeros((BLOCK, HEAD_DIM), F32)
    dots = jnp.zeros((BLOCK, HEAD_DIM), F32)
    for h in range(STEP_HEADS):
        cols = head_cols(h)
        state = split_rows(state_ref[h * HEAD_DIM : (h + 1) * HEAD_DIM, :])
        mixed = local_ref[:, cols] + dot(twice(query_ref[:, cols] * mask), state, NN)
        mixed_ref[:, cols] = mixed
        squares = squares + mixed * mixed
        dots = dots + mixed * (gain_ref[:, cols] * grad_ref[:, cols].astype(F32))

    @pl.when(step == 0)
    def _():
        acc_ref[0] = squares
        acc_ref[1] = dots

    @pl.when(step > 0)
    def _():
        acc_ref[0] += squares
        acc_ref[1] += dots

    @pl.when(step == pl.num_programs(0) - 1)
    def _():
        for n in range(2):
            sums_ref[n : n + 1, :] = jnp.sum(acc_ref[n].T, axis=0, keepdims=True)


def grad_kernel(
    lengths_ref,
    sums_ref,
    sums1_ref,
    sums2_ref,
    sums3_ref,
    mixed_ref,
    grad_ref,
    gain_ref,
    query_ref,
    normed_ref,
    grad_mixed_ref,
    upper_ref,
    scale_ref,
):
    @pl.when(pl.program_id(0) == 0)
    def _():
        total = sums_ref[...] + sums1_ref[...] + sums2_ref[...] + sums3_ref[...]
        root = jnp.sqrt(total[0:1, :] / WIDTH + EPSILON)
        inverse = 1.0 / root
        dots = total[1:2, :] * inverse / WIDTH
        scale_ref[0] = jnp.broadcast_to(inverse, (HEAD_DIM, BLOCK)).T
        scale_ref[1] = jnp.broadcast_to(dots, (HEAD_DIM, BLOCK)).T

    docs = grain_docs(lengths_ref)
    mask = rows_equal(docs, docs[1], HEAD_DIM, BF16)
    inverse = scale_ref[0]
    dots = scale_ref[1]
    for h in range(STEP_HEADS):
        cols = head_cols(h)
        gain = gain_ref[:, cols]
        normed = mixed_ref[:, cols] * inverse
        normed_ref[:, cols] = (normed * gain).astype(BF16)
        scaled = gain * grad_ref[:, cols].astype(F32)
        grad_mixed = ((scaled - normed * dots) * inverse).astype(BF16)
        grad_mixed_ref[:, cols] = grad_mixed
        upper_ref[h * HEAD_DIM : (h + 1) * HEAD_DIM, :] = dot(
            query_ref[:, cols] * mask, grad_mixed, TN
        )


def back_kernel(
    lengths_ref,
    query_ref,
    key_ref,
    value_ref,
    grad_ref,
    state_ref,
    query_out_ref,
    key_out_ref,
    value_out_ref,
    mask_ref,
):
    docs = grain_docs(lengths_ref)

    @pl.when(pl.program_id(0) == 0)
    def _():
        mask_ref[...] = pair_mask(docs)

    follows = rows_equal(docs, docs[0], HEAD_DIM, BF16)
    for h in range(STEP_HEADS):
        cols = head_cols(h)
        state = split_cols(state_ref[h * HEAD_DIM : (h + 1) * HEAD_DIM, :])
        from_state = dot(twice(grad_ref[:, cols] * follows), state, NT)
        for r in range(2):
            rows = slice(r * HALF, (r + 1) * HALF)
            upto = (r + 1) * HALF
            mask = mask_ref[rows, :upto]
            weights = dot(query_ref[rows, cols], key_ref[:upto, cols], NT).astype(BF16) * mask
            grads = dot(grad_ref[rows, cols], value_ref[:upto, cols], NT).astype(BF16) * mask
            query_out_ref[rows, cols] = (
                dot(grads, key_ref[:upto, cols], NN) + from_state[rows, :]
            ).astype(BF16)
            key_part = dot(grads, query_ref[rows, cols], TN)
            value_part = dot(weights, grad_ref[rows, cols], TN)
            if r == 0:
                key_out_ref[:HALF, cols] = key_part
                value_out_ref[:HALF, cols] = value_part
            else:
                key_out_ref[:HALF, cols] += key_part[:HALF, :]
                value_out_ref[:HALF, cols] += value_part[:HALF, :]
                key_out_ref[HALF:, cols] = key_part[HALF:, :]
                value_out_ref[HALF:, cols] = value_part[HALF:, :]


def final_kernel(
    lengths_ref, key_ref, value_ref, key_part_ref, value_part_ref, upper_ref, key_out_ref, value_out_ref
):
    docs = grain_docs(lengths_ref)
    leads = rows_equal(docs, docs[GRAINS + 1], HEAD_DIM, BF16)
    for h in range(STEP_HEADS):
        cols = head_cols(h)
        upper = upper_ref[h * HEAD_DIM : (h + 1) * HEAD_DIM, :]
        from_values = dot(twice(value_ref[:, cols] * leads), split_cols(upper), NT)
        from_keys = dot(twice(key_ref[:, cols] * leads), split_rows(upper), NN)
        key_out_ref[:, cols] = (key_part_ref[:, cols] + from_values).astype(BF16)
        value_out_ref[:, cols] = (value_part_ref[:, cols] + from_keys).astype(BF16)


def on_device(queries, key_input, value_input, norm_gain, out_grad, doc_lengths):
    rows_here, width_here = queries.shape
    steps = width_here // STEP_COLS
    devices = lax.axis_size("ctx")
    state_rows = width_here

    lengths = pl.BlockSpec(memory_space=pltpu.SMEM)
    wide = pl.BlockSpec((rows_here, STEP_COLS), lambda i: (0, i))
    state = pl.BlockSpec((STEP_COLS, HEAD_DIM), lambda i: (i, 0))
    gain_spec = pl.BlockSpec((1, STEP_COLS), lambda i: (0, i))
    sums_spec = pl.BlockSpec((2, rows_here), lambda i: (0, 0))

    wide_f32 = jax.ShapeDtypeStruct((rows_here, width_here), F32)
    wide_bf16 = jax.ShapeDtypeStruct((rows_here, width_here), BF16)
    state_f32 = jax.ShapeDtypeStruct((state_rows, HEAD_DIM), F32)
    sums_f32 = jax.ShapeDtypeStruct((2, rows_here), F32)
    mask_scratch = pltpu.VMEM((BLOCK, BLOCK), BF16)

    def call(body, name, ins, outs, shapes, flops, moved, scratch=(), grid=(steps,)):
        return pl.pallas_call(
            body,
            name=name,
            grid=grid,
            in_specs=[lengths] + ins,
            out_specs=outs,
            out_shape=shapes,
            scratch_shapes=list(scratch),
            compiler_params=pltpu.CompilerParams(vmem_limit_bytes=24 << 20),
            cost_estimate=pl.CostEstimate(flops=flops, bytes_accessed=moved, transcendentals=0),
        )

    gain = norm_gain.reshape(1, width_here)
    product = 2 * rows_here * HEAD_DIM * width_here
    size = rows_here * width_here

    def exchange(parts):
        shaped = parts.reshape(devices, state_rows // devices, HEAD_DIM)
        return lax.all_to_all(shaped, "ctx", 0, 0, tiled=True)

    def scan(parts, backward):
        got = exchange(parts)
        whole = pl.BlockSpec(got.shape, lambda: (0, 0, 0))
        entries = call(
            lambda *refs: scan_kernel(*refs, backward=backward),
            "scan_back" if backward else "scan_ahead",
            [whole],
            whole,
            jax.ShapeDtypeStruct(got.shape, F32),
            2 * got.size,
            8 * got.size,
            [pltpu.SMEM((devices,), jnp.int32)],
            (),
        )(doc_lengths, got)
        return lax.all_to_all(entries, "ctx", 0, 0, tiled=True).reshape(state_rows, HEAD_DIM)

    parts = call(state_kernel, "states", [wide, wide], state, state_f32, product, 8 * size)(
        doc_lengths, key_input, value_input
    )
    local = call(
        local_kernel,
        "local_mix",
        [wide, wide, wide],
        wide,
        wide_f32,
        6 * product,
        10 * size,
        [mask_scratch],
    )(doc_lengths, queries, key_input, value_input)
    entry = scan(parts, False)
    mixed, sums = call(
        mixed_kernel,
        "mix_states",
        [wide, wide, state, wide, gain_spec],
        [wide, sums_spec],
        [wide_f32, sums_f32],
        2 * product,
        14 * size,
        [pltpu.VMEM((2, rows_here, HEAD_DIM), F32)],
    )(doc_lengths, queries, local, entry, out_grad, gain)
    others = [
        lax.ppermute(sums, "head", [(i, i ^ flip) for i in range(lax.axis_size("head"))])
        for flip in (1, 3, 2)
    ]
    normed_out, grad_mixed, upper_parts = call(
        grad_kernel,
        "norm_grad",
        [sums_spec] * 4 + [wide, wide, gain_spec, wide],
        [wide, wide, state],
        [wide_bf16, wide_bf16, state_f32],
        product,
        14 * size,
        [pltpu.VMEM((2, rows_here, HEAD_DIM), F32)],
    )(doc_lengths, sums, *others, mixed, out_grad, gain, queries)
    query_grad, key_part, value_part = call(
        back_kernel,
        "local_back",
        [wide, wide, wide, wide, state],
        [wide, wide, wide],
        [wide_bf16, wide_f32, wide_f32],
        15 * product,
        20 * size,
        [mask_scratch],
    )(doc_lengths, queries, key_input, value_input, grad_mixed, entry)
    upper = scan(upper_parts, True)
    key_grad, value_grad = call(
        final_kernel,
        "back_states",
        [wide, wide, wide, wide, state],
        [wide, wide],
        [wide_bf16, wide_bf16],
        4 * product,
        16 * size,
    )(doc_lengths, key_input, value_input, key_part, value_part, upper)
    return (normed_out, query_grad, key_grad, value_grad)


def solution(mesh):
    wide = P("ctx", "head")
    return jax.shard_map(
        on_device,
        mesh=mesh,
        in_specs=(wide, wide, wide, P("head"), wide, P()),
        out_specs=(wide, wide, wide, wide),
        check_vma=False,
    )
```

time: 374 us -> 106 us (0.28)
  waiting for transfers between devices: 133 us -> 8.26 us
  other arithmetic: 87.7 us -> 0 us
  blocking collectives: 80.7 us -> 37.9 us
  matrix products: 30.8 us -> 0 us
  Pallas kernels: 0 us -> 29.3 us
  between operations: 16.9 us -> 0.8 us
  starting transfers between devices: 0.08 us -> 13 us
  local copies, waits for them, and re-layouts: 20.7 us -> 15.9 us
    all_gather x2 -> x0, waiting for transfers between devices: 133 us -> none  [prefix(): gathered = jax.tree.map(lambda a: lax.all_gather(a, axis), part)]
    unnamed x1 -> x0, blocking collectives: 66 us -> none
    add x33 -> x0, other arithmetic: 58.6 us -> none  [the longest x31 58.5 us: join_reset(): nearer[1] + (1.0 - nearer[0]) * earlier[1]]
    all_to_all x0 -> x2, blocking collectives: none -> 37.9 us  [exchange(): return lax.all_to_all(shaped, 'ctx', 0, 0, tiled=True)]
    dot_general x12 -> x0, matrix products: 30.8 us -> none  [the longest x1 4.26 us: on_device(): jnp.einsum('hij,ihe->jhe', weights_kept[segment], grad_heads, preferred_e...]
    pallas_call x0 -> x8, Pallas kernels: none -> 29.3 us  [the longest x1 9.38 us: on_device(): call(back_kernel, 'local_back', [wide, wide, wide, wide, state], [wide, w...]
    sub x32 -> x0, other arithmetic: 18.8 us -> none  [the longest x31 18.2 us: join_reset(): 1.0 - nearer[0]]
    psum x2 -> x0, blocking collectives: 14.7 us -> none  [the longest x1 8.5 us: on_device(): square_sum = lax.psum(jnp.sum(flat_mixed * flat_mixed, axis=1), 'head')]
  transfers between devices with their start and end apart: 2 -> 5, of which waited for: 1 -> 3; matrix products, arithmetic and copies ran while one was open for 6% -> 0% of each run, Pallas kernels for 0% -> 14%
where the time goes in v2:
time: 106 us; the launch traced here: 105 us
  blocking collectives  37.9 us (36%)
  Pallas kernels  29.3 us (28%)
  local copies, waits for them, and re-layouts  15.9 us (15%)
  starting transfers between devices  13 us (12%)
  waiting for transfers between devices  8.26 us (8%)
    all_to_all x2, blocking collectives, exchange(): return lax.all_to_all(shaped, 'ctx', 0, 0, tiled=True)  37.9 us
    unnamed x40, local copies, waits for them, and re-layouts  15.9 us
    pallas_call x1, Pallas kernels, on_device(): call(back_kernel, 'local_back', [wide, wide, wide, wide, state], [wide, w...  9.38 us
    all_to_all x2, starting transfers between devices, scan(): lax.all_to_all(entries, 'ctx', 0, 0, tiled=True)  9.29 us
    all_to_all x2, waiting for transfers between devices, scan(): lax.all_to_all(entries, 'ctx', 0, 0, tiled=True)  5.45 us
    pallas_call x1, Pallas kernels, on_device(): call(local_kernel, 'local_mix', [wide, wide, wide], wide, wide_f32, 6 * p...  4.86 us
    pallas_call x1, Pallas kernels, on_device(): call(final_kernel, 'back_states', [wide, wide, wide, wide, state], [wide,...  4.61 us
    ppermute x3, starting transfers between devices, on_device(): lax.ppermute(sums, 'head', [(i, i ^ flip) for i in range(lax.axis_size('h...  3.68 us
  transfers between devices with their start and end apart: 5, of which 3 were waited for; matrix products, arithmetic and copies ran while one was open for 0% of the time, Pallas kernels for 14%

profile of v2, /device:TPU:1, one launch (start us, length us, event | category | flops | bytes accessed | tf_op | source)
XLA Modules:
  0.0 105.1 jit_solution(3049030847199887384)
XLA Ops:
  0.6 1.2 %copy-done.1 = bf16[512,1024]{1,0:T(8,128)(2,1)S(1)} copy-done((bf16[512,1024]{1,0:T(8,128)(2,1)S(1)}, bf16[512,1024]{1,0:T(8,128)(2,1)}, u32[]{:S(2)}) %copy-start.1) | copy-done | bytes 1048600
  1.9 1.2 %copy-done.3 = bf16[512,1024]{1,0:T(8,128)(2,1)S(1)} copy-done((bf16[512,1024]{1,0:T(8,128)(2,1)S(1)}, bf16[512,1024]{1,0:T(8,128)(2,1)}, u32[]{:S(2)}) %copy-start.3) | copy-done | bytes 1048600
  3.7 2.1 %states.1 = f32[1024,128]{1,0:T(8,128)S(1)} custom-call(s32[8]{0:T(128)S(1)} %copy-done.15, bf16[512,1024]{1,0:T(8,128)(2,1)S(1)} %copy-done.1, bf16[512,1024]{1,0:T(8,128)(2,1)S(1)} %copy-done.3), custom_call_target="tpu_custom_call" | custom-call | flops 134217728 | bytes 4194304 | tf_op jit(solution)/shard_map/states/pallas_call | solution.py:321
  5.9 21.2 %all_to_all.20.refs_1_ = f32[32,32,128]{2,1,0:T(8,128)S(1)} all-to-all(f32[32,32,128]{2,1,0:T(8,128)S(1)} %bitcast.5), channel_id=1, replica_groups=mesh['head'=4,'ctx'=32] {'ctx'}, dimensions={0} | all-to-all | bytes 1048576 | tf_op jit(solution)/shard_map/all_to_all | solution.py:303
  28.5 4.6 %all-to-all-start.1 = ((f32[32,32,128]{2,1,0:T(8,128)}), f32[32,32,128]{2,1,0:T(8,128)}, u32[]{:S(2)}, u32[]{:S(2)}) async-start(f32[32,32,128]{2,1,0:T(8,128)} %copy-done.14), calls=%async_computation.1 | async-start | bytes 1048576 | tf_op jit(solution)/shard_map/all_to_all | solution.py:319
  33.2 4.9 %local_mix.1.local_ref = f32[512,1024]{1,0:T(8,128)S(1)} custom-call(s32[8]{0:T(128)S(1)} %copy-done.16, bf16[512,1024]{1,0:T(8,128)(2,1)S(1)} %copy-done, bf16[512,1024]{1,0:T(8,128)(2,1)S(1)} %copy-done.2, bf16[512,1024]{1,0:T(8,128)(2,1)S(1)} %copy-done.4), custom_call_target="tpu_custom_call" | custom-call | flops 805306368 | bytes 5242880 | tf_op jit(solution)/shard_map/local_mix/pallas_call | solution.py:324
  38.1 1.3 %copy-done.5 = f32[512,1024]{1,0:T(8,128)} copy-done((f32[512,1024]{1,0:T(8,128)}, f32[512,1024]{1,0:T(8,128)S(1)}, u32[]{:S(2)}) %copy-start.5) | copy-done | bytes 2097176
  39.5 5.4 %all-to-all-done.1 = f32[32,32,128]{2,1,0:T(8,128)} async-done(((f32[32,32,128]{2,1,0:T(8,128)}), f32[32,32,128]{2,1,0:T(8,128)}, u32[]{:S(2)}, u32[]{:S(2)}) %all-to-all-start.1) | async-done | bytes 524320 | tf_op jit(solution)/shard_map/all_to_all | solution.py:319
  44.9 1.6 %copy-done.6 = f32[512,1024]{1,0:T(8,128)S(1)} copy-done((f32[512,1024]{1,0:T(8,128)S(1)}, f32[512,1024]{1,0:T(8,128)}, u32[]{:S(2)}) %copy-start.6) | copy-done | bytes 2097176
  46.5 1.2 %copy-done.7 = bf16[512,1024]{1,0:T(8,128)(2,1)S(1)} copy-done((bf16[512,1024]{1,0:T(8,128)(2,1)S(1)}, bf16[512,1024]{1,0:T(8,128)(2,1)}, u32[]{:S(2)}) %copy-start.7) | copy-done | bytes 1048600
  47.7 3.6 %mix_states.1 = (f32[512,1024]{1,0:T(8,128)S(1)}, f32[2,512]{1,0:T(2,128)S(1)}) custom-call(s32[8]{0:T(128)S(1)} %copy-done.16, bf16[512,1024]{1,0:T(8,128)(2,1)S(1)} %copy-done, f32[512,1024]{1,0:T(8,128)S(1)} %copy-done.6, f32[1024,128]{1,0:T(8,128)} %bitcast.1.state_ref, bf16[512,1024]{1,0:T(8,128)(2,1)S(1)} %copy-done.7, f32[1,1024]{1,0:T(1,128)S(1)} %bitcast.7), custom_call_target="tpu_custom_call" | custom-call | flops 268435456 | bytes 7340032 | tf_op jit(solution)/shard_map/mix_states/pallas_call | solution.py:335
  51.3 2.8 %collective-permute-start.2 = (f32[2,512]{1,0:T(2,128)S(1)}, f32[2,512]{1,0:T(2,128)S(1)}, u32[]{:S(2)}, u32[]{:S(2)}) collective-permute-start(f32[2,512]{1,0:T(2,128)S(1)} %get-tuple-element.14.sums_ref), channel_id=1, source_target_pairs={{0,64},{32,96},{64,0},{96,32},{1,65},{33,97},{65,1},{97,33},{2,66}... | collective-permute-start | bytes 12296 | tf_op jit(solution)/shard_map/ppermute | solution.py:346
  54.2 0.9 collective-permute-start.1
  55.4 2.5 %collective-permute-done.1.sums2_ref = f32[2,512]{1,0:T(2,128)S(1)} collective-permute-done((f32[2,512]{1,0:T(2,128)S(1)}, f32[2,512]{1,0:T(2,128)S(1)}, u32[]{:S(2)}, u32[]{:S(2)}) %collective-permute-start.1) | collective-permute-done | bytes 4128 | tf_op jit(solution)/shard_map/ppermute | solution.py:346
  57.8 3.5 %norm_grad.1 = (bf16[512,1024]{1,0:T(8,128)(2,1)}, bf16[512,1024]{1,0:T(8,128)(2,1)S(1)}, f32[1024,128]{1,0:T(8,128)S(1)}) custom-call(s32[8]{0:T(128)S(1)} %copy-done.16, f32[2,512]{1,0:T(2,128)S(1)} %get-tuple-element.14.sums_ref, f32[2,512]{1,0:T(2,128)S(1)} %collective-permute-done.sums1_ref, f32[2,512]{1,0:T(2,128)S(1)} %collective-permute-done.1.sums2_ref, ...), custom_call_target="tpu_custom_call" | custom-call | flops 134217728 | bytes 7340032 | tf_op jit(solution)/shard_map/norm_grad/pallas_call | solution.py:349
  61.3 16.6 %all_to_all.21.refs_1_ = f32[32,32,128]{2,1,0:T(8,128)S(1)} all-to-all(f32[32,32,128]{2,1,0:T(8,128)S(1)} %bitcast.6), channel_id=1, replica_groups=mesh['head'=4,'ctx'=32] {'ctx'}, dimensions={0} | all-to-all | bytes 1048576 | tf_op jit(solution)/shard_map/all_to_all | solution.py:303
  79.4 4.6 %all-to-all-start.3 = ((f32[32,32,128]{2,1,0:T(8,128)}), f32[32,32,128]{2,1,0:T(8,128)}, u32[]{:S(2)}, u32[]{:S(2)}) async-start(f32[32,32,128]{2,1,0:T(8,128)} %copy-done.13), calls=%async_computation.3 | async-start | bytes 1048576 | tf_op jit(solution)/shard_map/all_to_all | solution.py:319
  84.1 1.2 %copy-done.19 = bf16[512,1024]{1,0:T(8,128)(2,1)S(1)} copy-done((bf16[512,1024]{1,0:T(8,128)(2,1)S(1)}, bf16[512,1024]{1,0:T(8,128)(2,1)}, u32[]{:S(2)}) %copy-start.19) | copy-done | bytes 1048600
  85.3 9.4 %local_back.1 = (bf16[512,1024]{1,0:T(8,128)(2,1)}, f32[512,1024]{1,0:T(8,128)S(1)}, f32[512,1024]{1,0:T(8,128)S(1)}) custom-call(s32[8]{0:T(128)S(1)} %copy-done.16, bf16[512,1024]{1,0:T(8,128)(2,1)S(1)} %copy-done, bf16[512,1024]{1,0:T(8,128)(2,1)S(1)} %copy-done.2, bf16[512,1024]{1,0:T(8,128)(2,1)S(1)} %copy-done.4, bf16[512,1024]{1,0:T(8,128)(2,1)S(1)} %copy-done.19, ...), custom_call_target="tpu_custom_call" | custom-call | flops 2013265920 | bytes 10485760 | tf_op jit(solution)/shard_map/local_back/pallas_call | solution.py:359
  94.7 1.4 %copy-done.9 = f32[512,1024]{1,0:T(8,128)} copy-done((f32[512,1024]{1,0:T(8,128)}, f32[512,1024]{1,0:T(8,128)S(1)}, u32[]{:S(2)}) %copy-start.9) | copy-done | bytes 2097176
  96.0 1.3 %copy-done.11 = f32[512,1024]{1,0:T(8,128)} copy-done((f32[512,1024]{1,0:T(8,128)}, f32[512,1024]{1,0:T(8,128)S(1)}, u32[]{:S(2)}) %copy-start.11) | copy-done | bytes 2097176
  97.3 1.6 %copy-done.10 = f32[512,1024]{1,0:T(8,128)S(1)} copy-done((f32[512,1024]{1,0:T(8,128)S(1)}, f32[512,1024]{1,0:T(8,128)}, u32[]{:S(2)}) %copy-start.10) | copy-done | bytes 2097176
  98.9 1.6 %copy-done.12 = f32[512,1024]{1,0:T(8,128)S(1)} copy-done((f32[512,1024]{1,0:T(8,128)S(1)}, f32[512,1024]{1,0:T(8,128)}, u32[]{:S(2)}) %copy-start.12) | copy-done | bytes 2097176
  100.5 4.6 %back_states.1 = (bf16[512,1024]{1,0:T(8,128)(2,1)}, bf16[512,1024]{1,0:T(8,128)(2,1)}) custom-call(s32[8]{0:T(128)S(1)} %copy-done.16, bf16[512,1024]{1,0:T(8,128)(2,1)S(1)} %copy-done.2, bf16[512,1024]{1,0:T(8,128)(2,1)S(1)} %copy-done.4, f32[512,1024]{1,0:T(8,128)S(1)} %copy-done.10, f32[512,1024]{1,0:T(8,128)S(1)} %copy-done.12, ...), custom_call_target="tpu_custom_call" | custom-call | flops 536870912 | bytes 8388608 | tf_op jit(solution)/shard_map/back_states/pallas_call | solution.py:370
  (36 shorter events, 4.0 us)
Async XLA Ops:
  0.6 1.2 %copy-start.1 = (bf16[512,1024]{1,0:T(8,128)(2,1)S(1)}, bf16[512,1024]{1,0:T(8,128)(2,1)}, u32[]{:S(2)}) copy-start(bf16[512,1024]{1,0:T(8,128)(2,1)} %key_ref.7) | copy-start | bytes 3145732
  1.9 1.2 %copy-start.3 = (bf16[512,1024]{1,0:T(8,128)(2,1)S(1)}, bf16[512,1024]{1,0:T(8,128)(2,1)}, u32[]{:S(2)}) copy-start(bf16[512,1024]{1,0:T(8,128)(2,1)} %value_ref.7) | copy-start | bytes 3145732
  3.7 23.3 %copy-start.16 = (s32[8]{0:T(128)S(1)}, s32[8]{0:T(128)}, u32[]{:S(2)}) copy-start(s32[8]{0:T(128)} %lengths_ref.11) | copy-start | bytes 100
  5.8 27.4 %copy-start = (bf16[512,1024]{1,0:T(8,128)(2,1)S(1)}, bf16[512,1024]{1,0:T(8,128)(2,1)}, u32[]{:S(2)}) copy-start(bf16[512,1024]{1,0:T(8,128)(2,1)} %query_ref.7) | copy-start | bytes 3145732
  5.8 27.4 %copy-start.2 = (bf16[512,1024]{1,0:T(8,128)(2,1)S(1)}, bf16[512,1024]{1,0:T(8,128)(2,1)}, u32[]{:S(2)}) copy-start(bf16[512,1024]{1,0:T(8,128)(2,1)} %key_ref.7) | copy-start | bytes 3145732
  5.8 27.4 %copy-start.4 = (bf16[512,1024]{1,0:T(8,128)(2,1)S(1)}, bf16[512,1024]{1,0:T(8,128)(2,1)}, u32[]{:S(2)}) copy-start(bf16[512,1024]{1,0:T(8,128)(2,1)} %value_ref.7) | copy-start | bytes 3145732
  27.7 0.8 copy-start.14
  28.5 16.4 %all-to-all-start.1 = ((f32[32,32,128]{2,1,0:T(8,128)}), f32[32,32,128]{2,1,0:T(8,128)}, u32[]{:S(2)}, u32[]{:S(2)}) async-start(f32[32,32,128]{2,1,0:T(8,128)} %copy-done.14), calls=%async_computation.1 | async-start | bytes 1048576 | tf_op jit(solution)/shard_map/all_to_all | solution.py:319
  33.2 11.7 %copy-start.17 = (f32[1024]{0:T(1024)S(1)}, f32[1024]{0:T(1024)}, u32[]{:S(2)}) copy-start(f32[1024]{0:T(1024)} %param.9) | copy-start | bytes 12292
  38.1 1.4 %copy-start.5 = (f32[512,1024]{1,0:T(8,128)}, f32[512,1024]{1,0:T(8,128)S(1)}, u32[]{:S(2)}) copy-start(f32[512,1024]{1,0:T(8,128)S(1)} %local_mix.1.local_ref) | copy-start | bytes 6291460
  44.9 1.6 %copy-start.6 = (f32[512,1024]{1,0:T(8,128)S(1)}, f32[512,1024]{1,0:T(8,128)}, u32[]{:S(2)}) copy-start(f32[512,1024]{1,0:T(8,128)} %copy-done.5) | copy-start | bytes 6291460
  46.5 1.2 %copy-start.7 = (bf16[512,1024]{1,0:T(8,128)(2,1)S(1)}, bf16[512,1024]{1,0:T(8,128)(2,1)}, u32[]{:S(2)}) copy-start(bf16[512,1024]{1,0:T(8,128)(2,1)} %grad_ref.3) | copy-start | bytes 3145732
  47.7 10.1 %copy-start.8 = (bf16[512,1024]{1,0:T(8,128)(2,1)S(1)}, bf16[512,1024]{1,0:T(8,128)(2,1)}, u32[]{:S(2)}) copy-start(bf16[512,1024]{1,0:T(8,128)(2,1)} %grad_ref.3) | copy-start | bytes 3145732
  51.3 4.0 %collective-permute-start.2 = (f32[2,512]{1,0:T(2,128)S(1)}, f32[2,512]{1,0:T(2,128)S(1)}, u32[]{:S(2)}, u32[]{:S(2)}) collective-permute-start(f32[2,512]{1,0:T(2,128)S(1)} %get-tuple-element.14.sums_ref), channel_id=1, source_target_pairs={{0,64},{32,96},{64,0},{96,32},{1,65},{33,97},{65,1},{97,33},{2,66}... | collective-permute-start | bytes 12296 | tf_op jit(solution)/shard_map/ppermute | solution.py:346
  54.2 3.7 %collective-permute-start.1 = (f32[2,512]{1,0:T(2,128)S(1)}, f32[2,512]{1,0:T(2,128)S(1)}, u32[]{:S(2)}, u32[]{:S(2)}) collective-permute-start(f32[2,512]{1,0:T(2,128)S(1)} %get-tuple-element.14.sums_ref), channel_id=1, source_target_pairs={{0,96},{32,64},{64,32},{96,0},{1,97},{33,65},{65,33},{97,1},{2,98}... | collective-permute-start | bytes 12296 | tf_op jit(solution)/shard_map/ppermute | solution.py:346
  55.0 2.8 %collective-permute-start = (f32[2,512]{1,0:T(2,128)S(1)}, f32[2,512]{1,0:T(2,128)S(1)}, u32[]{:S(2)}, u32[]{:S(2)}) collective-permute-start(f32[2,512]{1,0:T(2,128)S(1)} %get-tuple-element.14.sums_ref), channel_id=1, source_target_pairs={{0,32},{32,0},{64,96},{96,64},{1,33},{33,1},{65,97},{97,65},{2,34}... | collective-permute-start | bytes 12296 | tf_op jit(solution)/shard_map/ppermute | solution.py:346
  61.3 16.6 %copy-start.18 = (bf16[512,1024]{1,0:T(8,128)(2,1)}, bf16[512,1024]{1,0:T(8,128)(2,1)S(1)}, u32[]{:S(2)}) copy-start(bf16[512,1024]{1,0:T(8,128)(2,1)S(1)} %get-tuple-element.17.grad_ref) | copy-start | bytes 3145732
  78.6 0.8 copy-start.13
  79.4 17.9 %all-to-all-start.3 = ((f32[32,32,128]{2,1,0:T(8,128)}), f32[32,32,128]{2,1,0:T(8,128)}, u32[]{:S(2)}, u32[]{:S(2)}) async-start(f32[32,32,128]{2,1,0:T(8,128)} %copy-done.13), calls=%async_computation.3 | async-start | bytes 1048576 | tf_op jit(solution)/shard_map/all_to_all | solution.py:319
  84.1 1.2 %copy-start.19 = (bf16[512,1024]{1,0:T(8,128)(2,1)S(1)}, bf16[512,1024]{1,0:T(8,128)(2,1)}, u32[]{:S(2)}) copy-start(bf16[512,1024]{1,0:T(8,128)(2,1)} %copy-done.18) | copy-start | bytes 3145732
  94.7 1.4 %copy-start.9 = (f32[512,1024]{1,0:T(8,128)}, f32[512,1024]{1,0:T(8,128)S(1)}, u32[]{:S(2)}) copy-start(f32[512,1024]{1,0:T(8,128)S(1)} %get-tuple-element.19.key_part_ref) | copy-start | bytes 6291460
  96.0 1.3 %copy-start.11 = (f32[512,1024]{1,0:T(8,128)}, f32[512,1024]{1,0:T(8,128)S(1)}, u32[]{:S(2)}) copy-start(f32[512,1024]{1,0:T(8,128)S(1)} %get-tuple-element.20.value_part_ref) | copy-start | bytes 6291460
  97.3 1.6 %copy-start.10 = (f32[512,1024]{1,0:T(8,128)S(1)}, f32[512,1024]{1,0:T(8,128)}, u32[]{:S(2)}) copy-start(f32[512,1024]{1,0:T(8,128)} %copy-done.9) | copy-start | bytes 6291460
  98.9 1.6 %copy-start.12 = (f32[512,1024]{1,0:T(8,128)S(1)}, f32[512,1024]{1,0:T(8,128)}, u32[]{:S(2)}) copy-start(f32[512,1024]{1,0:T(8,128)} %copy-done.11) | copy-start | bytes 6291460
  (1 other events, 0.7 us)

commit v3 on v2

v3 whole, which is shorter than its diff:
```python
import jax
import jax.numpy as jnp
from jax import lax
from jax.experimental import pallas as pl
from jax.experimental.pallas import tpu as pltpu
from jax.sharding import PartitionSpec as P

HEADS = 32
HEAD_DIM = 128
BLOCK = 512
GRAIN = 128
NDOCS = 8
GRAINS = BLOCK // GRAIN
WIDTH = HEADS * HEAD_DIM
HALF = BLOCK // 2
EPSILON = 1e-06

CORES = 2
COLUMNS = 4
ROWS = 4
FLIPS = (2, 1, 3)

F32 = jnp.float32
BF16 = jnp.bfloat16
I32 = jnp.int32

NN = ((1,), (0,))
NT = ((1,), (1,))
TN = ((0,), (0,))


def dot(a, b, dims):
    return lax.dot_general(a, b, (dims, ((), ())), preferred_element_type=F32)


def place():
    index = lax.axis_index("ctx")
    return index // (CORES * COLUMNS), (index // CORES) % COLUMNS, index % CORES


def doc_starts(lengths_ref):
    starts = [I32(0)]
    for i in range(NDOCS - 1):
        starts.append(starts[-1] + lengths_ref[i])
    return starts


def grain_docs(lengths_ref):
    total = lax.axis_size("ctx") * GRAINS
    first = lax.axis_index("ctx") * GRAINS
    starts = doc_starts(lengths_ref)
    docs = []
    for k in range(-1, GRAINS + 1):
        grain = first + k
        count = (grain >= total).astype(I32) - 1
        for s in starts:
            count = count + (s <= grain).astype(I32)
        docs.append(count)
    return docs


def unbroken(lengths_ref, first, grains, backward):
    hits = I32(0)
    for s in doc_starts(lengths_ref)[1:]:
        at = s - 1 if backward else s
        hits = hits + ((at >= first) & (at < first + grains)).astype(I32)
    return (hits == 0).astype(F32)


FROM_OWN, FROM_GOT, KEEPS, NEAR, FAR, KEEP_BLOCK = 0, 1, 2, 6, 7, 8
DIRECTION = 9
FOLLOWS = 2 * DIRECTION
FIRST = FOLLOWS + GRAINS
LEADS = FIRST + GRAINS
FLAGS = 32


def write_flags(lengths_ref, flags_ref):
    index = lax.axis_index("ctx")
    row, _, core = place()
    block_of = index - core
    width = CORES * GRAINS
    span = COLUMNS * width

    def put(at, value):
        flags_ref[at : at + 1, :] = jnp.full((1, HEAD_DIM), value, F32)

    for backward in (False, True):
        base = DIRECTION if backward else 0
        earlier = block_of + (1 if backward else 0)
        later = block_of + (0 if backward else 1)
        keep = unbroken(lengths_ref, later * GRAINS, GRAINS, backward)
        is_later = index == later
        put(base + FROM_OWN, jnp.where(is_later, 1.0, keep))
        put(base + FROM_GOT, jnp.where(is_later, keep, 1.0))
        for q in range(COLUMNS):
            first = row * span + q * width
            put(base + KEEPS + q, unbroken(lengths_ref, first, width, backward))
        behind = (ROWS - 1 - row) if backward else row
        near_row = row + 1 if backward else row - 1
        near_keep = unbroken(lengths_ref, near_row * span, span, backward)
        put(base + NEAR, (behind >= 1).astype(F32))
        put(base + FAR, (behind >= 2).astype(F32) * near_keep)
        put(base + KEEP_BLOCK, unbroken(lengths_ref, earlier * GRAINS, GRAINS, backward))
    docs = grain_docs(lengths_ref)
    for base, doc in ((FOLLOWS, docs[0]), (FIRST, docs[1]), (LEADS, docs[GRAINS + 1])):
        for g in range(GRAINS):
            put(base + g, (docs[1 + g] == doc).astype(F32))


def flag(flags_ref, at):
    return flags_ref[at : at + 1, :]


def row_mask(flags_ref, base):
    parts = [
        jnp.broadcast_to(flag(flags_ref, base + g), (GRAIN, HEAD_DIM)) for g in range(GRAINS)
    ]
    return jnp.concatenate(parts, axis=0).astype(BF16)


def rows_equal(docs, doc):
    parts = [
        jnp.full((GRAIN, HEAD_DIM), (docs[1 + g] == doc).astype(F32), F32) for g in range(GRAINS)
    ]
    return jnp.concatenate(parts, axis=0).astype(BF16)


def pair_mask(docs):
    rows = lax.broadcasted_iota(I32, (GRAIN, GRAIN), 0)
    cols = lax.broadcasted_iota(I32, (GRAIN, GRAIN), 1)
    lower = jnp.where(rows >= cols, 1.0, 0.0).astype(F32)
    out = []
    for i in range(GRAINS):
        line = []
        for j in range(GRAINS):
            if j < i:
                same = (docs[1 + i] == docs[1 + j]).astype(F32)
                line.append(jnp.full((GRAIN, GRAIN), same, F32))
            elif j == i:
                line.append(lower)
            else:
                line.append(jnp.zeros((GRAIN, GRAIN), F32))
        out.append(jnp.concatenate(line, axis=1))
    return jnp.concatenate(out, axis=0).astype(BF16)


def split(x):
    high = x.astype(BF16)
    low = (x - high.astype(F32)).astype(BF16)
    return jnp.concatenate([high, low], axis=0)


def twice(x):
    return jnp.concatenate([x, x], axis=1)


def head(k, core=None):
    if core is None:
        return slice(k * HEAD_DIM, (k + 1) * HEAD_DIM)
    return pl.ds(pl.multiple_of((core * COLUMNS + k) * HEAD_DIM, HEAD_DIM), HEAD_DIM)


def rows_of(k):
    return slice(k * HEAD_DIM, (k + 1) * HEAD_DIM)


def piece(index):
    return pl.ds(pl.multiple_of(index * HEAD_DIM, HEAD_DIM), HEAD_DIM)


def state_kernel(
    lengths_ref, key_ref, value_ref, own_ref, other_ref, flags_ref, key_buf, value_buf, sems
):
    core = lax.axis_index("ctx") % CORES
    loads = []
    for g in range(GRAINS):
        rows = slice(g * GRAIN, (g + 1) * GRAIN)
        pair = []
        for m, (source, to) in enumerate(((key_ref, key_buf), (value_ref, value_buf))):
            copy = pltpu.make_async_copy(source.at[rows], to.at[rows], sems.at[m, g])
            copy.start()
            pair.append(copy)
        loads.append(pair)
    write_flags(lengths_ref, flags_ref)
    docs = grain_docs(lengths_ref)
    for g in range(0, GRAINS, 2):
        for copy in loads[g] + loads[g + 1]:
            copy.wait()
        rows = slice(g * GRAIN, (g + 2) * GRAIN)
        parts = [
            jnp.full((GRAIN, HEAD_DIM), (docs[1 + i] == docs[GRAINS]).astype(F32), F32)
            for i in (g, g + 1)
        ]
        mask = jnp.concatenate(parts, axis=0).astype(BF16)
        for side, out_ref in ((1 - core, other_ref), (core, own_ref)):
            for k in range(COLUMNS):
                cols = head(k, side)
                state = dot(key_buf[rows, cols] * mask, value_buf[rows, cols], TN)
                if g == 0:
                    out_ref[rows_of(k), :] = state
                else:
                    out_ref[rows_of(k), :] += state


def pair_kernel(flags_ref, own_ref, got_ref, keep_ref, *send_refs, base):
    _, column, _ = place()
    from_own = flag(flags_ref, base + FROM_OWN)
    from_got = flag(flags_ref, base + FROM_GOT)
    for flip, out_ref in zip((0,) + FLIPS, (keep_ref,) + send_refs):
        rows = piece(column ^ flip)
        out_ref[...] = from_own * own_ref[rows, :] + from_got * got_ref[rows, :]


def chip_order(base):
    return list(range(COLUMNS))[:: -1 if base else 1]


def row_kernel(flags_ref, keep_ref, *refs, base):
    got_refs, (parts_ref, total_ref) = refs[: len(FLIPS)], refs[len(FLIPS) :]
    _, column, _ = place()
    for flip, in_ref in zip((0,) + FLIPS, (keep_ref,) + got_refs):
        parts_ref[piece(column ^ flip), :] = in_ref[...]
    order = chip_order(base)
    running = parts_ref[rows_of(order[0]), :]
    for q in order[1:]:
        running = parts_ref[rows_of(q), :] + flag(flags_ref, base + KEEPS + q) * running
    total_ref[...] = running


def enter_kernel(flags_ref, parts_ref, near_ref, far_ref, keep_ref, *refs, base):
    send_refs, (entries_ref,) = refs[: len(FLIPS)], refs[len(FLIPS) :]
    _, column, _ = place()
    running = flag(flags_ref, base + NEAR) * near_ref[...]
    running = running + flag(flags_ref, base + FAR) * far_ref[...]
    for q in chip_order(base):
        entries_ref[rows_of(q), :] = running
        running = parts_ref[rows_of(q), :] + flag(flags_ref, base + KEEPS + q) * running
    for flip, out_ref in zip((0,) + FLIPS, (keep_ref,) + send_refs):
        out_ref[...] = entries_ref[piece(column ^ flip), :]


def unpair_kernel(flags_ref, own_ref, got_ref, keep_ref, *refs, base):
    back_refs, (mine_ref, send_ref, whole_ref) = refs[: len(FLIPS)], refs[len(FLIPS) :]
    _, column, core = place()
    for flip, in_ref in zip((0,) + FLIPS, (keep_ref,) + back_refs):
        whole_ref[piece(column ^ flip), :] = in_ref[...]
    keep = flag(flags_ref, base + KEEP_BLOCK)
    is_earlier = (core == 1) if base else (core == 0)

    @pl.when(is_earlier)
    def _():
        mine_ref[...] = whole_ref[...]
        send_ref[...] = own_ref[...] + keep * whole_ref[...]

    @pl.when(jnp.logical_not(is_earlier))
    def _():
        mine_ref[...] = got_ref[...] + keep * whole_ref[...]
        send_ref[...] = whole_ref[...]


def mask_kernel(lengths_ref, mask_ref):
    mask_ref[...] = pair_mask(grain_docs(lengths_ref))


def local_kernel(query_ref, key_ref, value_ref, mask_ref, out_ref, *, heads):
    for n, k in enumerate(heads):
        cols = head(k)
        for r in range(2):
            rows = slice(r * HALF, (r + 1) * HALF)
            upto = (r + 1) * HALF
            weights = dot(query_ref[rows, cols], key_ref[:upto, cols], NT).astype(BF16)
            weights = weights * mask_ref[rows, :upto]
            out_ref[rows, head(n)] = dot(weights, value_ref[:upto, cols], NN)


def gather_states(own_ref, got_ref, out_ref):
    core = lax.axis_index("ctx") % CORES
    for side, in_ref in ((core, own_ref), (1 - core, got_ref)):
        for k in range(COLUMNS):
            out_ref[side * COLUMNS + k] = split(in_ref[rows_of(k), :])


def beside(state):
    return jnp.concatenate([state[:HEAD_DIM], state[HEAD_DIM:]], axis=1)


def mixed_kernel(
    flags_ref, query_ref, *refs, groups
):
    local_refs, refs = refs[:groups], refs[groups:]
    own_ref, got_ref, grad_ref, gain_ref, mixed_ref, sums_ref, states_ref = refs
    gather_states(own_ref, got_ref, states_ref)
    mask = row_mask(flags_ref, FOLLOWS)
    size = CORES * COLUMNS // groups
    squares = jnp.zeros((BLOCK, HEAD_DIM), F32)
    dots = jnp.zeros((BLOCK, HEAD_DIM), F32)
    for k in range(CORES * COLUMNS):
        cols = head(k)
        group, n = divmod(k, size)
        mixed = local_refs[group][:, head(n)] + dot(
            twice(query_ref[:, cols] * mask), states_ref[k], NN
        )
        mixed_ref[:, cols] = mixed
        squares = squares + mixed * mixed
        dots = dots + mixed * (gain_ref[:, cols] * grad_ref[:, cols].astype(F32))
    sums_ref[0:1, :] = jnp.sum(squares.T, axis=0, keepdims=True)
    sums_ref[1:2, :] = jnp.sum(dots.T, axis=0, keepdims=True)


def grad_kernel(
    flags_ref,
    sums_ref,
    sums1_ref,
    sums2_ref,
    sums3_ref,
    mixed_ref,
    grad_ref,
    gain_ref,
    query_ref,
    grad_mixed_ref,
    own_ref,
    other_ref,
    inverse_ref,
):
    core = lax.axis_index("ctx") % CORES
    total = sums_ref[...] + sums1_ref[...] + sums2_ref[...] + sums3_ref[...]
    root = jnp.sqrt(total[0:1, :] / WIDTH + EPSILON)
    over = 1.0 / root
    inverse = jnp.broadcast_to(over, (HEAD_DIM, BLOCK)).T
    inverse_ref[...] = inverse
    dots = jnp.broadcast_to(total[1:2, :] * over / WIDTH, (HEAD_DIM, BLOCK)).T
    mask = row_mask(flags_ref, FIRST)
    for side, out_ref in ((1 - core, other_ref), (core, own_ref)):
        for k in range(COLUMNS):
            cols = head(k, side)
            normed = mixed_ref[:, cols] * inverse
            scaled = gain_ref[:, cols] * grad_ref[:, cols].astype(F32)
            grad_mixed = ((scaled - normed * dots) * inverse).astype(BF16)
            grad_mixed_ref[:, cols] = grad_mixed
            out_ref[rows_of(k), :] = dot(query_ref[:, cols] * mask, grad_mixed, TN)


def normed_kernel(mixed_ref, inverse_ref, gain_ref, out_ref):
    inverse = inverse_ref[...]
    for k in range(CORES * COLUMNS):
        cols = head(k)
        out_ref[:, cols] = (mixed_ref[:, cols] * inverse * gain_ref[:, cols]).astype(BF16)


def back_kernel(
    flags_ref,
    query_ref,
    key_ref,
    value_ref,
    mask_ref,
    grad_ref,
    states_ref,
    query_out_ref,
    key_out_ref,
    value_out_ref,
    *,
    heads,
):
    follows = row_mask(flags_ref, FOLLOWS)
    for n, k in enumerate(heads):
        cols = head(k)
        to = head(n)
        from_state = dot(twice(grad_ref[:, cols] * follows), beside(states_ref[k]), NT)
        for r in range(2):
            rows = slice(r * HALF, (r + 1) * HALF)
            upto = (r + 1) * HALF
            mask = mask_ref[rows, :upto]
            weights = dot(query_ref[rows, cols], key_ref[:upto, cols], NT).astype(BF16) * mask
            grads = dot(grad_ref[rows, cols], value_ref[:upto, cols], NT).astype(BF16) * mask
            query_out_ref[rows, to] = (
                dot(grads, key_ref[:upto, cols], NN) + from_state[rows, :]
            ).astype(BF16)
            key_part = dot(grads, query_ref[rows, cols], TN)
            value_part = dot(weights, grad_ref[rows, cols], TN)
            if r == 0:
                key_out_ref[:HALF, to] = key_part
                value_out_ref[:HALF, to] = value_part
            else:
                key_out_ref[:HALF, to] += key_part[:HALF, :]
                value_out_ref[:HALF, to] += value_part[:HALF, :]
                key_out_ref[HALF:, to] = key_part[HALF:, :]
                value_out_ref[HALF:, to] = value_part[HALF:, :]


def final_kernel(flags_ref, key_ref, value_ref, *refs, groups):
    parts, refs = refs[: 3 * groups], refs[3 * groups :]
    own_ref, got_ref, query_out_ref, key_out_ref, value_out_ref = refs[:5]
    key_buf, value_buf, states_ref, sems = refs[5:]
    size = CORES * COLUMNS // groups
    copies = []

    def send(source, target, sem):
        copies.append(pltpu.make_async_copy(source, target, sem))
        copies[-1].start()

    for g in range(groups):
        cols = slice(g * size * HEAD_DIM, (g + 1) * size * HEAD_DIM)
        send(parts[3 * g], query_out_ref.at[:, cols], sems.at[2, g])
    gather_states(own_ref, got_ref, states_ref)
    leads = row_mask(flags_ref, LEADS)
    for k in range(CORES * COLUMNS):
        cols = head(k)
        group, n = divmod(k, size)
        state = states_ref[k]
        from_values = dot(twice(value_ref[:, cols] * leads), beside(state), NT)
        key_buf[:, cols] = (parts[3 * group + 1][:, head(n)] + from_values).astype(BF16)
        send(key_buf.at[:, cols], key_out_ref.at[:, cols], sems.at[0, k])
        from_keys = dot(twice(key_ref[:, cols] * leads), state, NN)
        value_buf[:, cols] = (parts[3 * group + 2][:, head(n)] + from_keys).astype(BF16)
        send(value_buf.at[:, cols], value_out_ref.at[:, cols], sems.at[1, k])
    for copy in copies:
        copy.wait()


MIX_GROUPS = 2
BACK_GROUPS = 4


def on_device(queries, key_input, value_input, norm_gain, out_grad, doc_lengths):
    rows_here, width_here = queries.shape
    heads_here = width_here // HEAD_DIM
    devices = lax.axis_size("ctx")
    half_rows = COLUMNS * HEAD_DIM

    scalars = pl.BlockSpec(memory_space=pltpu.SMEM)
    vmem = pl.BlockSpec(memory_space=pltpu.VMEM)
    hbm = pl.BlockSpec(memory_space=pltpu.HBM)

    def array(rows, cols, kind=F32):
        return jax.ShapeDtypeStruct((rows, cols), kind)

    wide_f32 = array(rows_here, width_here)
    wide_bf16 = array(rows_here, width_here, BF16)
    wide_buffer = pltpu.VMEM((rows_here, width_here), BF16)
    half = array(half_rows, HEAD_DIM)
    part = array(HEAD_DIM, HEAD_DIM)
    states = jax.ShapeDtypeStruct((heads_here, 2 * HEAD_DIM, HEAD_DIM), BF16)

    product = 2 * rows_here * HEAD_DIM * HEAD_DIM

    def call(body, name, args, shapes, flops, scratch=(), ins=None, outs=None, limit=32, **fixed):
        moved = sum(a.size * a.dtype.itemsize for a in list(args) + list(shapes))
        return pl.pallas_call(
            lambda *refs: body(*refs, **fixed),
            name=name,
            in_specs=ins or [vmem] * len(args),
            out_specs=outs or [vmem] * len(shapes),
            out_shape=list(shapes),
            scratch_shapes=list(scratch),
            compiler_params=pltpu.CompilerParams(vmem_limit_bytes=limit << 20),
            cost_estimate=pl.CostEstimate(flops=flops, bytes_accessed=moved, transcendentals=0),
        )(*args)

    gain = norm_gain.reshape(1, width_here)

    def move(values, source):
        return lax.ppermute(values, "ctx", [(source(i), i) for i in range(devices)])

    def swap(values):
        return move(values, lambda i: i ^ 1)

    def along_row(values):
        return [move(v, lambda i, f=f: i ^ (f * CORES)) for v, f in zip(values, FLIPS)]

    def beneath(after, moved, work):
        started = lax.optimization_barrier((after, *work[0]))
        done = work[1](started[1:])
        moved, done = lax.optimization_barrier((moved, done))
        return moved, done

    def scan(flags, own, other, base, works):
        tag = "back" if base else "ahead"
        row = CORES * COLUMNS
        sign = row if base else -row
        results = []
        got = swap(other)
        keep, *sends = call(
            pair_kernel, "pair_" + tag, (flags, own, got), [part] * 4, 4 * half.size, base=base
        )
        gathered, done = beneath(keep, along_row(sends), works[0])
        results.append(done)
        parts, total = call(
            row_kernel, "row_" + tag, (flags, keep, *gathered), [half, part], 2 * half.size, base=base
        )
        far = move(total, lambda i: (i + 2 * sign) % devices)
        near = move(total, lambda i: (i + sign) % devices)
        (near, far), done = beneath(parts, (near, far), works[1])
        results.append(done)
        keep, *sends = call(
            enter_kernel,
            "enter_" + tag,
            (flags, parts, near, far),
            [part] * 4,
            4 * half.size,
            [pltpu.VMEM((half_rows, HEAD_DIM), F32)],
            base=base,
        )
        back, done = beneath(keep, along_row(sends), works[2])
        results.append(done)
        mine, send = call(
            unpair_kernel,
            "unpair_" + tag,
            (flags, own, got, keep, *back),
            [half, half],
            4 * half.size,
            [pltpu.VMEM((half_rows, HEAD_DIM), F32)],
            base=base,
        )
        return mine, swap(send), results

    own, other, flags = call(
        state_kernel,
        "states",
        (doc_lengths, key_input, value_input),
        [half, half, array(FLAGS, HEAD_DIM)],
        8 * product,
        [wide_buffer, wide_buffer, pltpu.SemaphoreType.DMA((2, GRAINS))],
        [scalars, hbm, hbm],
        limit=53,
    )
    inputs = (queries, key_input, value_input)

    def mask_work(_):
        return call(
            mask_kernel,
            "pair_mask",
            (doc_lengths,),
            [jax.ShapeDtypeStruct((BLOCK, BLOCK), BF16)],
            BLOCK * BLOCK,
            ins=[scalars],
        )

    size = heads_here // MIX_GROUPS
    pair_masks = mask_work(None)

    def mix_work(g):
        def run(args):
            return call(
                local_kernel,
                "local_mix",
                args,
                [array(rows_here, size * HEAD_DIM)],
                6 * size * product,
                heads=range(g * size, (g + 1) * size),
            )

        return (*inputs, *pair_masks), run

    nothing = ((), lambda args: [])
    *entry, local = scan(flags, own, other, 0, [mix_work(0), mix_work(1), nothing])
    local = [x for done in local for x in done]
    mixed, sums, entry_states = call(
        mixed_kernel,
        "mix_states",
        (flags, queries, *local, *entry, out_grad, gain),
        [wide_f32, array(2, rows_here), states],
        16 * product,
        groups=MIX_GROUPS,
    )
    others = [
        lax.ppermute(sums, "head", [(i, i ^ flip) for i in range(lax.axis_size("head"))])
        for flip in FLIPS
    ]
    grad_mixed, own, other, inverse = call(
        grad_kernel,
        "norm_grad",
        (flags, sums, *others, mixed, out_grad, gain, queries),
        [wide_bf16, half, half, array(rows_here, HEAD_DIM)],
        8 * product,
    )
    groups = heads_here // BACK_GROUPS

    def back_work(which, normed=False):
        def run(args):
            out = []
            for g in which:
                out += call(
                    back_kernel,
                    "local_back",
                    args[:7],
                    [array(rows_here, groups * HEAD_DIM, BF16)]
                    + [array(rows_here, groups * HEAD_DIM)] * 2,
                    17 * groups * product,
                    heads=range(g * groups, (g + 1) * groups),
                )
            if normed:
                out += call(normed_kernel, "normed", args[7:], [wide_bf16], 2 * wide_f32.size)
            return out

        args = (flags, *inputs, *pair_masks, grad_mixed, entry_states)
        return args + ((mixed, inverse, gain) if normed else ()), run

    *leave, pieces = scan(
        flags, own, other, DIRECTION, [back_work((0, 1)), back_work((2,)), back_work((3,), True)]
    )
    normed_out = pieces[2].pop()
    pieces = [x for done in pieces for x in done]
    query_grad, key_grad, value_grad = call(
        final_kernel,
        "back_states",
        (flags, key_input, value_input, *pieces, *leave),
        [wide_bf16] * 3,
        32 * product,
        [
            wide_buffer,
            wide_buffer,
            pltpu.VMEM((heads_here, 2 * HEAD_DIM, HEAD_DIM), BF16),
            pltpu.SemaphoreType.DMA((3, heads_here)),
        ],
        outs=[hbm] * 3,
        groups=BACK_GROUPS,
    )
    return (normed_out, query_grad, key_grad, value_grad)


def solution(mesh):
    wide = P("ctx", "head")
    return jax.shard_map(
        on_device,
        mesh=mesh,
        in_specs=(wide, wide, wide, P("head"), wide, P()),
        out_specs=(wide, wide, wide, wide),
        check_vma=False,
    )
```

time: 106 us -> 74.9 us (0.71)
  blocking collectives: 37.9 us -> 0 us
  starting transfers between devices: 13 us -> 37.3 us
  local copies, waits for them, and re-layouts: 15.9 us -> 0.82 us
  Pallas kernels: 29.3 us -> 19.8 us
  waiting for transfers between devices: 8.26 us -> 15.9 us
    all_to_all x2 -> x0, blocking collectives: 37.9 us -> none  [exchange(): return lax.all_to_all(shaped, 'ctx', 0, 0, tiled=True)]
    ppermute x0 -> x20, starting transfers between devices: none -> 33.6 us  [move(): return lax.ppermute(values, 'ctx', [(source(i), i) for i in range(devices)])]
    unnamed x40 -> x12, local copies, waits for them, and re-layouts: 15.9 us -> 0.82 us
    ppermute x0 -> x20, waiting for transfers between devices: none -> 12.8 us  [move(): return lax.ppermute(values, 'ctx', [(source(i), i) for i in range(devices)])]
    pallas_call x8 -> x20, Pallas kernels: 29.3 us -> 19.8 us  [call(): pl.pallas_call(lambda *refs: body(*refs, **fixed), name=name, in_specs=in...]
    all_to_all x2 -> x0, starting transfers between devices: 9.29 us -> none  [scan(): lax.all_to_all(entries, 'ctx', 0, 0, tiled=True)]
    all_to_all x2 -> x0, waiting for transfers between devices: 5.45 us -> none  [scan(): lax.all_to_all(entries, 'ctx', 0, 0, tiled=True)]
  transfers between devices with their start and end apart: 5 -> 23, of which waited for: 3 -> 16; matrix products, arithmetic and copies ran while one was open for 0% -> 0% of each run, Pallas kernels for 14% -> 16%
where the time goes in v3:
time: 74.9 us; the launch traced here: 74.7 us
  starting transfers between devices  37.3 us (50%)
  Pallas kernels  19.8 us (26%)
  waiting for transfers between devices  15.9 us (21%)
  between operations  1.03 us (1%)
  local copies, waits for them, and re-layouts  0.82 us (1%)
    ppermute x20, starting transfers between devices, move(): return lax.ppermute(values, 'ctx', [(source(i), i) for i in range(devices)])  33.6 us
    pallas_call x20, Pallas kernels, call(): pl.pallas_call(lambda *refs: body(*refs, **fixed), name=name, in_specs=in...  19.8 us
    ppermute x20, waiting for transfers between devices, move(): return lax.ppermute(values, 'ctx', [(source(i), i) for i in range(devices)])  12.8 us
    ppermute x3, starting transfers between devices, on_device(): lax.ppermute(sums, 'head', [(i, i ^ flip) for i in range(lax.axis_size('h...  3.69 us
    ppermute x3, waiting for transfers between devices, on_device(): lax.ppermute(sums, 'head', [(i, i ^ flip) for i in range(lax.axis_size('h...  3.11 us
  transfers between devices with their start and end apart: 23, of which 16 were waited for; matrix products, arithmetic and copies ran while one was open for 0% of the time, Pallas kernels for 16%

profile of v3, /device:TPU:1, one launch (start us, length us, event | category | flops | bytes accessed | tf_op | source)
XLA Modules:
  0.0 74.7 jit_solution(198828501358173042)
XLA Ops:
  1.5 2.8 %states.1 = (f32[512,128]{1,0:T(8,128)S(1)}, f32[512,128]{1,0:T(8,128)S(1)}, f32[32,128]{1,0:T(8,128)S(1)}) custom-call(s32[8]{0:T(128)S(1)} %copy-done.5, bf16[512,1024]{1,0:T(8,128)(2,1)} %refs_1_.11, bf16[512,1024]{1,0:T(8,128)(2,1)} %refs_2_.9), custom_call_target="tpu_custom_call" | custom-call | flops 134217728 | bytes 2637856 | tf_op jit(solution)/shard_map/states/pallas_call | solution.py:449
  4.2 1.5 %collective-permute-start = (f32[512,128]{1,0:T(8,128)S(1)}, f32[512,128]{1,0:T(8,128)S(1)}, u32[]{:S(2)}, u32[]{:S(2)}) collective-permute-start(f32[512,128]{1,0:T(8,128)S(1)} %get-tuple-element.118), channel_id=1, source_target_pairs={{1,0},{0,1},{3,2},{2,3},{5,4},{4,5},{7,6},{6,7},{9,8},{8,9},{11,10... | collective-permute-start | bytes 786440 | tf_op jit(solution)/shard_map/ppermute | solution.py:463
  6.9 3.1 %collective-permute-start.1 = (f32[128,128]{1,0:T(8,128)S(1)}, f32[128,128]{1,0:T(8,128)S(1)}, u32[]{:S(2)}, u32[]{:S(2)}) collective-permute-start(f32[128,128]{1,0:T(8,128)S(1)} %get-tuple-element.119), channel_id=1, source_target_pairs={{4,0},{5,1},{6,2},{7,3},{0,4},{1,5},{2,6},{3,7},{12,8},{13,9},{14,... | collective-permute-start | bytes 196616 | tf_op jit(solution)/shard_map/ppermute | solution.py:463
  11.4 1.5 %local_mix.2.refs_2_ = f32[512,512]{1,0:T(8,128)S(1)} custom-call(bf16[512,1024]{1,0:T(8,128)(2,1)S(1)} %copy-done.2, bf16[512,1024]{1,0:T(8,128)(2,1)S(1)} %copy-done, bf16[512,1024]{1,0:T(8,128)(2,1)S(1)} %copy-done.1, bf16[512,512]{1,0:T(8,128)(2,1)S(1)} %pair_mask.1.refs_3_.refs_4_), custom_call_target="tpu_custom_call" | custom-call | flops 402653184 | bytes 4718592 | tf_op jit(solution)/shard_map/local_mix/pallas_call | solution.py:449
  14.8 1.7 %collective-permute-start.4 = (f32[128,128]{1,0:T(8,128)S(1)}, f32[128,128]{1,0:T(8,128)S(1)}, u32[]{:S(2)}, u32[]{:S(2)}) collective-permute-start(f32[128,128]{1,0:T(8,128)S(1)} %get-tuple-element.131), channel_id=1, source_target_pairs={{24,0},{25,1},{26,2},{27,3},{28,4},{29,5},{30,6},{31,7},{0,8},{1,9... | collective-permute-start | bytes 196616 | tf_op jit(solution)/shard_map/ppermute | solution.py:463
  16.5 3.3 %collective-permute-start.5 = (f32[128,128]{1,0:T(8,128)S(1)}, f32[128,128]{1,0:T(8,128)S(1)}, u32[]{:S(2)}, u32[]{:S(2)}) collective-permute-start(f32[128,128]{1,0:T(8,128)S(1)} %get-tuple-element.131), channel_id=1, source_target_pairs={{16,0},{17,1},{18,2},{19,3},{20,4},{21,5},{22,6},{23,7},{24,8},{25... | collective-permute-start | bytes 196616 | tf_op jit(solution)/shard_map/ppermute | solution.py:463
  19.8 1.5 %local_mix.3.refs_3_ = f32[512,512]{1,0:T(8,128)S(1)} custom-call(bf16[512,1024]{1,0:T(8,128)(2,1)S(1)} %copy-done.2, bf16[512,1024]{1,0:T(8,128)(2,1)S(1)} %copy-done, bf16[512,1024]{1,0:T(8,128)(2,1)S(1)} %copy-done.1, bf16[512,512]{1,0:T(8,128)(2,1)S(1)} %pair_mask.1.refs_3_.refs_4_), custom_call_target="tpu_custom_call" | custom-call | flops 402653184 | bytes 4718592 | tf_op jit(solution)/shard_map/local_mix/pallas_call | solution.py:449
  22.2 1.7 %collective-permute-start.6 = (f32[128,128]{1,0:T(8,128)S(1)}, f32[128,128]{1,0:T(8,128)S(1)}, u32[]{:S(2)}, u32[]{:S(2)}) collective-permute-start(f32[128,128]{1,0:T(8,128)S(1)} %get-tuple-element.141), channel_id=1, source_target_pairs={{4,0},{5,1},{6,2},{7,3},{0,4},{1,5},{2,6},{3,7},{12,8},{13,9},{14,... | collective-permute-start | bytes 196616 | tf_op jit(solution)/shard_map/ppermute | solution.py:463
  25.6 1.4 %collective-permute-done.6.refs_4_ = f32[128,128]{1,0:T(8,128)S(1)} collective-permute-done((f32[128,128]{1,0:T(8,128)S(1)}, f32[128,128]{1,0:T(8,128)S(1)}, u32[]{:S(2)}, u32[]{:S(2)}) %collective-permute-start.6) | collective-permute-done | bytes 65568 | tf_op jit(solution)/shard_map/ppermute | solution.py:463
  27.1 1.7 %collective-permute-done.8.refs_6_ = f32[128,128]{1,0:T(8,128)S(1)} collective-permute-done((f32[128,128]{1,0:T(8,128)S(1)}, f32[128,128]{1,0:T(8,128)S(1)}, u32[]{:S(2)}, u32[]{:S(2)}) %collective-permute-start.8) | collective-permute-done | bytes 65568 | tf_op jit(solution)/shard_map/ppermute | solution.py:463
  28.9 3.9 %collective-permute-start.9 = (f32[512,128]{1,0:T(8,128)S(1)}, f32[512,128]{1,0:T(8,128)S(1)}, u32[]{:S(2)}, u32[]{:S(2)}) collective-permute-start(f32[512,128]{1,0:T(8,128)S(1)} %get-tuple-element.148), channel_id=1, source_target_pairs={{1,0},{0,1},{3,2},{2,3},{5,4},{4,5},{7,6},{6,7},{9,8},{8,9},{11,10... | collective-permute-start | bytes 786440 | tf_op jit(solution)/shard_map/ppermute | solution.py:463
  35.1 2.8 %collective-permute-start.10 = (f32[2,512]{1,0:T(2,128)S(1)}, f32[2,512]{1,0:T(2,128)S(1)}, u32[]{:S(2)}, u32[]{:S(2)}) collective-permute-start(f32[2,512]{1,0:T(2,128)S(1)} %get-tuple-element.149.refs_1_), channel_id=1, source_target_pairs={{0,64},{32,96},{64,0},{96,32},{1,65},{33,97},{65,1},{97,33},{2,66}... | collective-permute-start | bytes 12296 | tf_op jit(solution)/shard_map/ppermute | solution.py:567
  40.3 1.5 %collective-permute-done.12.refs_4_ = f32[2,512]{1,0:T(2,128)S(1)} collective-permute-done((f32[2,512]{1,0:T(2,128)S(1)}, f32[2,512]{1,0:T(2,128)S(1)}, u32[]{:S(2)}, u32[]{:S(2)}) %collective-permute-start.12) | collective-permute-done | bytes 4128 | tf_op jit(solution)/shard_map/ppermute | solution.py:567
  41.9 1.4 %norm_grad.1 = (bf16[512,1024]{1,0:T(8,128)(2,1)S(1)}, f32[512,128]{1,0:T(8,128)S(1)}, f32[512,128]{1,0:T(8,128)S(1)}, f32[512,128]{1,0:T(8,128)S(1)}) custom-call(f32[32,128]{1,0:T(8,128)S(1)} %get-tuple-element.194.refs_0_, f32[2,512]{1,0:T(2,128)S(1)} %get-tuple-element.149.refs_1_, f32[2,512]{1,0:T(2,128)S(1)} %collective-permute-done.10.refs_2_, ...), custom_call_target="tpu_custom_call" | custom-call | flops 134217728 | bytes 6066176 | tf_op jit(solution)/shard_map/norm_grad/pallas_call | solution.py:449
  43.3 2.2 %collective-permute-start.13 = (f32[512,128]{1,0:T(8,128)S(1)}, f32[512,128]{1,0:T(8,128)S(1)}, u32[]{:S(2)}, u32[]{:S(2)}) collective-permute-start(f32[512,128]{1,0:T(8,128)S(1)} %get-tuple-element.152), channel_id=1, source_target_pairs={{1,0},{0,1},{3,2},{2,3},{5,4},{4,5},{7,6},{6,7},{9,8},{8,9},{11,10... | collective-permute-start | bytes 786440 | tf_op jit(solution)/shard_map/ppermute | solution.py:463
  47.9 1.6 %collective-permute-start.15 = (f32[128,128]{1,0:T(8,128)S(1)}, f32[128,128]{1,0:T(8,128)S(1)}, u32[]{:S(2)}, u32[]{:S(2)}) collective-permute-start(f32[128,128]{1,0:T(8,128)S(1)} %get-tuple-element.155), channel_id=1, source_target_pairs={{2,0},{3,1},{0,2},{1,3},{6,4},{7,5},{4,6},{5,7},{10,8},{11,9},{8,1... | collective-permute-start | bytes 196616 | tf_op jit(solution)/shard_map/ppermute | solution.py:463
  50.0 1.7 %local_back.5 = (bf16[512,256]{1,0:T(8,128)(2,1)S(1)}, f32[512,256]{1,0:T(8,128)S(1)}, f32[512,256]{1,0:T(8,128)S(1)}) custom-call(f32[32,128]{1,0:T(8,128)S(1)} %get-tuple-element.194.refs_0_, bf16[512,1024]{1,0:T(8,128)(2,1)S(1)} %copy-done.2, bf16[512,1024]{1,0:T(8,128)(2,1)S(1)} %copy-done, bf16[512,1024]{1,0:T(8,128)(2,1)S(1)} %copy-done.1, ...), custom_call_target="tpu_custom_call" | custom-call | flops 570425344 | bytes 6569984 | tf_op jit(solution)/shard_map/local_back/pallas_call | solution.py:449
  51.7 1.7 %local_back.4 = (bf16[512,256]{1,0:T(8,128)(2,1)S(1)}, f32[512,256]{1,0:T(8,128)S(1)}, f32[512,256]{1,0:T(8,128)S(1)}) custom-call(f32[32,128]{1,0:T(8,128)S(1)} %get-tuple-element.194.refs_0_, bf16[512,1024]{1,0:T(8,128)(2,1)S(1)} %copy-done.2, bf16[512,1024]{1,0:T(8,128)(2,1)S(1)} %copy-done, bf16[512,1024]{1,0:T(8,128)(2,1)S(1)} %copy-done.1, ...), custom_call_target="tpu_custom_call" | custom-call | flops 570425344 | bytes 6569984 | tf_op jit(solution)/shard_map/local_back/pallas_call | solution.py:449
  55.1 1.5 %collective-permute-start.18 = (f32[128,128]{1,0:T(8,128)S(1)}, f32[128,128]{1,0:T(8,128)S(1)}, u32[]{:S(2)}, u32[]{:S(2)}) collective-permute-start(f32[128,128]{1,0:T(8,128)S(1)} %get-tuple-element.176), channel_id=1, source_target_pairs={{16,0},{17,1},{18,2},{19,3},{20,4},{21,5},{22,6},{23,7},{24,8},{25... | collective-permute-start | bytes 196616 | tf_op jit(solution)/shard_map/ppermute | solution.py:463
  56.6 1.7 %local_back.6 = (bf16[512,256]{1,0:T(8,128)(2,1)S(1)}, f32[512,256]{1,0:T(8,128)S(1)}, f32[512,256]{1,0:T(8,128)S(1)}) custom-call(f32[32,128]{1,0:T(8,128)S(1)} %get-tuple-element.194.refs_0_, bf16[512,1024]{1,0:T(8,128)(2,1)S(1)} %copy-done.2, bf16[512,1024]{1,0:T(8,128)(2,1)S(1)} %copy-done, bf16[512,1024]{1,0:T(8,128)(2,1)S(1)} %copy-done.1, ...), custom_call_target="tpu_custom_call" | custom-call | flops 570425344 | bytes 6569984 | tf_op jit(solution)/shard_map/local_back/pallas_call | solution.py:449
  60.9 1.5 %collective-permute-start.20 = (f32[128,128]{1,0:T(8,128)S(1)}, f32[128,128]{1,0:T(8,128)S(1)}, u32[]{:S(2)}, u32[]{:S(2)}) collective-permute-start(f32[128,128]{1,0:T(8,128)S(1)} %get-tuple-element.190), channel_id=1, source_target_pairs={{2,0},{3,1},{0,2},{1,3},{6,4},{7,5},{4,6},{5,7},{10,8},{11,9},{8,1... | collective-permute-start | bytes 196616 | tf_op jit(solution)/shard_map/ppermute | solution.py:463
  64.5 1.7 %local_back.7 = (bf16[512,256]{1,0:T(8,128)(2,1)S(1)}, f32[512,256]{1,0:T(8,128)S(1)}, f32[512,256]{1,0:T(8,128)S(1)}) custom-call(f32[32,128]{1,0:T(8,128)S(1)} %get-tuple-element.194.refs_0_, bf16[512,1024]{1,0:T(8,128)(2,1)S(1)} %copy-done.2, bf16[512,1024]{1,0:T(8,128)(2,1)S(1)} %copy-done, bf16[512,1024]{1,0:T(8,128)(2,1)S(1)} %copy-done.1, ...), custom_call_target="tpu_custom_call" | custom-call | flops 570425344 | bytes 6569984 | tf_op jit(solution)/shard_map/local_back/pallas_call | solution.py:449
  66.8 4.4 %collective-permute-start.22 = (f32[512,128]{1,0:T(8,128)S(1)}, f32[512,128]{1,0:T(8,128)S(1)}, u32[]{:S(2)}, u32[]{:S(2)}) collective-permute-start(f32[512,128]{1,0:T(8,128)S(1)} %get-tuple-element.224), channel_id=1, source_target_pairs={{1,0},{0,1},{3,2},{2,3},{5,4},{4,5},{7,6},{6,7},{9,8},{8,9},{11,10... | collective-permute-start | bytes 786440 | tf_op jit(solution)/shard_map/ppermute | solution.py:463
  72.3 2.2 %back_states.1 = (bf16[512,1024]{1,0:T(8,128)(2,1)}, bf16[512,1024]{1,0:T(8,128)(2,1)}, bf16[512,1024]{1,0:T(8,128)(2,1)}) custom-call(f32[32,128]{1,0:T(8,128)S(1)} %get-tuple-element.194.refs_0_, bf16[512,1024]{1,0:T(8,128)(2,1)S(1)} %copy-done, bf16[512,1024]{1,0:T(8,128)(2,1)S(1)} %copy-done.1, bf16[512,256]{1,0:T(8,128)(2,1)S(1)} %get-tuple-element.208.refs_3_, ...), custom_call_target="tpu_custom_call" | custom-call | flops 536870912 | bytes 11026432 | tf_op jit(solution)/shard_map/back_states/pallas_call | solution.py:449
  (54 shorter events, 23.6 us)
Async XLA Ops:
  4.2 2.7 %collective-permute-start = (f32[512,128]{1,0:T(8,128)S(1)}, f32[512,128]{1,0:T(8,128)S(1)}, u32[]{:S(2)}, u32[]{:S(2)}) collective-permute-start(f32[512,128]{1,0:T(8,128)S(1)} %get-tuple-element.118), channel_id=1, source_target_pairs={{1,0},{0,1},{3,2},{2,3},{5,4},{4,5},{7,6},{6,7},{9,8},{8,9},{11,10... | collective-permute-start | bytes 786440 | tf_op jit(solution)/shard_map/ppermute | solution.py:463
  6.9 6.0 %collective-permute-start.1 = (f32[128,128]{1,0:T(8,128)S(1)}, f32[128,128]{1,0:T(8,128)S(1)}, u32[]{:S(2)}, u32[]{:S(2)}) collective-permute-start(f32[128,128]{1,0:T(8,128)S(1)} %get-tuple-element.119), channel_id=1, source_target_pairs={{4,0},{5,1},{6,2},{7,3},{0,4},{1,5},{2,6},{3,7},{12,8},{13,9},{14,... | collective-permute-start | bytes 196616 | tf_op jit(solution)/shard_map/ppermute | solution.py:463
  10.0 3.9 %collective-permute-start.2 = (f32[128,128]{1,0:T(8,128)S(1)}, f32[128,128]{1,0:T(8,128)S(1)}, u32[]{:S(2)}, u32[]{:S(2)}) collective-permute-start(f32[128,128]{1,0:T(8,128)S(1)} %get-tuple-element.120), channel_id=1, source_target_pairs={{2,0},{3,1},{0,2},{1,3},{6,4},{7,5},{4,6},{5,7},{10,8},{11,9},{8,1... | collective-permute-start | bytes 196616 | tf_op jit(solution)/shard_map/ppermute | solution.py:463
  10.4 4.3 %collective-permute-start.3 = (f32[128,128]{1,0:T(8,128)S(1)}, f32[128,128]{1,0:T(8,128)S(1)}, u32[]{:S(2)}, u32[]{:S(2)}) collective-permute-start(f32[128,128]{1,0:T(8,128)S(1)} %get-tuple-element.121), channel_id=1, source_target_pairs={{6,0},{7,1},{4,2},{5,3},{2,4},{3,5},{0,6},{1,7},{14,8},{15,9},{12,... | collective-permute-start | bytes 196616 | tf_op jit(solution)/shard_map/ppermute | solution.py:463
  14.8 6.5 %collective-permute-start.4 = (f32[128,128]{1,0:T(8,128)S(1)}, f32[128,128]{1,0:T(8,128)S(1)}, u32[]{:S(2)}, u32[]{:S(2)}) collective-permute-start(f32[128,128]{1,0:T(8,128)S(1)} %get-tuple-element.131), channel_id=1, source_target_pairs={{24,0},{25,1},{26,2},{27,3},{28,4},{29,5},{30,6},{31,7},{0,8},{1,9... | collective-permute-start | bytes 196616 | tf_op jit(solution)/shard_map/ppermute | solution.py:463
  16.5 5.7 %collective-permute-start.5 = (f32[128,128]{1,0:T(8,128)S(1)}, f32[128,128]{1,0:T(8,128)S(1)}, u32[]{:S(2)}, u32[]{:S(2)}) collective-permute-start(f32[128,128]{1,0:T(8,128)S(1)} %get-tuple-element.131), channel_id=1, source_target_pairs={{16,0},{17,1},{18,2},{19,3},{20,4},{21,5},{22,6},{23,7},{24,8},{25... | collective-permute-start | bytes 196616 | tf_op jit(solution)/shard_map/ppermute | solution.py:463
  19.8 14.1 %copy-start.4 = (f32[1024]{0:T(1024)S(1)}, f32[1024]{0:T(1024)}, u32[]{:S(2)}) copy-start(f32[1024]{0:T(1024)} %param.9) | copy-start | bytes 12292
  22.2 4.7 %collective-permute-start.6 = (f32[128,128]{1,0:T(8,128)S(1)}, f32[128,128]{1,0:T(8,128)S(1)}, u32[]{:S(2)}, u32[]{:S(2)}) collective-permute-start(f32[128,128]{1,0:T(8,128)S(1)} %get-tuple-element.141), channel_id=1, source_target_pairs={{4,0},{5,1},{6,2},{7,3},{0,4},{1,5},{2,6},{3,7},{12,8},{13,9},{14,... | collective-permute-start | bytes 196616 | tf_op jit(solution)/shard_map/ppermute | solution.py:463
  24.0 3.1 %collective-permute-start.7 = (f32[128,128]{1,0:T(8,128)S(1)}, f32[128,128]{1,0:T(8,128)S(1)}, u32[]{:S(2)}, u32[]{:S(2)}) collective-permute-start(f32[128,128]{1,0:T(8,128)S(1)} %get-tuple-element.142), channel_id=1, source_target_pairs={{2,0},{3,1},{0,2},{1,3},{6,4},{7,5},{4,6},{5,7},{10,8},{11,9},{8,1... | collective-permute-start | bytes 196616 | tf_op jit(solution)/shard_map/ppermute | solution.py:463
  24.5 4.3 %collective-permute-start.8 = (f32[128,128]{1,0:T(8,128)S(1)}, f32[128,128]{1,0:T(8,128)S(1)}, u32[]{:S(2)}, u32[]{:S(2)}) collective-permute-start(f32[128,128]{1,0:T(8,128)S(1)} %get-tuple-element.143), channel_id=1, source_target_pairs={{6,0},{7,1},{4,2},{5,3},{2,4},{3,5},{0,6},{1,7},{14,8},{15,9},{12,... | collective-permute-start | bytes 196616 | tf_op jit(solution)/shard_map/ppermute | solution.py:463
  28.9 5.1 %collective-permute-start.9 = (f32[512,128]{1,0:T(8,128)S(1)}, f32[512,128]{1,0:T(8,128)S(1)}, u32[]{:S(2)}, u32[]{:S(2)}) collective-permute-start(f32[512,128]{1,0:T(8,128)S(1)} %get-tuple-element.148), channel_id=1, source_target_pairs={{1,0},{0,1},{3,2},{2,3},{5,4},{4,5},{7,6},{6,7},{9,8},{8,9},{11,10... | collective-permute-start | bytes 786440 | tf_op jit(solution)/shard_map/ppermute | solution.py:463
  35.1 4.0 %collective-permute-start.10 = (f32[2,512]{1,0:T(2,128)S(1)}, f32[2,512]{1,0:T(2,128)S(1)}, u32[]{:S(2)}, u32[]{:S(2)}) collective-permute-start(f32[2,512]{1,0:T(2,128)S(1)} %get-tuple-element.149.refs_1_), channel_id=1, source_target_pairs={{0,64},{32,96},{64,0},{96,32},{1,65},{33,97},{65,1},{97,33},{2,66}... | collective-permute-start | bytes 12296 | tf_op jit(solution)/shard_map/ppermute | solution.py:567
  37.9 2.5 %collective-permute-start.11 = (f32[2,512]{1,0:T(2,128)S(1)}, f32[2,512]{1,0:T(2,128)S(1)}, u32[]{:S(2)}, u32[]{:S(2)}) collective-permute-start(f32[2,512]{1,0:T(2,128)S(1)} %get-tuple-element.149.refs_1_), channel_id=1, source_target_pairs={{0,32},{32,0},{64,96},{96,64},{1,33},{33,1},{65,97},{97,65},{2,34}... | collective-permute-start | bytes 12296 | tf_op jit(solution)/shard_map/ppermute | solution.py:567
  38.2 3.7 %collective-permute-start.12 = (f32[2,512]{1,0:T(2,128)S(1)}, f32[2,512]{1,0:T(2,128)S(1)}, u32[]{:S(2)}, u32[]{:S(2)}) collective-permute-start(f32[2,512]{1,0:T(2,128)S(1)} %get-tuple-element.149.refs_1_), channel_id=1, source_target_pairs={{0,96},{32,64},{64,32},{96,0},{1,97},{33,65},{65,33},{97,1},{2,98}... | collective-permute-start | bytes 12296 | tf_op jit(solution)/shard_map/ppermute | solution.py:567
  43.3 3.3 %collective-permute-start.13 = (f32[512,128]{1,0:T(8,128)S(1)}, f32[512,128]{1,0:T(8,128)S(1)}, u32[]{:S(2)}, u32[]{:S(2)}) collective-permute-start(f32[512,128]{1,0:T(8,128)S(1)} %get-tuple-element.152), channel_id=1, source_target_pairs={{1,0},{0,1},{3,2},{2,3},{5,4},{4,5},{7,6},{6,7},{9,8},{8,9},{11,10... | collective-permute-start | bytes 786440 | tf_op jit(solution)/shard_map/ppermute | solution.py:463
  46.6 6.8 %collective-permute-start.14 = (f32[128,128]{1,0:T(8,128)S(1)}, f32[128,128]{1,0:T(8,128)S(1)}, u32[]{:S(2)}, u32[]{:S(2)}) collective-permute-start(f32[128,128]{1,0:T(8,128)S(1)} %get-tuple-element.154), channel_id=1, source_target_pairs={{4,0},{5,1},{6,2},{7,3},{0,4},{1,5},{2,6},{3,7},{12,8},{13,9},{14,... | collective-permute-start | bytes 196616 | tf_op jit(solution)/shard_map/ppermute | solution.py:463
  47.9 5.6 %collective-permute-start.15 = (f32[128,128]{1,0:T(8,128)S(1)}, f32[128,128]{1,0:T(8,128)S(1)}, u32[]{:S(2)}, u32[]{:S(2)}) collective-permute-start(f32[128,128]{1,0:T(8,128)S(1)} %get-tuple-element.155), channel_id=1, source_target_pairs={{2,0},{3,1},{0,2},{1,3},{6,4},{7,5},{4,6},{5,7},{10,8},{11,9},{8,1... | collective-permute-start | bytes 196616 | tf_op jit(solution)/shard_map/ppermute | solution.py:463
  49.5 4.3 %collective-permute-start.16 = (f32[128,128]{1,0:T(8,128)S(1)}, f32[128,128]{1,0:T(8,128)S(1)}, u32[]{:S(2)}, u32[]{:S(2)}) collective-permute-start(f32[128,128]{1,0:T(8,128)S(1)} %get-tuple-element.156), channel_id=1, source_target_pairs={{6,0},{7,1},{4,2},{5,3},{2,4},{3,5},{0,6},{1,7},{14,8},{15,9},{12,... | collective-permute-start | bytes 196616 | tf_op jit(solution)/shard_map/ppermute | solution.py:463
  53.9 4.5 %collective-permute-start.17 = (f32[128,128]{1,0:T(8,128)S(1)}, f32[128,128]{1,0:T(8,128)S(1)}, u32[]{:S(2)}, u32[]{:S(2)}) collective-permute-start(f32[128,128]{1,0:T(8,128)S(1)} %get-tuple-element.176), channel_id=1, source_target_pairs={{8,0},{9,1},{10,2},{11,3},{12,4},{13,5},{14,6},{15,7},{16,8},{17,9... | collective-permute-start | bytes 196616 | tf_op jit(solution)/shard_map/ppermute | solution.py:463
  55.1 4.6 %collective-permute-start.18 = (f32[128,128]{1,0:T(8,128)S(1)}, f32[128,128]{1,0:T(8,128)S(1)}, u32[]{:S(2)}, u32[]{:S(2)}) collective-permute-start(f32[128,128]{1,0:T(8,128)S(1)} %get-tuple-element.176), channel_id=1, source_target_pairs={{16,0},{17,1},{18,2},{19,3},{20,4},{21,5},{22,6},{23,7},{24,8},{25... | collective-permute-start | bytes 196616 | tf_op jit(solution)/shard_map/ppermute | solution.py:463
  59.8 6.4 %collective-permute-start.19 = (f32[128,128]{1,0:T(8,128)S(1)}, f32[128,128]{1,0:T(8,128)S(1)}, u32[]{:S(2)}, u32[]{:S(2)}) collective-permute-start(f32[128,128]{1,0:T(8,128)S(1)} %get-tuple-element.189), channel_id=1, source_target_pairs={{4,0},{5,1},{6,2},{7,3},{0,4},{1,5},{2,6},{3,7},{12,8},{13,9},{14,... | collective-permute-start | bytes 196616 | tf_op jit(solution)/shard_map/ppermute | solution.py:463
  60.9 5.3 %collective-permute-start.20 = (f32[128,128]{1,0:T(8,128)S(1)}, f32[128,128]{1,0:T(8,128)S(1)}, u32[]{:S(2)}, u32[]{:S(2)}) collective-permute-start(f32[128,128]{1,0:T(8,128)S(1)} %get-tuple-element.190), channel_id=1, source_target_pairs={{2,0},{3,1},{0,2},{1,3},{6,4},{7,5},{4,6},{5,7},{10,8},{11,9},{8,1... | collective-permute-start | bytes 196616 | tf_op jit(solution)/shard_map/ppermute | solution.py:463
  62.3 4.3 %collective-permute-start.21 = (f32[128,128]{1,0:T(8,128)S(1)}, f32[128,128]{1,0:T(8,128)S(1)}, u32[]{:S(2)}, u32[]{:S(2)}) collective-permute-start(f32[128,128]{1,0:T(8,128)S(1)} %get-tuple-element.191), channel_id=1, source_target_pairs={{6,0},{7,1},{4,2},{5,3},{2,4},{3,5},{0,6},{1,7},{14,8},{15,9},{12,... | collective-permute-start | bytes 196616 | tf_op jit(solution)/shard_map/ppermute | solution.py:463
  66.8 5.6 %collective-permute-start.22 = (f32[512,128]{1,0:T(8,128)S(1)}, f32[512,128]{1,0:T(8,128)S(1)}, u32[]{:S(2)}, u32[]{:S(2)}) collective-permute-start(f32[512,128]{1,0:T(8,128)S(1)} %get-tuple-element.224), channel_id=1, source_target_pairs={{1,0},{0,1},{3,2},{2,3},{5,4},{4,5},{7,6},{6,7},{9,8},{8,9},{11,10... | collective-permute-start | bytes 786440 | tf_op jit(solution)/shard_map/ppermute | solution.py:463
  (5 other events, 47.3 us)

commit v4 on v3

--- a/solution.py
+++ b/solution.py
@@ -36,6 +36,11 @@
 def place():
     index = lax.axis_index("ctx")
     return index // (CORES * COLUMNS), (index // CORES) % COLUMNS, index % CORES
+
+
+def half_kept():
+    row, column, core = place()
+    return (row + column + core) % CORES
 
 
 def doc_starts(lengths_ref):
@@ -72,7 +77,8 @@
 FOLLOWS = 2 * DIRECTION
 FIRST = FOLLOWS + GRAINS
 LEADS = FIRST + GRAINS
-FLAGS = 32
+SAME = LEADS + GRAINS
+FLAGS = 40
 
 
 def write_flags(lengths_ref, flags_ref):
@@ -106,6 +112,9 @@
     for base, doc in ((FOLLOWS, docs[0]), (FIRST, docs[1]), (LEADS, docs[GRAINS + 1])):
         for g in range(GRAINS):
             put(base + g, (docs[1 + g] == doc).astype(F32))
+    for i in range(GRAINS):
+        for j in range(i):
+            put(SAME + i * (i - 1) // 2 + j, (docs[1 + i] == docs[1 + j]).astype(F32))
 
 
 def flag(flags_ref, at):
@@ -119,14 +128,7 @@
     return jnp.concatenate(parts, axis=0).astype(BF16)
 
 
-def rows_equal(docs, doc):
-    parts = [
-        jnp.full((GRAIN, HEAD_DIM), (docs[1 + g] == doc).astype(F32), F32) for g in range(GRAINS)
-    ]
-    return jnp.concatenate(parts, axis=0).astype(BF16)
-
-
-def pair_mask(docs):
+def pair_mask(flags_ref):
     rows = lax.broadcasted_iota(I32, (GRAIN, GRAIN), 0)
     cols = lax.broadcasted_iota(I32, (GRAIN, GRAIN), 1)
     lower = jnp.where(rows >= cols, 1.0, 0.0).astype(F32)
@@ -135,8 +137,8 @@
         line = []
         for j in range(GRAINS):
             if j < i:
-                same = (docs[1 + i] == docs[1 + j]).astype(F32)
-                line.append(jnp.full((GRAIN, GRAIN), same, F32))
+                same = flag(flags_ref, SAME + i * (i - 1) // 2 + j)
+                line.append(jnp.broadcast_to(same, (GRAIN, GRAIN)))
             elif j == i:
                 line.append(lower)
             else:
@@ -170,9 +172,11 @@
 
 
 def state_kernel(
-    lengths_ref, key_ref, value_ref, own_ref, other_ref, flags_ref, key_buf, value_buf, sems
+    given_ref, key_ref, value_ref, own_ref, other_ref, flags_ref, key_buf, value_buf, lengths_ref, sems
 ):
-    core = lax.axis_index("ctx") % CORES
+    mine = half_kept()
+    read = pltpu.make_async_copy(given_ref, lengths_ref, sems.at[2, 0])
+    read.start()
     loads = []
     for g in range(GRAINS):
         rows = slice(g * GRAIN, (g + 1) * GRAIN)
@@ -182,6 +186,7 @@
             copy.start()
             pair.append(copy)
         loads.append(pair)
+    read.wait()
     write_flags(lengths_ref, flags_ref)
     docs = grain_docs(lengths_ref)
     for g in range(0, GRAINS, 2):
@@ -193,7 +198,7 @@
             for i in (g, g + 1)
         ]
         mask = jnp.concatenate(parts, axis=0).astype(BF16)
-        for side, out_ref in ((1 - core, other_ref), (core, own_ref)):
+        for side, out_ref in ((1 - mine, other_ref), (mine, own_ref)):
             for k in range(COLUMNS):
                 cols = head(k, side)
                 state = dot(key_buf[rows, cols] * mask, value_buf[rows, cols], TN)
@@ -259,8 +264,8 @@
         send_ref[...] = whole_ref[...]
 
 
-def mask_kernel(lengths_ref, mask_ref):
-    mask_ref[...] = pair_mask(grain_docs(lengths_ref))
+def mask_kernel(flags_ref, mask_ref):
+    mask_ref[...] = pair_mask(flags_ref)
 
 
 def local_kernel(query_ref, key_ref, value_ref, mask_ref, out_ref, *, heads):
@@ -275,8 +280,8 @@
 
 
 def gather_states(own_ref, got_ref, out_ref):
-    core = lax.axis_index("ctx") % CORES
-    for side, in_ref in ((core, own_ref), (1 - core, got_ref)):
+    mine = half_kept()
+    for side, in_ref in ((mine, own_ref), (1 - mine, got_ref)):
         for k in range(COLUMNS):
             out_ref[side * COLUMNS + k] = split(in_ref[rows_of(k), :])
 
@@ -323,7 +328,7 @@
     other_ref,
     inverse_ref,
 ):
-    core = lax.axis_index("ctx") % CORES
+    mine = half_kept()
     total = sums_ref[...] + sums1_ref[...] + sums2_ref[...] + sums3_ref[...]
     root = jnp.sqrt(total[0:1, :] / WIDTH + EPSILON)
     over = 1.0 / root
@@ -331,7 +336,7 @@
     inverse_ref[...] = inverse
     dots = jnp.broadcast_to(total[1:2, :] * over / WIDTH, (HEAD_DIM, BLOCK)).T
     mask = row_mask(flags_ref, FIRST)
-    for side, out_ref in ((1 - core, other_ref), (core, own_ref)):
+    for side, out_ref in ((1 - mine, other_ref), (mine, own_ref)):
         for k in range(COLUMNS):
             cols = head(k, side)
             normed = mixed_ref[:, cols] * inverse
@@ -388,10 +393,22 @@
                 value_out_ref[HALF:, to] = value_part[HALF:, :]
 
 
+def store_kernel(*refs):
+    parts, (out_ref, sems) = refs[:-2], refs[-2:]
+    copies = []
+    for g, part_ref in enumerate(parts):
+        width = part_ref.shape[1]
+        to = out_ref.at[:, g * width : (g + 1) * width]
+        copies.append(pltpu.make_async_copy(part_ref, to, sems.at[g]))
+        copies[-1].start()
+    for copy in copies:
+        copy.wait()
+
+
 def final_kernel(flags_ref, key_ref, value_ref, *refs, groups):
-    parts, refs = refs[: 3 * groups], refs[3 * groups :]
-    own_ref, got_ref, query_out_ref, key_out_ref, value_out_ref = refs[:5]
-    key_buf, value_buf, states_ref, sems = refs[5:]
+    parts, refs = refs[: 2 * groups], refs[2 * groups :]
+    own_ref, got_ref, key_out_ref, value_out_ref = refs[:4]
+    key_buf, value_buf, states_ref, sems = refs[4:]
     size = CORES * COLUMNS // groups
     copies = []
 
@@ -399,9 +416,6 @@
         copies.append(pltpu.make_async_copy(source, target, sem))
         copies[-1].start()
 
-    for g in range(groups):
-        cols = slice(g * size * HEAD_DIM, (g + 1) * size * HEAD_DIM)
-        send(parts[3 * g], query_out_ref.at[:, cols], sems.at[2, g])
     gather_states(own_ref, got_ref, states_ref)
     leads = row_mask(flags_ref, LEADS)
     for k in range(CORES * COLUMNS):
@@ -409,10 +423,10 @@
         group, n = divmod(k, size)
         state = states_ref[k]
         from_values = dot(twice(value_ref[:, cols] * leads), beside(state), NT)
-        key_buf[:, cols] = (parts[3 * group + 1][:, head(n)] + from_values).astype(BF16)
+        key_buf[:, cols] = (parts[2 * group][:, head(n)] + from_values).astype(BF16)
         send(key_buf.at[:, cols], key_out_ref.at[:, cols], sems.at[0, k])
         from_keys = dot(twice(key_ref[:, cols] * leads), state, NN)
-        value_buf[:, cols] = (parts[3 * group + 2][:, head(n)] + from_keys).astype(BF16)
+        value_buf[:, cols] = (parts[2 * group + 1][:, head(n)] + from_keys).astype(BF16)
         send(value_buf.at[:, cols], value_out_ref.at[:, cols], sems.at[1, k])
     for copy in copies:
         copy.wait()
@@ -428,7 +442,6 @@
     devices = lax.axis_size("ctx")
     half_rows = COLUMNS * HEAD_DIM
 
-    scalars = pl.BlockSpec(memory_space=pltpu.SMEM)
     vmem = pl.BlockSpec(memory_space=pltpu.VMEM)
     hbm = pl.BlockSpec(memory_space=pltpu.HBM)
 
@@ -466,7 +479,9 @@
         return move(values, lambda i: i ^ 1)
 
     def along_row(values):
-        return [move(v, lambda i, f=f: i ^ (f * CORES)) for v, f in zip(values, FLIPS)]
+        return [
+            move(v, lambda i, f=f: i ^ (f * CORES) ^ (f % CORES)) for v, f in zip(values, FLIPS)
+        ]
 
     def beneath(after, moved, work):
         started = lax.optimization_barrier((after, *work[0]))
@@ -489,7 +504,7 @@
             row_kernel, "row_" + tag, (flags, keep, *gathered), [half, part], 2 * half.size, base=base
         )
         far = move(total, lambda i: (i + 2 * sign) % devices)
-        near = move(total, lambda i: (i + sign) % devices)
+        near = move(total, lambda i: (i + sign) % devices ^ 1)
         (near, far), done = beneath(parts, (near, far), works[1])
         results.append(done)
         keep, *sends = call(
@@ -512,28 +527,29 @@
             [pltpu.VMEM((half_rows, HEAD_DIM), F32)],
             base=base,
         )
-        return mine, swap(send), results
-
-    own, other, flags = call(
+        met, done = beneath(send, swap(send), works[3])
+        results.append(done)
+        return mine, met, results
+
+    own, other, flags, keys, values = call(
         state_kernel,
         "states",
         (doc_lengths, key_input, value_input),
-        [half, half, array(FLAGS, HEAD_DIM)],
+        [half, half, array(FLAGS, HEAD_DIM), wide_bf16, wide_bf16],
         8 * product,
-        [wide_buffer, wide_buffer, pltpu.SemaphoreType.DMA((2, GRAINS))],
-        [scalars, hbm, hbm],
-        limit=53,
+        [pltpu.SMEM((NDOCS,), I32), pltpu.SemaphoreType.DMA((3, GRAINS))],
+        [hbm, hbm, hbm],
+        limit=51,
     )
-    inputs = (queries, key_input, value_input)
+    inputs = (queries, keys, values)
 
     def mask_work(_):
         return call(
             mask_kernel,
             "pair_mask",
-            (doc_lengths,),
+            (flags,),
             [jax.ShapeDtypeStruct((BLOCK, BLOCK), BF16)],
             BLOCK * BLOCK,
-            ins=[scalars],
         )
 
     size = heads_here // MIX_GROUPS
@@ -553,7 +569,7 @@
         return (*inputs, *pair_masks), run
 
     nothing = ((), lambda args: [])
-    *entry, local = scan(flags, own, other, 0, [mix_work(0), mix_work(1), nothing])
+    *entry, local = scan(flags, own, other, 0, [mix_work(0), mix_work(1), nothing, nothing])
     local = [x for done in local for x in done]
     mixed, sums, entry_states = call(
         mixed_kernel,
@@ -576,44 +592,69 @@
     )
     groups = heads_here // BACK_GROUPS
 
-    def back_work(which, normed=False):
+    back_args = (flags, *inputs, *pair_masks, grad_mixed, entry_states)
+    query_parts, pieces = [], []
+
+    def back_work(which):
         def run(args):
-            out = []
             for g in which:
-                out += call(
+                query_part, *rest = call(
                     back_kernel,
                     "local_back",
-                    args[:7],
+                    args,
                     [array(rows_here, groups * HEAD_DIM, BF16)]
                     + [array(rows_here, groups * HEAD_DIM)] * 2,
                     17 * groups * product,
                     heads=range(g * groups, (g + 1) * groups),
                 )
-            if normed:
-                out += call(normed_kernel, "normed", args[7:], [wide_bf16], 2 * wide_f32.size)
-            return out
-
-        args = (flags, *inputs, *pair_masks, grad_mixed, entry_states)
-        return args + ((mixed, inverse, gain) if normed else ()), run
-
-    *leave, pieces = scan(
-        flags, own, other, DIRECTION, [back_work((0, 1)), back_work((2,)), back_work((3,), True)]
+                query_parts.append(query_part)
+                pieces.extend(rest)
+            return query_parts[-len(which) :], pieces[-2 * len(which) :]
+
+        return back_args, run
+
+    def first_work(args):
+        done = back_work((0,))[1](args[:-3])
+        return done, call(normed_kernel, "normed", args[-3:], [wide_bf16], 2 * wide_f32.size)
+
+    def store_work(_):
+        return call(
+            store_kernel,
+            "store",
+            query_parts,
+            [wide_bf16],
+            wide_f32.size,
+            [pltpu.SemaphoreType.DMA((BACK_GROUPS,))],
+            outs=[hbm],
+        )
+
+    *leave, results = scan(
+        flags,
+        own,
+        other,
+        DIRECTION,
+        [
+            (back_args + (mixed, inverse, gain), first_work),
+            back_work((1, 2)),
+            back_work((3,)),
+            ((), store_work),
+        ],
     )
-    normed_out = pieces[2].pop()
-    pieces = [x for done in pieces for x in done]
-    query_grad, key_grad, value_grad = call(
+    (first, (normed_out,)), second, third, (query_grad,) = results
+    pieces = [x for done in (first, second, third) for x in done[1]]
+    key_grad, value_grad = call(
         final_kernel,
         "back_states",
-        (flags, key_input, value_input, *pieces, *leave),
-        [wide_bf16] * 3,
+        (flags, keys, values, *pieces, *leave),
+        [wide_bf16] * 2,
         32 * product,
         [
             wide_buffer,
             wide_buffer,
             pltpu.VMEM((heads_here, 2 * HEAD_DIM, HEAD_DIM), BF16),
-            pltpu.SemaphoreType.DMA((3, heads_here)),
+            pltpu.SemaphoreType.DMA((2, heads_here)),
         ],
-        outs=[hbm] * 3,
+        outs=[hbm] * 2,
         groups=BACK_GROUPS,
     )
     return (normed_out, query_grad, key_grad, value_grad)

time: 74.9 us -> 71 us (0.948)
  starting transfers between devices: 37.3 us -> 29.5 us
  waiting for transfers between devices: 15.9 us -> 19.8 us
    ppermute x20, starting transfers between devices: 33.6 us -> 25.6 us  [move(): return lax.ppermute(values, 'ctx', [(source(i), i) for i in range(devices)])]
    ppermute x20, waiting for transfers between devices: 12.8 us -> 17.3 us  [move(): return lax.ppermute(values, 'ctx', [(source(i), i) for i in range(devices)])]
    pallas_call x20 -> x21, Pallas kernels: 19.8 us -> 19.7 us  [call(): pl.pallas_call(lambda *refs: body(*refs, **fixed), name=name, in_specs=in...]
  transfers between devices with their start and end apart: 23 -> 23, of which waited for: 16 -> 16; matrix products, arithmetic and copies ran while one was open for 0% -> 0% of each run, Pallas kernels for 16% -> 17%
where the time goes in v4:
time: 71 us; the launch traced here: 70.8 us
  starting transfers between devices  29.5 us (42%)
  waiting for transfers between devices  19.8 us (28%)
  Pallas kernels  19.7 us (28%)
  between operations  1.02 us (1%)
  local copies, waits for them, and re-layouts  0.75 us (1%)
    ppermute x20, starting transfers between devices, move(): return lax.ppermute(values, 'ctx', [(source(i), i) for i in range(devices)])  25.6 us
    pallas_call x21, Pallas kernels, call(): pl.pallas_call(lambda *refs: body(*refs, **fixed), name=name, in_specs=in...  19.7 us
    ppermute x20, waiting for transfers between devices, move(): return lax.ppermute(values, 'ctx', [(source(i), i) for i in range(devices)])  17.3 us
    ppermute x3, starting transfers between devices, on_device(): lax.ppermute(sums, 'head', [(i, i ^ flip) for i in range(lax.axis_size('h...  3.94 us
    ppermute x3, waiting for transfers between devices, on_device(): lax.ppermute(sums, 'head', [(i, i ^ flip) for i in range(lax.axis_size('h...  2.59 us
  transfers between devices with their start and end apart: 23, of which 16 were waited for; matrix products, arithmetic and copies ran while one was open for 0% of the time, Pallas kernels for 17%

profile of v4, /device:TPU:1, one launch (start us, length us, event | category | flops | bytes accessed | tf_op | source)
XLA Modules:
  0.0 70.8 jit_solution(2907619255909840719)
XLA Ops:
  1.4 2.3 %states.1 = (f32[512,128]{1,0:T(8,128)S(1)}, f32[512,128]{1,0:T(8,128)S(1)}, f32[40,128]{1,0:T(8,128)S(1)}, bf16[512,1024]{1,0:T(8,128)(2,1)S(1)}, bf16[512,1024]{1,0:T(8,128)(2,1)S(1)}) custom-call(s32[8]{0:T(128)S(1)} %copy-done.3, bf16[512,1024]{1,0:T(8,128)(2,1)} %refs_1_.2, bf16[512,1024]{1,0:T(8,128)(2,1)} %refs_2_.1), custom_call_target="tpu_custom_call" | custom-call | flops 134217728 | bytes 4739104 | tf_op jit(solution)/shard_map/states/pallas_call | solution.py:462
  3.7 1.5 %collective-permute-start = (f32[512,128]{1,0:T(8,128)S(1)}, f32[512,128]{1,0:T(8,128)S(1)}, u32[]{:S(2)}, u32[]{:S(2)}) collective-permute-start(f32[512,128]{1,0:T(8,128)S(1)} %get-tuple-element.117), channel_id=1, source_target_pairs={{1,0},{0,1},{3,2},{2,3},{5,4},{4,5},{7,6},{6,7},{9,8},{8,9},{11,10... | collective-permute-start | bytes 786440 | tf_op jit(solution)/shard_map/ppermute | solution.py:476
  6.4 3.1 %collective-permute-start.1 = (f32[128,128]{1,0:T(8,128)S(1)}, f32[128,128]{1,0:T(8,128)S(1)}, u32[]{:S(2)}, u32[]{:S(2)}) collective-permute-start(f32[128,128]{1,0:T(8,128)S(1)} %get-tuple-element.118), channel_id=1, source_target_pairs={{4,0},{5,1},{6,2},{7,3},{0,4},{1,5},{2,6},{3,7},{12,8},{13,9},{14,... | collective-permute-start | bytes 196616 | tf_op jit(solution)/shard_map/ppermute | solution.py:476
  10.8 1.5 %local_mix.2.refs_2_ = f32[512,512]{1,0:T(8,128)S(1)} custom-call(bf16[512,1024]{1,0:T(8,128)(2,1)S(1)} %copy-done, bf16[512,1024]{1,0:T(8,128)(2,1)S(1)} %get-tuple-element.201.refs_1_.refs_2_, bf16[512,1024]{1,0:T(8,128)(2,1)S(1)} %get-tuple-element.202.refs_2_.refs_3_, bf16[512,512]{1,0:T(8,128)(2,1)S(1)} %pair_mask.1.refs_3_.refs_4_), custom_call_target="tpu_custom_call" | custom-call | flops 402653184 | bytes 4718592 | tf_op jit(solution)/shard_map/local_mix/pallas_call | solution.py:462
  12.3 1.8 %collective-permute-done.2.refs_3_ = f32[128,128]{1,0:T(8,128)S(1)} collective-permute-done((f32[128,128]{1,0:T(8,128)S(1)}, f32[128,128]{1,0:T(8,128)S(1)}, u32[]{:S(2)}, u32[]{:S(2)}) %collective-permute-start.2) | collective-permute-done | bytes 65568 | tf_op jit(solution)/shard_map/ppermute | solution.py:476
  15.3 3.7 %collective-permute-start.5 = (f32[128,128]{1,0:T(8,128)S(1)}, f32[128,128]{1,0:T(8,128)S(1)}, u32[]{:S(2)}, u32[]{:S(2)}) collective-permute-start(f32[128,128]{1,0:T(8,128)S(1)} %get-tuple-element.132), channel_id=1, source_target_pairs={{16,0},{17,1},{18,2},{19,3},{20,4},{21,5},{22,6},{23,7},{24,8},{25... | collective-permute-start | bytes 196616 | tf_op jit(solution)/shard_map/ppermute | solution.py:476
  19.8 1.5 %local_mix.3.refs_3_ = f32[512,512]{1,0:T(8,128)S(1)} custom-call(bf16[512,1024]{1,0:T(8,128)(2,1)S(1)} %copy-done, bf16[512,1024]{1,0:T(8,128)(2,1)S(1)} %get-tuple-element.201.refs_1_.refs_2_, bf16[512,1024]{1,0:T(8,128)(2,1)S(1)} %get-tuple-element.202.refs_2_.refs_3_, bf16[512,512]{1,0:T(8,128)(2,1)S(1)} %pair_mask.1.refs_3_.refs_4_), custom_call_target="tpu_custom_call" | custom-call | flops 402653184 | bytes 4718592 | tf_op jit(solution)/shard_map/local_mix/pallas_call | solution.py:462
  21.6 2.4 %collective-permute-done.4.refs_2_ = f32[128,128]{1,0:T(8,128)S(1)} collective-permute-done((f32[128,128]{1,0:T(8,128)S(1)}, f32[128,128]{1,0:T(8,128)S(1)}, u32[]{:S(2)}, u32[]{:S(2)}) %collective-permute-start.4) | collective-permute-done | bytes 65568 | tf_op jit(solution)/shard_map/ppermute | solution.py:476
  24.1 1.8 %collective-permute-start.6 = (f32[128,128]{1,0:T(8,128)S(1)}, f32[128,128]{1,0:T(8,128)S(1)}, u32[]{:S(2)}, u32[]{:S(2)}) collective-permute-start(f32[128,128]{1,0:T(8,128)S(1)} %get-tuple-element.142), channel_id=1, source_target_pairs={{4,0},{5,1},{6,2},{7,3},{0,4},{1,5},{2,6},{3,7},{12,8},{13,9},{14,... | collective-permute-start | bytes 196616 | tf_op jit(solution)/shard_map/ppermute | solution.py:476
  27.7 1.5 %collective-permute-done.6.refs_4_ = f32[128,128]{1,0:T(8,128)S(1)} collective-permute-done((f32[128,128]{1,0:T(8,128)S(1)}, f32[128,128]{1,0:T(8,128)S(1)}, u32[]{:S(2)}, u32[]{:S(2)}) %collective-permute-start.6) | collective-permute-done | bytes 65568 | tf_op jit(solution)/shard_map/ppermute | solution.py:476
  29.2 1.7 %collective-permute-done.7.refs_5_ = f32[128,128]{1,0:T(8,128)S(1)} collective-permute-done((f32[128,128]{1,0:T(8,128)S(1)}, f32[128,128]{1,0:T(8,128)S(1)}, u32[]{:S(2)}, u32[]{:S(2)}) %collective-permute-start.7) | collective-permute-done | bytes 65568 | tf_op jit(solution)/shard_map/ppermute | solution.py:476
  32.3 1.5 %collective-permute-done.9.refs_5_ = f32[512,128]{1,0:T(8,128)S(1)} collective-permute-done((f32[512,128]{1,0:T(8,128)S(1)}, f32[512,128]{1,0:T(8,128)S(1)}, u32[]{:S(2)}, u32[]{:S(2)}) %collective-permute-start.9) | collective-permute-done | bytes 262176 | tf_op jit(solution)/shard_map/ppermute | solution.py:476
  35.0 2.6 %collective-permute-start.12 = (f32[2,512]{1,0:T(2,128)S(1)}, f32[2,512]{1,0:T(2,128)S(1)}, u32[]{:S(2)}, u32[]{:S(2)}) collective-permute-start(f32[2,512]{1,0:T(2,128)S(1)} %get-tuple-element.150.refs_1_), channel_id=1, source_target_pairs={{0,96},{32,64},{64,32},{96,0},{1,97},{33,65},{65,33},{97,1},{2,98}... | collective-permute-start | bytes 12296 | tf_op jit(solution)/shard_map/ppermute | solution.py:583
  37.6 1.4 %collective-permute-start.10 = (f32[2,512]{1,0:T(2,128)S(1)}, f32[2,512]{1,0:T(2,128)S(1)}, u32[]{:S(2)}, u32[]{:S(2)}) collective-permute-start(f32[2,512]{1,0:T(2,128)S(1)} %get-tuple-element.150.refs_1_), channel_id=1, source_target_pairs={{0,64},{32,96},{64,0},{96,32},{1,65},{33,97},{65,1},{97,33},{2,66}... | collective-permute-start | bytes 12296 | tf_op jit(solution)/shard_map/ppermute | solution.py:583
  40.0 1.5 %collective-permute-done.10.refs_2_ = f32[2,512]{1,0:T(2,128)S(1)} collective-permute-done((f32[2,512]{1,0:T(2,128)S(1)}, f32[2,512]{1,0:T(2,128)S(1)}, u32[]{:S(2)}, u32[]{:S(2)}) %collective-permute-start.10) | collective-permute-done | bytes 4128 | tf_op jit(solution)/shard_map/ppermute | solution.py:583
  41.5 1.5 %norm_grad.1 = (bf16[512,1024]{1,0:T(8,128)(2,1)S(1)}, f32[512,128]{1,0:T(8,128)S(1)}, f32[512,128]{1,0:T(8,128)S(1)}, f32[512,128]{1,0:T(8,128)S(1)}) custom-call(f32[40,128]{1,0:T(8,128)S(1)} %get-tuple-element.199.refs_0_, f32[2,512]{1,0:T(2,128)S(1)} %get-tuple-element.150.refs_1_, f32[2,512]{1,0:T(2,128)S(1)} %collective-permute-done.10.refs_2_, ...), custom_call_target="tpu_custom_call" | custom-call | flops 134217728 | bytes 6070272 | tf_op jit(solution)/shard_map/norm_grad/pallas_call | solution.py:462
  43.0 1.9 %collective-permute-start.13 = (f32[512,128]{1,0:T(8,128)S(1)}, f32[512,128]{1,0:T(8,128)S(1)}, u32[]{:S(2)}, u32[]{:S(2)}) collective-permute-start(f32[512,128]{1,0:T(8,128)S(1)} %get-tuple-element.153), channel_id=1, source_target_pairs={{1,0},{0,1},{3,2},{2,3},{5,4},{4,5},{7,6},{6,7},{9,8},{8,9},{11,10... | collective-permute-start | bytes 786440 | tf_op jit(solution)/shard_map/ppermute | solution.py:476
  51.0 1.7 %local_back.4 = (bf16[512,256]{1,0:T(8,128)(2,1)S(1)}, f32[512,256]{1,0:T(8,128)S(1)}, f32[512,256]{1,0:T(8,128)S(1)}) custom-call(f32[40,128]{1,0:T(8,128)S(1)} %get-tuple-element.199.refs_0_, bf16[512,1024]{1,0:T(8,128)(2,1)S(1)} %copy-done, bf16[512,1024]{1,0:T(8,128)(2,1)S(1)} %get-tuple-element.201.refs_1_.refs_2_, ...), custom_call_target="tpu_custom_call" | custom-call | flops 570425344 | bytes 6574080 | tf_op jit(solution)/shard_map/local_back/pallas_call | solution.py:462
  54.3 1.5 %collective-permute-start.17 = (f32[128,128]{1,0:T(8,128)S(1)}, f32[128,128]{1,0:T(8,128)S(1)}, u32[]{:S(2)}, u32[]{:S(2)}) collective-permute-start(f32[128,128]{1,0:T(8,128)S(1)} %get-tuple-element.179), channel_id=1, source_target_pairs={{9,0},{8,1},{11,2},{10,3},{13,4},{12,5},{15,6},{14,7},{17,8},{16,9... | collective-permute-start | bytes 196616 | tf_op jit(solution)/shard_map/ppermute | solution.py:476
  55.8 1.8 %local_back.6 = (bf16[512,256]{1,0:T(8,128)(2,1)S(1)}, f32[512,256]{1,0:T(8,128)S(1)}, f32[512,256]{1,0:T(8,128)S(1)}) custom-call(f32[40,128]{1,0:T(8,128)S(1)} %get-tuple-element.199.refs_0_, bf16[512,1024]{1,0:T(8,128)(2,1)S(1)} %copy-done, bf16[512,1024]{1,0:T(8,128)(2,1)S(1)} %get-tuple-element.201.refs_1_.refs_2_, ...), custom_call_target="tpu_custom_call" | custom-call | flops 570425344 | bytes 6574080 | tf_op jit(solution)/shard_map/local_back/pallas_call | solution.py:462
  57.5 1.7 %local_back.5 = (bf16[512,256]{1,0:T(8,128)(2,1)S(1)}, f32[512,256]{1,0:T(8,128)S(1)}, f32[512,256]{1,0:T(8,128)S(1)}) custom-call(f32[40,128]{1,0:T(8,128)S(1)} %get-tuple-element.199.refs_0_, bf16[512,1024]{1,0:T(8,128)(2,1)S(1)} %copy-done, bf16[512,1024]{1,0:T(8,128)(2,1)S(1)} %get-tuple-element.201.refs_1_.refs_2_, ...), custom_call_target="tpu_custom_call" | custom-call | flops 570425344 | bytes 6574080 | tf_op jit(solution)/shard_map/local_back/pallas_call | solution.py:462
  60.2 1.7 %collective-permute-start.20 = (f32[128,128]{1,0:T(8,128)S(1)}, f32[128,128]{1,0:T(8,128)S(1)}, u32[]{:S(2)}, u32[]{:S(2)}) collective-permute-start(f32[128,128]{1,0:T(8,128)S(1)} %get-tuple-element.197), channel_id=1, source_target_pairs={{3,0},{2,1},{1,2},{0,3},{7,4},{6,5},{5,6},{4,7},{11,8},{10,9},{9,1... | collective-permute-start | bytes 196616 | tf_op jit(solution)/shard_map/ppermute | solution.py:476
  63.0 1.7 %local_back.7 = (bf16[512,256]{1,0:T(8,128)(2,1)S(1)}, f32[512,256]{1,0:T(8,128)S(1)}, f32[512,256]{1,0:T(8,128)S(1)}) custom-call(f32[40,128]{1,0:T(8,128)S(1)} %get-tuple-element.199.refs_0_, bf16[512,1024]{1,0:T(8,128)(2,1)S(1)} %copy-done, bf16[512,1024]{1,0:T(8,128)(2,1)S(1)} %get-tuple-element.201.refs_1_.refs_2_, ...), custom_call_target="tpu_custom_call" | custom-call | flops 570425344 | bytes 6574080 | tf_op jit(solution)/shard_map/local_back/pallas_call | solution.py:462
  68.5 2.2 %back_states.1 = (bf16[512,1024]{1,0:T(8,128)(2,1)}, bf16[512,1024]{1,0:T(8,128)(2,1)}) custom-call(f32[40,128]{1,0:T(8,128)S(1)} %get-tuple-element.199.refs_0_, bf16[512,1024]{1,0:T(8,128)(2,1)S(1)} %get-tuple-element.201.refs_1_.refs_2_, bf16[512,1024]{1,0:T(8,128)(2,1)S(1)} %get-tuple-element.202.refs_2_.refs_3_, ...), custom_call_target="tpu_custom_call" | custom-call | flops 536870912 | bytes 8933376 | tf_op jit(solution)/shard_map/back_states/pallas_call | solution.py:462
  (51 shorter events, 24.5 us)
Async XLA Ops:
  3.7 2.7 %collective-permute-start = (f32[512,128]{1,0:T(8,128)S(1)}, f32[512,128]{1,0:T(8,128)S(1)}, u32[]{:S(2)}, u32[]{:S(2)}) collective-permute-start(f32[512,128]{1,0:T(8,128)S(1)} %get-tuple-element.117), channel_id=1, source_target_pairs={{1,0},{0,1},{3,2},{2,3},{5,4},{4,5},{7,6},{6,7},{9,8},{8,9},{11,10... | collective-permute-start | bytes 786440 | tf_op jit(solution)/shard_map/ppermute | solution.py:476
  6.4 5.9 %collective-permute-start.1 = (f32[128,128]{1,0:T(8,128)S(1)}, f32[128,128]{1,0:T(8,128)S(1)}, u32[]{:S(2)}, u32[]{:S(2)}) collective-permute-start(f32[128,128]{1,0:T(8,128)S(1)} %get-tuple-element.118), channel_id=1, source_target_pairs={{4,0},{5,1},{6,2},{7,3},{0,4},{1,5},{2,6},{3,7},{12,8},{13,9},{14,... | collective-permute-start | bytes 196616 | tf_op jit(solution)/shard_map/ppermute | solution.py:476
  9.4 4.7 %collective-permute-start.2 = (f32[128,128]{1,0:T(8,128)S(1)}, f32[128,128]{1,0:T(8,128)S(1)}, u32[]{:S(2)}, u32[]{:S(2)}) collective-permute-start(f32[128,128]{1,0:T(8,128)S(1)} %get-tuple-element.119), channel_id=1, source_target_pairs={{3,0},{2,1},{1,2},{0,3},{7,4},{6,5},{5,6},{4,7},{11,8},{10,9},{9,1... | collective-permute-start | bytes 196616 | tf_op jit(solution)/shard_map/ppermute | solution.py:476
  10.4 4.9 %collective-permute-start.3 = (f32[128,128]{1,0:T(8,128)S(1)}, f32[128,128]{1,0:T(8,128)S(1)}, u32[]{:S(2)}, u32[]{:S(2)}) collective-permute-start(f32[128,128]{1,0:T(8,128)S(1)} %get-tuple-element.120), channel_id=1, source_target_pairs={{7,0},{6,1},{5,2},{4,3},{3,4},{2,5},{1,6},{0,7},{15,8},{14,9},{13,... | collective-permute-start | bytes 196616 | tf_op jit(solution)/shard_map/ppermute | solution.py:476
  15.3 6.3 %collective-permute-start.5 = (f32[128,128]{1,0:T(8,128)S(1)}, f32[128,128]{1,0:T(8,128)S(1)}, u32[]{:S(2)}, u32[]{:S(2)}) collective-permute-start(f32[128,128]{1,0:T(8,128)S(1)} %get-tuple-element.132), channel_id=1, source_target_pairs={{16,0},{17,1},{18,2},{19,3},{20,4},{21,5},{22,6},{23,7},{24,8},{25... | collective-permute-start | bytes 196616 | tf_op jit(solution)/shard_map/ppermute | solution.py:476
  19.0 5.1 %collective-permute-start.4 = (f32[128,128]{1,0:T(8,128)S(1)}, f32[128,128]{1,0:T(8,128)S(1)}, u32[]{:S(2)}, u32[]{:S(2)}) collective-permute-start(f32[128,128]{1,0:T(8,128)S(1)} %get-tuple-element.132), channel_id=1, source_target_pairs={{25,0},{24,1},{27,2},{26,3},{29,4},{28,5},{31,6},{30,7},{1,8},{0,9... | collective-permute-start | bytes 196616 | tf_op jit(solution)/shard_map/ppermute | solution.py:476
  19.8 14.1 %copy-start.2 = (f32[1024]{0:T(1024)S(1)}, f32[1024]{0:T(1024)}, u32[]{:S(2)}) copy-start(f32[1024]{0:T(1024)} %param.9) | copy-start | bytes 12292
  24.1 5.1 %collective-permute-start.6 = (f32[128,128]{1,0:T(8,128)S(1)}, f32[128,128]{1,0:T(8,128)S(1)}, u32[]{:S(2)}, u32[]{:S(2)}) collective-permute-start(f32[128,128]{1,0:T(8,128)S(1)} %get-tuple-element.142), channel_id=1, source_target_pairs={{4,0},{5,1},{6,2},{7,3},{0,4},{1,5},{2,6},{3,7},{12,8},{13,9},{14,... | collective-permute-start | bytes 196616 | tf_op jit(solution)/shard_map/ppermute | solution.py:476
  25.9 5.0 %collective-permute-start.7 = (f32[128,128]{1,0:T(8,128)S(1)}, f32[128,128]{1,0:T(8,128)S(1)}, u32[]{:S(2)}, u32[]{:S(2)}) collective-permute-start(f32[128,128]{1,0:T(8,128)S(1)} %get-tuple-element.143), channel_id=1, source_target_pairs={{3,0},{2,1},{1,2},{0,3},{7,4},{6,5},{5,6},{4,7},{11,8},{10,9},{9,1... | collective-permute-start | bytes 196616 | tf_op jit(solution)/shard_map/ppermute | solution.py:476
  27.3 4.9 %collective-permute-start.8 = (f32[128,128]{1,0:T(8,128)S(1)}, f32[128,128]{1,0:T(8,128)S(1)}, u32[]{:S(2)}, u32[]{:S(2)}) collective-permute-start(f32[128,128]{1,0:T(8,128)S(1)} %get-tuple-element.144), channel_id=1, source_target_pairs={{7,0},{6,1},{5,2},{4,3},{3,4},{2,5},{1,6},{0,7},{15,8},{14,9},{13,... | collective-permute-start | bytes 196616 | tf_op jit(solution)/shard_map/ppermute | solution.py:476
  32.2 1.6 %collective-permute-start.9 = (f32[512,128]{1,0:T(8,128)S(1)}, f32[512,128]{1,0:T(8,128)S(1)}, u32[]{:S(2)}, u32[]{:S(2)}) collective-permute-start(f32[512,128]{1,0:T(8,128)S(1)} %get-tuple-element.149), channel_id=1, source_target_pairs={{1,0},{0,1},{3,2},{2,3},{5,4},{4,5},{7,6},{6,7},{9,8},{8,9},{11,10... | collective-permute-start | bytes 786440 | tf_op jit(solution)/shard_map/ppermute | solution.py:476
  35.0 3.9 %collective-permute-start.12 = (f32[2,512]{1,0:T(2,128)S(1)}, f32[2,512]{1,0:T(2,128)S(1)}, u32[]{:S(2)}, u32[]{:S(2)}) collective-permute-start(f32[2,512]{1,0:T(2,128)S(1)} %get-tuple-element.150.refs_1_), channel_id=1, source_target_pairs={{0,96},{32,64},{64,32},{96,0},{1,97},{33,65},{65,33},{97,1},{2,98}... | collective-permute-start | bytes 12296 | tf_op jit(solution)/shard_map/ppermute | solution.py:583
  37.6 2.5 %collective-permute-start.11 = (f32[2,512]{1,0:T(2,128)S(1)}, f32[2,512]{1,0:T(2,128)S(1)}, u32[]{:S(2)}, u32[]{:S(2)}) collective-permute-start(f32[2,512]{1,0:T(2,128)S(1)} %get-tuple-element.150.refs_1_), channel_id=1, source_target_pairs={{0,32},{32,0},{64,96},{96,64},{1,33},{33,1},{65,97},{97,65},{2,34}... | collective-permute-start | bytes 12296 | tf_op jit(solution)/shard_map/ppermute | solution.py:583
  37.6 4.0 %collective-permute-start.10 = (f32[2,512]{1,0:T(2,128)S(1)}, f32[2,512]{1,0:T(2,128)S(1)}, u32[]{:S(2)}, u32[]{:S(2)}) collective-permute-start(f32[2,512]{1,0:T(2,128)S(1)} %get-tuple-element.150.refs_1_), channel_id=1, source_target_pairs={{0,64},{32,96},{64,0},{96,32},{1,65},{33,97},{65,1},{97,33},{2,66}... | collective-permute-start | bytes 12296 | tf_op jit(solution)/shard_map/ppermute | solution.py:583
  43.0 3.0 %collective-permute-start.13 = (f32[512,128]{1,0:T(8,128)S(1)}, f32[512,128]{1,0:T(8,128)S(1)}, u32[]{:S(2)}, u32[]{:S(2)}) collective-permute-start(f32[512,128]{1,0:T(8,128)S(1)} %get-tuple-element.153), channel_id=1, source_target_pairs={{1,0},{0,1},{3,2},{2,3},{5,4},{4,5},{7,6},{6,7},{9,8},{8,9},{11,10... | collective-permute-start | bytes 786440 | tf_op jit(solution)/shard_map/ppermute | solution.py:476
  46.1 6.7 %collective-permute-start.14 = (f32[128,128]{1,0:T(8,128)S(1)}, f32[128,128]{1,0:T(8,128)S(1)}, u32[]{:S(2)}, u32[]{:S(2)}) collective-permute-start(f32[128,128]{1,0:T(8,128)S(1)} %get-tuple-element.154), channel_id=1, source_target_pairs={{4,0},{5,1},{6,2},{7,3},{0,4},{1,5},{2,6},{3,7},{12,8},{13,9},{14,... | collective-permute-start | bytes 196616 | tf_op jit(solution)/shard_map/ppermute | solution.py:476
  47.2 5.6 %collective-permute-start.15 = (f32[128,128]{1,0:T(8,128)S(1)}, f32[128,128]{1,0:T(8,128)S(1)}, u32[]{:S(2)}, u32[]{:S(2)}) collective-permute-start(f32[128,128]{1,0:T(8,128)S(1)} %get-tuple-element.155), channel_id=1, source_target_pairs={{3,0},{2,1},{1,2},{0,3},{7,4},{6,5},{5,6},{4,7},{11,8},{10,9},{9,1... | collective-permute-start | bytes 196616 | tf_op jit(solution)/shard_map/ppermute | solution.py:476
  48.3 5.1 %collective-permute-start.16 = (f32[128,128]{1,0:T(8,128)S(1)}, f32[128,128]{1,0:T(8,128)S(1)}, u32[]{:S(2)}, u32[]{:S(2)}) collective-permute-start(f32[128,128]{1,0:T(8,128)S(1)} %get-tuple-element.156), channel_id=1, source_target_pairs={{7,0},{6,1},{5,2},{4,3},{3,4},{2,5},{1,6},{0,7},{15,8},{14,9},{13,... | collective-permute-start | bytes 196616 | tf_op jit(solution)/shard_map/ppermute | solution.py:476
  53.5 5.8 %collective-permute-start.18 = (f32[128,128]{1,0:T(8,128)S(1)}, f32[128,128]{1,0:T(8,128)S(1)}, u32[]{:S(2)}, u32[]{:S(2)}) collective-permute-start(f32[128,128]{1,0:T(8,128)S(1)} %get-tuple-element.179), channel_id=1, source_target_pairs={{16,0},{17,1},{18,2},{19,3},{20,4},{21,5},{22,6},{23,7},{24,8},{25... | collective-permute-start | bytes 196616 | tf_op jit(solution)/shard_map/ppermute | solution.py:476
  54.3 5.0 %collective-permute-start.17 = (f32[128,128]{1,0:T(8,128)S(1)}, f32[128,128]{1,0:T(8,128)S(1)}, u32[]{:S(2)}, u32[]{:S(2)}) collective-permute-start(f32[128,128]{1,0:T(8,128)S(1)} %get-tuple-element.179), channel_id=1, source_target_pairs={{9,0},{8,1},{11,2},{10,3},{13,4},{12,5},{15,6},{14,7},{17,8},{16,9... | collective-permute-start | bytes 196616 | tf_op jit(solution)/shard_map/ppermute | solution.py:476
  59.4 5.4 %collective-permute-start.19 = (f32[128,128]{1,0:T(8,128)S(1)}, f32[128,128]{1,0:T(8,128)S(1)}, u32[]{:S(2)}, u32[]{:S(2)}) collective-permute-start(f32[128,128]{1,0:T(8,128)S(1)} %get-tuple-element.196), channel_id=1, source_target_pairs={{4,0},{5,1},{6,2},{7,3},{0,4},{1,5},{2,6},{3,7},{12,8},{13,9},{14,... | collective-permute-start | bytes 196616 | tf_op jit(solution)/shard_map/ppermute | solution.py:476
  60.2 5.3 %collective-permute-start.20 = (f32[128,128]{1,0:T(8,128)S(1)}, f32[128,128]{1,0:T(8,128)S(1)}, u32[]{:S(2)}, u32[]{:S(2)}) collective-permute-start(f32[128,128]{1,0:T(8,128)S(1)} %get-tuple-element.197), channel_id=1, source_target_pairs={{3,0},{2,1},{1,2},{0,3},{7,4},{6,5},{5,6},{4,7},{11,8},{10,9},{9,1... | collective-permute-start | bytes 196616 | tf_op jit(solution)/shard_map/ppermute | solution.py:476
  61.9 4.9 %collective-permute-start.21 = (f32[128,128]{1,0:T(8,128)S(1)}, f32[128,128]{1,0:T(8,128)S(1)}, u32[]{:S(2)}, u32[]{:S(2)}) collective-permute-start(f32[128,128]{1,0:T(8,128)S(1)} %get-tuple-element.198), channel_id=1, source_target_pairs={{7,0},{6,1},{5,2},{4,3},{3,4},{2,5},{1,6},{0,7},{15,8},{14,9},{13,... | collective-permute-start | bytes 196616 | tf_op jit(solution)/shard_map/ppermute | solution.py:476
  66.9 1.6 %collective-permute-start.22 = (f32[512,128]{1,0:T(8,128)S(1)}, f32[512,128]{1,0:T(8,128)S(1)}, u32[]{:S(2)}, u32[]{:S(2)}) collective-permute-start(f32[512,128]{1,0:T(8,128)S(1)} %get-tuple-element.212), channel_id=1, source_target_pairs={{1,0},{0,1},{3,2},{2,3},{5,4},{4,5},{7,6},{6,7},{9,8},{8,9},{11,10... | collective-permute-start | bytes 786440 | tf_op jit(solution)/shard_map/ppermute | solution.py:476
  (3 other events, 25.0 us)

commit v5 on v4

v5 whole, which is shorter than its diff:
```python
import jax
import jax.numpy as jnp
from jax import lax
from jax.experimental import pallas as pl
from jax.experimental.pallas import tpu as pltpu
from jax.sharding import PartitionSpec as P

HEADS = 32
HEAD_DIM = 128
BLOCK = 512
GRAIN = 128
NDOCS = 8
GRAINS = BLOCK // GRAIN
WIDTH = HEADS * HEAD_DIM
HALF = BLOCK // 2
EPSILON = 1e-06

CORES = 2
COLUMNS = 4
ROWS = 4
FLIPS = (2, 1, 3)

F32 = jnp.float32
BF16 = jnp.bfloat16
I32 = jnp.int32

NN = ((1,), (0,))
NT = ((1,), (1,))
TN = ((0,), (0,))


def dot(a, b, dims):
    return lax.dot_general(a, b, (dims, ((), ())), preferred_element_type=F32)


def place():
    index = lax.axis_index("ctx")
    return index // (CORES * COLUMNS), (index // CORES) % COLUMNS, index % CORES


def half_kept():
    row, column, core = place()
    return (row + column + core) % CORES


def doc_starts(lengths_ref):
    starts = [I32(0)]
    for i in range(NDOCS - 1):
        starts.append(starts[-1] + lengths_ref[i])
    return starts


def grain_docs(lengths_ref):
    total = lax.axis_size("ctx") * GRAINS
    first = lax.axis_index("ctx") * GRAINS
    starts = doc_starts(lengths_ref)
    docs = []
    for k in range(-1, GRAINS + 1):
        grain = first + k
        count = (grain >= total).astype(I32) - 1
        for s in starts:
            count = count + (s <= grain).astype(I32)
        docs.append(count)
    return docs


def unbroken(lengths_ref, first, grains, backward):
    hits = I32(0)
    for s in doc_starts(lengths_ref)[1:]:
        at = s - 1 if backward else s
        hits = hits + ((at >= first) & (at < first + grains)).astype(I32)
    return (hits == 0).astype(F32)


FROM_OWN, FROM_GOT, KEEPS, NEAR, FAR, KEEP_BLOCK = 0, 1, 2, 6, 7, 8
DIRECTION = 9
FOLLOWS = 2 * DIRECTION
FIRST = FOLLOWS + GRAINS
LEADS = FIRST + GRAINS
SAME = LEADS + GRAINS
TAIL = SAME + GRAINS * (GRAINS - 1) // 2
FLAGS = 40


def write_flags(lengths_ref, flags_ref):
    index = lax.axis_index("ctx")
    row, _, core = place()
    block_of = index - core
    width = CORES * GRAINS
    span = COLUMNS * width

    def put(at, value):
        flags_ref[at : at + 1, :] = jnp.full((1, HEAD_DIM), value, F32)

    for backward in (False, True):
        base = DIRECTION if backward else 0
        earlier = block_of + (1 if backward else 0)
        later = block_of + (0 if backward else 1)
        keep = unbroken(lengths_ref, later * GRAINS, GRAINS, backward)
        is_later = index == later
        put(base + FROM_OWN, jnp.where(is_later, 1.0, keep))
        put(base + FROM_GOT, jnp.where(is_later, keep, 1.0))
        for q in range(COLUMNS):
            first = row * span + q * width
            put(base + KEEPS + q, unbroken(lengths_ref, first, width, backward))
        behind = (ROWS - 1 - row) if backward else row
        near_row = row + 1 if backward else row - 1
        near_keep = unbroken(lengths_ref, near_row * span, span, backward)
        put(base + NEAR, (behind >= 1).astype(F32))
        put(base + FAR, (behind >= 2).astype(F32) * near_keep)
        put(base + KEEP_BLOCK, unbroken(lengths_ref, earlier * GRAINS, GRAINS, backward))
    docs = grain_docs(lengths_ref)
    for base, doc in ((FOLLOWS, docs[0]), (FIRST, docs[1]), (LEADS, docs[GRAINS + 1]), (TAIL, docs[GRAINS])):
        for g in range(GRAINS):
            put(base + g, (docs[1 + g] == doc).astype(F32))
    for i in range(GRAINS):
        for j in range(i):
            put(SAME + i * (i - 1) // 2 + j, (docs[1 + i] == docs[1 + j]).astype(F32))


def flag(flags_ref, at):
    return flags_ref[at : at + 1, :]


def row_mask(flags_ref, base):
    parts = [
        jnp.broadcast_to(flag(flags_ref, base + g), (GRAIN, HEAD_DIM)) for g in range(GRAINS)
    ]
    return jnp.concatenate(parts, axis=0).astype(BF16)


def pair_mask(flags_ref):
    rows = lax.broadcasted_iota(I32, (GRAIN, GRAIN), 0)
    cols = lax.broadcasted_iota(I32, (GRAIN, GRAIN), 1)
    lower = jnp.where(rows >= cols, 1.0, 0.0).astype(F32)
    out = []
    for i in range(GRAINS):
        line = []
        for j in range(GRAINS):
            if j < i:
                same = flag(flags_ref, SAME + i * (i - 1) // 2 + j)
                line.append(jnp.broadcast_to(same, (GRAIN, GRAIN)))
            elif j == i:
                line.append(lower)
            else:
                line.append(jnp.zeros((GRAIN, GRAIN), F32))
        out.append(jnp.concatenate(line, axis=1))
    return jnp.concatenate(out, axis=0).astype(BF16)


def split(x):
    high = x.astype(BF16)
    low = (x - high.astype(F32)).astype(BF16)
    return jnp.concatenate([high, low], axis=0)


def twice(x):
    return jnp.concatenate([x, x], axis=1)


def head(k):
    return slice(k * HEAD_DIM, (k + 1) * HEAD_DIM)


def side_of(own):
    mine = half_kept()
    return mine if own else 1 - mine


def column(k, own, heads=1):
    start = (side_of(own) * COLUMNS + k) * HEAD_DIM
    return pl.ds(pl.multiple_of(start, heads * HEAD_DIM), heads * HEAD_DIM)


def rows_of(k):
    return slice(k * HEAD_DIM, (k + 1) * HEAD_DIM)


def piece(index):
    return pl.ds(pl.multiple_of(index * HEAD_DIM, HEAD_DIM), HEAD_DIM)


def state_kernel(
    given_ref, key_ref, value_ref, other_ref, flags_ref, key_buf, value_buf, lengths_ref, sems
):
    read = pltpu.make_async_copy(given_ref, lengths_ref, sems.at[2, 0])
    read.start()
    loads = []
    for g in range(GRAINS):
        rows = slice(g * GRAIN, (g + 1) * GRAIN)
        pair = []
        for m, (source, to) in enumerate(((key_ref, key_buf), (value_ref, value_buf))):
            copy = pltpu.make_async_copy(source.at[rows], to.at[rows], sems.at[m, g])
            copy.start()
            pair.append(copy)
        loads.append(pair)
    read.wait()
    write_flags(lengths_ref, flags_ref)
    docs = grain_docs(lengths_ref)
    for g in range(GRAINS):
        for copy in loads[g]:
            copy.wait()
        rows = slice(g * GRAIN, (g + 1) * GRAIN)
        same = (docs[1 + g] == docs[GRAINS]).astype(F32)
        mask = jnp.full((GRAIN, HEAD_DIM), same, F32).astype(BF16)
        for k in range(COLUMNS):
            cols = column(k, False)
            state = dot(key_buf[rows, cols] * mask, value_buf[rows, cols], TN)
            if g == 0:
                other_ref[rows_of(k), :] = state
            else:
                other_ref[rows_of(k), :] += state


def own_state_kernel(flags_ref, key_ref, value_ref, own_ref):
    mask = row_mask(flags_ref, TAIL)
    for k in range(COLUMNS):
        cols = column(k, True)
        own_ref[rows_of(k), :] = dot(key_ref[:, cols] * mask, value_ref[:, cols], TN)


def pair_kernel(flags_ref, own_ref, got_ref, keep_ref, *send_refs, base):
    _, at, _ = place()
    from_own = flag(flags_ref, base + FROM_OWN)
    from_got = flag(flags_ref, base + FROM_GOT)
    for flip, out_ref in zip((0,) + FLIPS, (keep_ref,) + send_refs):
        rows = piece(at ^ flip)
        out_ref[...] = from_own * own_ref[rows, :] + from_got * got_ref[rows, :]


def chip_order(base):
    return list(range(COLUMNS))[:: -1 if base else 1]


def row_kernel(flags_ref, keep_ref, *refs, base):
    got_refs, (parts_ref, total_ref) = refs[: len(FLIPS)], refs[len(FLIPS) :]
    _, at, _ = place()
    for flip, in_ref in zip((0,) + FLIPS, (keep_ref,) + got_refs):
        parts_ref[piece(at ^ flip), :] = in_ref[...]
    order = chip_order(base)
    running = parts_ref[rows_of(order[0]), :]
    for q in order[1:]:
        running = parts_ref[rows_of(q), :] + flag(flags_ref, base + KEEPS + q) * running
    total_ref[...] = running


def enter_kernel(flags_ref, parts_ref, near_ref, far_ref, keep_ref, *refs, base):
    send_refs, (entries_ref,) = refs[: len(FLIPS)], refs[len(FLIPS) :]
    _, at, _ = place()
    running = flag(flags_ref, base + NEAR) * near_ref[...]
    running = running + flag(flags_ref, base + FAR) * far_ref[...]
    for q in chip_order(base):
        entries_ref[rows_of(q), :] = running
        running = parts_ref[rows_of(q), :] + flag(flags_ref, base + KEEPS + q) * running
    for flip, out_ref in zip((0,) + FLIPS, (keep_ref,) + send_refs):
        out_ref[...] = entries_ref[piece(at ^ flip), :]


def unpair_kernel(flags_ref, own_ref, got_ref, keep_ref, *refs, base):
    back_refs, (mine_ref, send_ref, whole_ref) = refs[: len(FLIPS)], refs[len(FLIPS) :]
    _, at, core = place()
    for flip, in_ref in zip((0,) + FLIPS, (keep_ref,) + back_refs):
        whole_ref[piece(at ^ flip), :] = in_ref[...]
    keep = flag(flags_ref, base + KEEP_BLOCK)
    is_earlier = (core == 1) if base else (core == 0)

    @pl.when(is_earlier)
    def _():
        mine_ref[...] = whole_ref[...]
        send_ref[...] = own_ref[...] + keep * whole_ref[...]

    @pl.when(jnp.logical_not(is_earlier))
    def _():
        mine_ref[...] = got_ref[...] + keep * whole_ref[...]
        send_ref[...] = whole_ref[...]


def mask_kernel(flags_ref, mask_ref):
    mask_ref[...] = pair_mask(flags_ref)


def local_kernel(query_ref, key_ref, value_ref, mask_ref, out_ref, *, own):
    for k in range(COLUMNS):
        cols = column(k, own)
        for r in range(2):
            rows = slice(r * HALF, (r + 1) * HALF)
            upto = (r + 1) * HALF
            weights = dot(query_ref[rows, cols], key_ref[:upto, cols], NT).astype(BF16)
            weights = weights * mask_ref[rows, :upto]
            out_ref[rows, head(k)] = dot(weights, value_ref[:upto, cols], NN)


def beside(state):
    return jnp.concatenate([state[:HEAD_DIM], state[HEAD_DIM:]], axis=1)


def mixed_kernel(flags_ref, query_ref, local_ref, entry_ref, grad_ref, gain_ref, *refs, own):
    if own:
        mixed_ref, states_ref, squares_ref, dots_ref = refs
        squares = jnp.zeros((BLOCK, HEAD_DIM), F32)
        dots = jnp.zeros((BLOCK, HEAD_DIM), F32)
    else:
        squares_ref, dots_ref, mixed_ref, states_ref, sums_ref = refs
        squares = squares_ref[...]
        dots = dots_ref[...]
    mask = row_mask(flags_ref, FOLLOWS)
    for k in range(COLUMNS):
        cols = column(k, own)
        state = split(entry_ref[rows_of(k), :])
        states_ref[k] = state
        mixed = local_ref[:, head(k)] + dot(twice(query_ref[:, cols] * mask), state, NN)
        mixed_ref[:, head(k)] = mixed
        squares = squares + mixed * mixed
        dots = dots + mixed * (gain_ref[:, cols] * grad_ref[:, cols].astype(F32))
    if own:
        squares_ref[...] = squares
        dots_ref[...] = dots
    else:
        sums_ref[0:1, :] = jnp.sum(squares.T, axis=0, keepdims=True)
        sums_ref[1:2, :] = jnp.sum(dots.T, axis=0, keepdims=True)


def grad_kernel(flags_ref, query_ref, grad_ref, gain_ref, mixed_ref, *refs, own):
    if own:
        inverse_ref, dots_ref, grad_mixed_ref, upper_ref = refs
        inverse = inverse_ref[...]
        dots = dots_ref[...]
    else:
        sums_refs, (grad_mixed_ref, upper_ref, inverse_ref, dots_ref) = refs[:4], refs[4:]
        total = sums_refs[0][...]
        for more_ref in sums_refs[1:]:
            total = total + more_ref[...]
        over = 1.0 / jnp.sqrt(total[0:1, :] / WIDTH + EPSILON)
        inverse = jnp.broadcast_to(over, (HEAD_DIM, BLOCK)).T
        dots = jnp.broadcast_to(total[1:2, :] * over / WIDTH, (HEAD_DIM, BLOCK)).T
        inverse_ref[...] = inverse
        dots_ref[...] = dots
    mask = row_mask(flags_ref, FIRST)
    for k in range(COLUMNS):
        cols = column(k, own)
        normed = mixed_ref[:, head(k)] * inverse
        scaled = gain_ref[:, cols] * grad_ref[:, cols].astype(F32)
        grad_mixed = ((scaled - normed * dots) * inverse).astype(BF16)
        grad_mixed_ref[:, head(k)] = grad_mixed
        upper_ref[rows_of(k), :] = dot(query_ref[:, cols] * mask, grad_mixed, TN)


def normed_kernel(own_ref, other_ref, inverse_ref, gain_ref, out_ref):
    inverse = inverse_ref[...]
    for own, mixed_ref in ((True, own_ref), (False, other_ref)):
        for k in range(COLUMNS):
            cols = column(k, own)
            out_ref[:, cols] = (mixed_ref[:, head(k)] * inverse * gain_ref[:, cols]).astype(BF16)


def back_kernel(
    flags_ref,
    query_ref,
    key_ref,
    value_ref,
    mask_ref,
    grad_ref,
    states_ref,
    query_out_ref,
    key_out_ref,
    value_out_ref,
    *,
    own,
    heads,
):
    follows = row_mask(flags_ref, FOLLOWS)
    for n, k in enumerate(heads):
        cols = column(k, own)
        at = head(k)
        to = head(n)
        from_state = dot(twice(grad_ref[:, at] * follows), beside(states_ref[k]), NT)
        for r in range(2):
            rows = slice(r * HALF, (r + 1) * HALF)
            upto = (r + 1) * HALF
            mask = mask_ref[rows, :upto]
            weights = dot(query_ref[rows, cols], key_ref[:upto, cols], NT).astype(BF16) * mask
            grads = dot(grad_ref[rows, at], value_ref[:upto, cols], NT).astype(BF16) * mask
            query_out_ref[rows, to] = (
                dot(grads, key_ref[:upto, cols], NN) + from_state[rows, :]
            ).astype(BF16)
            key_part = dot(grads, query_ref[rows, cols], TN)
            value_part = dot(weights, grad_ref[rows, at], TN)
            if r == 0:
                key_out_ref[:HALF, to] = key_part
                value_out_ref[:HALF, to] = value_part
            else:
                key_out_ref[:HALF, to] += key_part[:HALF, :]
                value_out_ref[:HALF, to] += value_part[:HALF, :]
                key_out_ref[HALF:, to] = key_part[HALF:, :]
                value_out_ref[HALF:, to] = value_part[HALF:, :]


def store_kernel(*refs):
    parts, (out_ref, sems) = refs[:-2], refs[-2:]
    copies = []
    for g, part_ref in enumerate(parts):
        own = g < BACK_GROUPS // 2
        to = out_ref.at[:, column(g % (BACK_GROUPS // 2) * BACK_HEADS, own, BACK_HEADS)]
        copies.append(pltpu.make_async_copy(part_ref, to, sems.at[g]))
        copies[-1].start()
    for copy in copies:
        copy.wait()


def final_kernel(flags_ref, key_ref, value_ref, *refs, own):
    count = BACK_GROUPS // 2
    parts, (entry_ref, *refs) = refs[: 2 * count], refs[2 * count :]
    key_out_ref, value_out_ref, key_buf, value_buf, sems = refs[0 if own else 2 :]
    copies = []

    def send(source, target, sem):
        copies.append(pltpu.make_async_copy(source, target, sem))
        copies[-1].start()

    leads = row_mask(flags_ref, LEADS)
    for k in range(COLUMNS):
        cols = column(k, own)
        at = head(k)
        group, n = divmod(k, BACK_HEADS)
        state = split(entry_ref[rows_of(k), :])
        from_values = dot(twice(value_ref[:, cols] * leads), beside(state), NT)
        key_buf[:, at] = (parts[2 * group][:, head(n)] + from_values).astype(BF16)
        send(key_buf.at[:, at], key_out_ref.at[:, cols], sems.at[0, k])
        from_keys = dot(twice(key_ref[:, cols] * leads), state, NN)
        value_buf[:, at] = (parts[2 * group + 1][:, head(n)] + from_keys).astype(BF16)
        send(value_buf.at[:, at], value_out_ref.at[:, cols], sems.at[1, k])
    for copy in copies:
        copy.wait()


BACK_GROUPS = 4
BACK_HEADS = CORES * COLUMNS // BACK_GROUPS


def on_device(queries, key_input, value_input, norm_gain, out_grad, doc_lengths):
    rows_here, width_here = queries.shape
    heads_here = width_here // HEAD_DIM
    devices = lax.axis_size("ctx")
    half_rows = COLUMNS * HEAD_DIM

    vmem = pl.BlockSpec(memory_space=pltpu.VMEM)
    hbm = pl.BlockSpec(memory_space=pltpu.HBM)

    def array(rows, cols, kind=F32):
        return jax.ShapeDtypeStruct((rows, cols), kind)

    wide_f32 = array(rows_here, width_here)
    wide_bf16 = array(rows_here, width_here, BF16)
    wide_buffer = pltpu.VMEM((rows_here, width_here), BF16)
    half = array(half_rows, HEAD_DIM)
    part = array(HEAD_DIM, HEAD_DIM)
    states = jax.ShapeDtypeStruct((heads_here, 2 * HEAD_DIM, HEAD_DIM), BF16)

    product = 2 * rows_here * HEAD_DIM * HEAD_DIM

    def call(body, name, args, shapes, flops, scratch=(), ins=None, outs=None, limit=32, alias=None, **fixed):
        moved = sum(a.size * a.dtype.itemsize for a in [*args, *shapes])
        return pl.pallas_call(
            lambda *refs: body(*refs, **fixed),
            name=name,
            in_specs=ins or [vmem] * len(args),
            out_specs=outs or [vmem] * len(shapes),
            out_shape=list(shapes),
            scratch_shapes=list(scratch),
            input_output_aliases=alias or {},
            compiler_params=pltpu.CompilerParams(vmem_limit_bytes=limit << 20),
            cost_estimate=pl.CostEstimate(flops=flops, bytes_accessed=moved, transcendentals=0),
        )(*args)

    gain = norm_gain.reshape(1, width_here)

    def move(values, source):
        return lax.ppermute(values, "ctx", [(source(i), i) for i in range(devices)])

    def swap(values):
        return move(values, lambda i: i ^ 1)

    def along_row(values):
        return [
            move(v, lambda i, f=f: i ^ (f * CORES) ^ (f % CORES)) for v, f in zip(values, FLIPS)
        ]

    def beneath(after, moved, work):
        started = lax.optimization_barrier((after, *work[0]))
        done = work[1](started[1:])
        moved, done = lax.optimization_barrier((moved, done))
        return moved, done

    def scan(flags, other, base, works):
        tag = "back" if base else "ahead"
        row = CORES * COLUMNS
        sign = row if base else -row
        results = []
        got, (own, *rest) = beneath(other, swap(other), works[0]())
        results.append(rest)
        keep, *sends = call(
            pair_kernel, "pair_" + tag, (flags, own, got), [part] * 4, 4 * half.size, base=base
        )
        gathered, done = beneath(keep, along_row(sends), works[1]())
        results.append(done)
        parts, total = call(
            row_kernel, "row_" + tag, (flags, keep, *gathered), [half, part], 2 * half.size, base=base
        )
        far = move(total, lambda i: (i + 2 * sign) % devices)
        near = move(total, lambda i: (i + sign) % devices ^ 1)
        (near, far), done = beneath(parts, (near, far), works[2]())
        results.append(done)
        keep, *sends = call(
            enter_kernel,
            "enter_" + tag,
            (flags, parts, near, far),
            [part] * 4,
            4 * half.size,
            [pltpu.VMEM((half_rows, HEAD_DIM), F32)],
            base=base,
        )
        back, done = beneath(keep, along_row(sends), works[3]())
        results.append(done)
        mine, send = call(
            unpair_kernel,
            "unpair_" + tag,
            (flags, own, got, keep, *back),
            [half, half],
            4 * half.size,
            [pltpu.VMEM((half_rows, HEAD_DIM), F32)],
            base=base,
        )
        met, done = beneath(send, swap(send), works[4](mine))
        results.append(done)
        return met, results

    other, flags, keys, values = call(
        state_kernel,
        "states",
        (doc_lengths, key_input, value_input),
        [half, array(FLAGS, HEAD_DIM), wide_bf16, wide_bf16],
        4 * product,
        [pltpu.SMEM((NDOCS,), I32), pltpu.SemaphoreType.DMA((3, GRAINS))],
        [hbm, hbm, hbm],
        limit=51,
    )
    inputs = (queries, keys, values)
    (pair_masks,) = call(
        mask_kernel,
        "pair_mask",
        (flags,),
        [jax.ShapeDtypeStruct((BLOCK, BLOCK), BF16)],
        BLOCK * BLOCK,
    )
    side_f32 = array(rows_here, COLUMNS * HEAD_DIM)
    side_bf16 = array(rows_here, COLUMNS * HEAD_DIM, BF16)
    side_states = jax.ShapeDtypeStruct((COLUMNS, 2 * HEAD_DIM, HEAD_DIM), BF16)
    column_f32 = array(rows_here, HEAD_DIM)

    def own_states(args):
        return call(own_state_kernel, "own_states", args, [half], 4 * product)

    def mix_work(own):
        def run(args):
            return call(local_kernel, "local_mix", args, [side_f32], 24 * product, own=own)

        return (*inputs, pair_masks), run

    def nothing():
        return (), lambda args: []

    local = {}

    def first_mix():
        args, run = mix_work(True)

        def keep_it(args):
            local[True] = run(args)[0]
            return [local[True]]

        return args, keep_it

    def mixed_work(mine):
        def run(args):
            return call(
                mixed_kernel,
                "mix_own",
                args,
                [side_f32, side_states, column_f32, column_f32],
                8 * product,
                own=True,
            )

        return (flags, queries, local[True], mine, out_grad, gain), run

    entry, results = scan(
        flags,
        other,
        0,
        [
            lambda: ((flags, keys, values), own_states),
            first_mix,
            lambda: mix_work(False),
            nothing,
            mixed_work,
        ],
    )
    _, _, (local_other,), _, (mixed_own, states_own, *sums_so_far) = results
    mixed_other, states_other, sums = call(
        mixed_kernel,
        "mix_states",
        (flags, queries, local_other, entry, out_grad, gain, *sums_so_far),
        [side_f32, side_states, array(2, rows_here)],
        8 * product,
        own=False,
    )
    others = [
        lax.ppermute(sums, "head", [(i, i ^ flip) for i in range(lax.axis_size("head"))])
        for flip in FLIPS
    ]
    grad_other, other, inverse, dots = call(
        grad_kernel,
        "norm_grad",
        (flags, queries, out_grad, gain, mixed_other, sums, *others),
        [side_bf16, half, column_f32, column_f32],
        4 * product,
        own=False,
    )
    made = {}
    query_parts, pieces = [], []

    def own_grad(args):
        grad_own, own = call(grad_kernel, "own_grad", args, [side_bf16, half], 4 * product, own=True)
        made[True] = grad_own
        return [own, grad_own]

    def back(own, g, args):
        first = g * BACK_HEADS
        query_part, *rest = call(
            back_kernel,
            "local_back",
            args,
            [array(rows_here, BACK_HEADS * HEAD_DIM, BF16)]
            + [array(rows_here, BACK_HEADS * HEAD_DIM)] * 2,
            17 * BACK_HEADS * product,
            own=own,
            heads=range(first, first + BACK_HEADS),
        )
        query_parts.append(query_part)
        pieces.append(rest)
        return [query_part, *rest]

    back_args = (flags, *inputs, pair_masks)

    def first_back():
        def run(args):
            done = back(True, 0, args[:7])
            return [*done, *call(normed_kernel, "normed", args[7:], [wide_bf16], 2 * wide_f32.size)]

        whole = (mixed_own, mixed_other, inverse, gain)
        return (*back_args, made[True], states_own, *whole), run

    def second_back():
        def run(args):
            return [*back(True, 1, args[:7]), *back(False, 0, (*args[:5], *args[7:]))]

        return (*back_args, made[True], states_own, grad_other, states_other), run

    def third_back():
        def run(args):
            back(False, 1, args)
            return call(
                store_kernel,
                "store",
                query_parts,
                [wide_bf16],
                wide_f32.size,
                [pltpu.SemaphoreType.DMA((BACK_GROUPS,))],
                outs=[hbm],
            )

        return (*back_args, grad_other, states_other), run

    def final(own, args, so_far=()):
        buffer = pltpu.VMEM((rows_here, COLUMNS * HEAD_DIM), BF16)
        return call(
            final_kernel,
            "own_final" if own else "back_states",
            (*args, *so_far),
            [wide_bf16] * 2,
            16 * product,
            [buffer, buffer, pltpu.SemaphoreType.DMA((2, COLUMNS))],
            ins=[vmem] * len(args) + [hbm] * len(so_far),
            outs=[hbm] * 2,
            alias={len(args) + n: n for n in range(len(so_far))},
            own=own,
        )

    def final_args(which, entry):
        return (flags, keys, values, *(x for g in which for x in pieces[g]), entry)

    leave, results = scan(
        flags,
        other,
        DIRECTION,
        [
            lambda: ((flags, queries, out_grad, gain, mixed_own, inverse, dots), own_grad),
            first_back,
            second_back,
            third_back,
            lambda mine: (final_args((0, 1), mine), lambda args: final(True, args)),
        ],
    )
    normed_out = results[1][-1]
    (query_grad,) = results[3]
    key_grad, value_grad = final(False, final_args((2, 3), leave), results[4])
    return (normed_out, query_grad, key_grad, value_grad)


def solution(mesh):
    wide = P("ctx", "head")
    return jax.shard_map(
        on_device,
        mesh=mesh,
        in_specs=(wide, wide, wide, P("head"), wide, P()),
        out_specs=(wide, wide, wide, wide),
        check_vma=False,
    )
```

time: 71 us -> 68.7 us (0.968)
  waiting for transfers between devices: 19.8 us -> 16.1 us
  Pallas kernels: 19.7 us -> 20.6 us
    ppermute x20, waiting for transfers between devices: 17.3 us -> 13.5 us  [move(): return lax.ppermute(values, 'ctx', [(source(i), i) for i in range(devices)])]
    pallas_call x21 -> x25, Pallas kernels: 19.7 us -> 20.6 us  [call(): pl.pallas_call(lambda *refs: body(*refs, **fixed), name=name, in_specs=in...]
  transfers between devices with their start and end apart: 23 -> 23, of which waited for: 16 -> 14; matrix products, arithmetic and copies ran while one was open for 0% -> 0% of each run, Pallas kernels for 17% -> 22%
where the time goes in v5:
time: 68.7 us; the launch traced here: 68.6 us
  starting transfers between devices  29.5 us (43%)
  Pallas kernels  20.6 us (30%)
  waiting for transfers between devices  16.1 us (23%)
  local copies, waits for them, and re-layouts  1.24 us (2%)
  between operations  1.08 us (2%)
    ppermute x20, starting transfers between devices, move(): return lax.ppermute(values, 'ctx', [(source(i), i) for i in range(devices)])  25.6 us
    pallas_call x25, Pallas kernels, call(): pl.pallas_call(lambda *refs: body(*refs, **fixed), name=name, in_specs=in...  20.6 us
    ppermute x20, waiting for transfers between devices, move(): return lax.ppermute(values, 'ctx', [(source(i), i) for i in range(devices)])  13.5 us
    ppermute x3, starting transfers between devices, on_device(): lax.ppermute(sums, 'head', [(i, i ^ flip) for i in range(lax.axis_size('h...  3.94 us
    ppermute x3, waiting for transfers between devices, on_device(): lax.ppermute(sums, 'head', [(i, i ^ flip) for i in range(lax.axis_size('h...  2.58 us
  transfers between devices with their start and end apart: 23, of which 14 were waited for; matrix products, arithmetic and copies ran while one was open for 0% of the time, Pallas kernels for 22%

profile of v5, /device:TPU:1, one launch (start us, length us, event | category | flops | bytes accessed | tf_op | source)
XLA Modules:
  0.0 68.6 jit_solution(16424761300661949788)
XLA Ops:
  1.3 1.8 %states.1 = (f32[512,128]{1,0:T(8,128)S(1)}, f32[40,128]{1,0:T(8,128)S(1)}, bf16[512,1024]{1,0:T(8,128)(2,1)S(1)}, bf16[512,1024]{1,0:T(8,128)(2,1)S(1)}) custom-call(s32[8]{0:T(128)S(1)} %copy-done.3, bf16[512,1024]{1,0:T(8,128)(2,1)} %refs_1_.3, bf16[512,1024]{1,0:T(8,128)(2,1)} %refs_2_.2), custom_call_target="tpu_custom_call" | custom-call | flops 67108864 | bytes 4476960 | tf_op jit(solution)/shard_map/states/pallas_call | solution.py:463
  3.1 1.5 %collective-permute-start = (f32[512,128]{1,0:T(8,128)S(1)}, f32[512,128]{1,0:T(8,128)S(1)}, u32[]{:S(2)}, u32[]{:S(2)}) collective-permute-start(f32[512,128]{1,0:T(8,128)S(1)} %get-tuple-element.155), channel_id=1, source_target_pairs={{1,0},{0,1},{3,2},{2,3},{5,4},{4,5},{7,6},{6,7},{9,8},{8,9},{11,10... | collective-permute-start | bytes 786440 | tf_op jit(solution)/shard_map/ppermute | solution.py:478
  5.8 3.1 %collective-permute-start.1 = (f32[128,128]{1,0:T(8,128)S(1)}, f32[128,128]{1,0:T(8,128)S(1)}, u32[]{:S(2)}, u32[]{:S(2)}) collective-permute-start(f32[128,128]{1,0:T(8,128)S(1)} %get-tuple-element.164), channel_id=1, source_target_pairs={{4,0},{5,1},{6,2},{7,3},{0,4},{1,5},{2,6},{3,7},{12,8},{13,9},{14,... | collective-permute-start | bytes 196616 | tf_op jit(solution)/shard_map/ppermute | solution.py:478
  10.3 1.5 %local_mix.2.refs_2_ = f32[512,512]{1,0:T(8,128)S(1)} custom-call(bf16[512,1024]{1,0:T(8,128)(2,1)S(1)} %copy-done, bf16[512,1024]{1,0:T(8,128)(2,1)S(1)} %get-tuple-element.287.refs_1_.refs_2_, bf16[512,1024]{1,0:T(8,128)(2,1)S(1)} %get-tuple-element.288.refs_2_.refs_3_, bf16[512,512]{1,0:T(8,128)(2,1)S(1)} %pair_mask.1.refs_3_.refs_4_), custom_call_target="tpu_custom_call" | custom-call | flops 402653184 | bytes 4718592 | tf_op jit(solution)/shard_map/local_mix/pallas_call | solution.py:463
  11.8 1.8 %collective-permute-done.2.refs_3_ = f32[128,128]{1,0:T(8,128)S(1)} collective-permute-done((f32[128,128]{1,0:T(8,128)S(1)}, f32[128,128]{1,0:T(8,128)S(1)}, u32[]{:S(2)}, u32[]{:S(2)}) %collective-permute-start.2) | collective-permute-done | bytes 65568 | tf_op jit(solution)/shard_map/ppermute | solution.py:478
  14.8 3.7 %collective-permute-start.5 = (f32[128,128]{1,0:T(8,128)S(1)}, f32[128,128]{1,0:T(8,128)S(1)}, u32[]{:S(2)}, u32[]{:S(2)}) collective-permute-start(f32[128,128]{1,0:T(8,128)S(1)} %get-tuple-element.174), channel_id=1, source_target_pairs={{16,0},{17,1},{18,2},{19,3},{20,4},{21,5},{22,6},{23,7},{24,8},{25... | collective-permute-start | bytes 196616 | tf_op jit(solution)/shard_map/ppermute | solution.py:478
  19.2 1.4 %local_mix.3.refs_2_ = f32[512,512]{1,0:T(8,128)S(1)} custom-call(bf16[512,1024]{1,0:T(8,128)(2,1)S(1)} %copy-done, bf16[512,1024]{1,0:T(8,128)(2,1)S(1)} %get-tuple-element.287.refs_1_.refs_2_, bf16[512,1024]{1,0:T(8,128)(2,1)S(1)} %get-tuple-element.288.refs_2_.refs_3_, bf16[512,512]{1,0:T(8,128)(2,1)S(1)} %pair_mask.1.refs_3_.refs_4_), custom_call_target="tpu_custom_call" | custom-call | flops 402653184 | bytes 4718592 | tf_op jit(solution)/shard_map/local_mix/pallas_call | solution.py:463
  21.1 2.4 %collective-permute-done.4.refs_2_ = f32[128,128]{1,0:T(8,128)S(1)} collective-permute-done((f32[128,128]{1,0:T(8,128)S(1)}, f32[128,128]{1,0:T(8,128)S(1)}, u32[]{:S(2)}, u32[]{:S(2)}) %collective-permute-start.4) | collective-permute-done | bytes 65568 | tf_op jit(solution)/shard_map/ppermute | solution.py:478
  23.6 1.8 %collective-permute-start.6 = (f32[128,128]{1,0:T(8,128)S(1)}, f32[128,128]{1,0:T(8,128)S(1)}, u32[]{:S(2)}, u32[]{:S(2)}) collective-permute-start(f32[128,128]{1,0:T(8,128)S(1)} %get-tuple-element.184), channel_id=1, source_target_pairs={{4,0},{5,1},{6,2},{7,3},{0,4},{1,5},{2,6},{3,7},{12,8},{13,9},{14,... | collective-permute-start | bytes 196616 | tf_op jit(solution)/shard_map/ppermute | solution.py:478
  27.2 1.5 %collective-permute-done.6.refs_4_ = f32[128,128]{1,0:T(8,128)S(1)} collective-permute-done((f32[128,128]{1,0:T(8,128)S(1)}, f32[128,128]{1,0:T(8,128)S(1)}, u32[]{:S(2)}, u32[]{:S(2)}) %collective-permute-start.6) | collective-permute-done | bytes 65568 | tf_op jit(solution)/shard_map/ppermute | solution.py:478
  28.7 1.7 %collective-permute-done.7.refs_5_ = f32[128,128]{1,0:T(8,128)S(1)} collective-permute-done((f32[128,128]{1,0:T(8,128)S(1)}, f32[128,128]{1,0:T(8,128)S(1)}, u32[]{:S(2)}, u32[]{:S(2)}) %collective-permute-start.7) | collective-permute-done | bytes 65568 | tf_op jit(solution)/shard_map/ppermute | solution.py:478
  34.0 2.6 %collective-permute-start.12 = (f32[2,512]{1,0:T(2,128)S(1)}, f32[2,512]{1,0:T(2,128)S(1)}, u32[]{:S(2)}, u32[]{:S(2)}) collective-permute-start(f32[2,512]{1,0:T(2,128)S(1)} %get-tuple-element.206.refs_5_), channel_id=1, source_target_pairs={{0,96},{32,64},{64,32},{96,0},{1,97},{33,65},{65,33},{97,1},{2,98}... | collective-permute-start | bytes 12296 | tf_op jit(solution)/shard_map/ppermute | solution.py:618
  36.6 1.4 %collective-permute-start.10 = (f32[2,512]{1,0:T(2,128)S(1)}, f32[2,512]{1,0:T(2,128)S(1)}, u32[]{:S(2)}, u32[]{:S(2)}) collective-permute-start(f32[2,512]{1,0:T(2,128)S(1)} %get-tuple-element.206.refs_5_), channel_id=1, source_target_pairs={{0,64},{32,96},{64,0},{96,32},{1,65},{33,97},{65,1},{97,33},{2,66}... | collective-permute-start | bytes 12296 | tf_op jit(solution)/shard_map/ppermute | solution.py:618
  39.0 1.5 %collective-permute-done.10.refs_6_ = f32[2,512]{1,0:T(2,128)S(1)} collective-permute-done((f32[2,512]{1,0:T(2,128)S(1)}, f32[2,512]{1,0:T(2,128)S(1)}, u32[]{:S(2)}, u32[]{:S(2)}) %collective-permute-start.10) | collective-permute-done | bytes 4128 | tf_op jit(solution)/shard_map/ppermute | solution.py:618
  41.3 1.9 %collective-permute-start.13 = (f32[512,128]{1,0:T(8,128)S(1)}, f32[512,128]{1,0:T(8,128)S(1)}, u32[]{:S(2)}, u32[]{:S(2)}) collective-permute-start(f32[512,128]{1,0:T(8,128)S(1)} %get-tuple-element.207), channel_id=1, source_target_pairs={{1,0},{0,1},{3,2},{2,3},{5,4},{4,5},{7,6},{6,7},{9,8},{8,9},{11,10... | collective-permute-start | bytes 786440 | tf_op jit(solution)/shard_map/ppermute | solution.py:478
  46.7 1.3 %collective-permute-start.16 = (f32[128,128]{1,0:T(8,128)S(1)}, f32[128,128]{1,0:T(8,128)S(1)}, u32[]{:S(2)}, u32[]{:S(2)}) collective-permute-start(f32[128,128]{1,0:T(8,128)S(1)} %get-tuple-element.224), channel_id=1, source_target_pairs={{7,0},{6,1},{5,2},{4,3},{3,4},{2,5},{1,6},{0,7},{15,8},{14,9},{13,... | collective-permute-start | bytes 196616 | tf_op jit(solution)/shard_map/ppermute | solution.py:478
  49.3 1.8 %local_back.4 = (bf16[512,256]{1,0:T(8,128)(2,1)S(1)}, f32[512,256]{1,0:T(8,128)S(1)}, f32[512,256]{1,0:T(8,128)S(1)}) custom-call(f32[40,128]{1,0:T(8,128)S(1)} %get-tuple-element.286.refs_0_, bf16[512,1024]{1,0:T(8,128)(2,1)S(1)} %copy-done, bf16[512,1024]{1,0:T(8,128)(2,1)S(1)} %get-tuple-element.287.refs_1_.refs_2_, ...), custom_call_target="tpu_custom_call" | custom-call | flops 570425344 | bytes 5787648 | tf_op jit(solution)/shard_map/local_back/pallas_call | solution.py:463
  52.6 1.5 %collective-permute-start.17 = (f32[128,128]{1,0:T(8,128)S(1)}, f32[128,128]{1,0:T(8,128)S(1)}, u32[]{:S(2)}, u32[]{:S(2)}) collective-permute-start(f32[128,128]{1,0:T(8,128)S(1)} %get-tuple-element.246), channel_id=1, source_target_pairs={{9,0},{8,1},{11,2},{10,3},{13,4},{12,5},{15,6},{14,7},{17,8},{16,9... | collective-permute-start | bytes 196616 | tf_op jit(solution)/shard_map/ppermute | solution.py:478
  54.1 1.8 %local_back.5 = (bf16[512,256]{1,0:T(8,128)(2,1)S(1)}, f32[512,256]{1,0:T(8,128)S(1)}, f32[512,256]{1,0:T(8,128)S(1)}) custom-call(f32[40,128]{1,0:T(8,128)S(1)} %get-tuple-element.286.refs_0_, bf16[512,1024]{1,0:T(8,128)(2,1)S(1)} %copy-done, bf16[512,1024]{1,0:T(8,128)(2,1)S(1)} %get-tuple-element.287.refs_1_.refs_2_, ...), custom_call_target="tpu_custom_call" | custom-call | flops 570425344 | bytes 5787648 | tf_op jit(solution)/shard_map/local_back/pallas_call | solution.py:463
  55.9 1.8 %local_back.6 = (bf16[512,256]{1,0:T(8,128)(2,1)S(1)}, f32[512,256]{1,0:T(8,128)S(1)}, f32[512,256]{1,0:T(8,128)S(1)}) custom-call(f32[40,128]{1,0:T(8,128)S(1)} %get-tuple-element.286.refs_0_, bf16[512,1024]{1,0:T(8,128)(2,1)S(1)} %copy-done, bf16[512,1024]{1,0:T(8,128)(2,1)S(1)} %get-tuple-element.287.refs_1_.refs_2_, ...), custom_call_target="tpu_custom_call" | custom-call | flops 570425344 | bytes 5787648 | tf_op jit(solution)/shard_map/local_back/pallas_call | solution.py:463
  58.5 1.7 %collective-permute-start.20 = (f32[128,128]{1,0:T(8,128)S(1)}, f32[128,128]{1,0:T(8,128)S(1)}, u32[]{:S(2)}, u32[]{:S(2)}) collective-permute-start(f32[128,128]{1,0:T(8,128)S(1)} %get-tuple-element.267), channel_id=1, source_target_pairs={{3,0},{2,1},{1,2},{0,3},{7,4},{6,5},{5,6},{4,7},{11,8},{10,9},{9,1... | collective-permute-start | bytes 196616 | tf_op jit(solution)/shard_map/ppermute | solution.py:478
  61.4 1.8 %local_back.7 = (bf16[512,256]{1,0:T(8,128)(2,1)S(1)}, f32[512,256]{1,0:T(8,128)S(1)}, f32[512,256]{1,0:T(8,128)S(1)}) custom-call(f32[40,128]{1,0:T(8,128)S(1)} %get-tuple-element.286.refs_0_, bf16[512,1024]{1,0:T(8,128)(2,1)S(1)} %copy-done, bf16[512,1024]{1,0:T(8,128)(2,1)S(1)} %get-tuple-element.287.refs_1_.refs_2_, ...), custom_call_target="tpu_custom_call" | custom-call | flops 570425344 | bytes 5787648 | tf_op jit(solution)/shard_map/local_back/pallas_call | solution.py:463
  65.4 1.5 %own_final.1 = (bf16[512,1024]{1,0:T(8,128)(2,1)}, bf16[512,1024]{1,0:T(8,128)(2,1)}) custom-call(f32[40,128]{1,0:T(8,128)S(1)} %get-tuple-element.286.refs_0_, bf16[512,1024]{1,0:T(8,128)(2,1)S(1)} %get-tuple-element.287.refs_1_.refs_2_, bf16[512,1024]{1,0:T(8,128)(2,1)S(1)} %get-tuple-element.288.refs_2_.refs_3_, ...), custom_call_target="tpu_custom_call" | custom-call | flops 268435456 | bytes 6574080 | tf_op jit(solution)/shard_map/own_final/pallas_call | solution.py:463
  66.9 1.5 %back_states.1 = (bf16[512,1024]{1,0:T(8,128)(2,1)}, bf16[512,1024]{1,0:T(8,128)(2,1)}) custom-call(f32[40,128]{1,0:T(8,128)S(1)} %get-tuple-element.286.refs_0_, bf16[512,1024]{1,0:T(8,128)(2,1)S(1)} %get-tuple-element.287.refs_1_.refs_2_, bf16[512,1024]{1,0:T(8,128)(2,1)S(1)} %get-tuple-element.288.refs_2_.refs_3_, ...), custom_call_target="tpu_custom_call", output_to_operand_aliasing={{0}: (8, {}), {1}: (9, {})} | custom-call | flops 268435456 | bytes 8671232 | tf_op jit(solution)/shard_map/back_states/pallas_call | solution.py:463
  (55 shorter events, 23.4 us)
Async XLA Ops:
  3.1 2.7 %collective-permute-start = (f32[512,128]{1,0:T(8,128)S(1)}, f32[512,128]{1,0:T(8,128)S(1)}, u32[]{:S(2)}, u32[]{:S(2)}) collective-permute-start(f32[512,128]{1,0:T(8,128)S(1)} %get-tuple-element.155), channel_id=1, source_target_pairs={{1,0},{0,1},{3,2},{2,3},{5,4},{4,5},{7,6},{6,7},{9,8},{8,9},{11,10... | collective-permute-start | bytes 786440 | tf_op jit(solution)/shard_map/ppermute | solution.py:478
  5.8 5.9 %collective-permute-start.1 = (f32[128,128]{1,0:T(8,128)S(1)}, f32[128,128]{1,0:T(8,128)S(1)}, u32[]{:S(2)}, u32[]{:S(2)}) collective-permute-start(f32[128,128]{1,0:T(8,128)S(1)} %get-tuple-element.164), channel_id=1, source_target_pairs={{4,0},{5,1},{6,2},{7,3},{0,4},{1,5},{2,6},{3,7},{12,8},{13,9},{14,... | collective-permute-start | bytes 196616 | tf_op jit(solution)/shard_map/ppermute | solution.py:478
  8.9 4.7 %collective-permute-start.2 = (f32[128,128]{1,0:T(8,128)S(1)}, f32[128,128]{1,0:T(8,128)S(1)}, u32[]{:S(2)}, u32[]{:S(2)}) collective-permute-start(f32[128,128]{1,0:T(8,128)S(1)} %get-tuple-element.165), channel_id=1, source_target_pairs={{3,0},{2,1},{1,2},{0,3},{7,4},{6,5},{5,6},{4,7},{11,8},{10,9},{9,1... | collective-permute-start | bytes 196616 | tf_op jit(solution)/shard_map/ppermute | solution.py:478
  9.8 4.9 %collective-permute-start.3 = (f32[128,128]{1,0:T(8,128)S(1)}, f32[128,128]{1,0:T(8,128)S(1)}, u32[]{:S(2)}, u32[]{:S(2)}) collective-permute-start(f32[128,128]{1,0:T(8,128)S(1)} %get-tuple-element.166), channel_id=1, source_target_pairs={{7,0},{6,1},{5,2},{4,3},{3,4},{2,5},{1,6},{0,7},{15,8},{14,9},{13,... | collective-permute-start | bytes 196616 | tf_op jit(solution)/shard_map/ppermute | solution.py:478
  14.8 6.3 %collective-permute-start.5 = (f32[128,128]{1,0:T(8,128)S(1)}, f32[128,128]{1,0:T(8,128)S(1)}, u32[]{:S(2)}, u32[]{:S(2)}) collective-permute-start(f32[128,128]{1,0:T(8,128)S(1)} %get-tuple-element.174), channel_id=1, source_target_pairs={{16,0},{17,1},{18,2},{19,3},{20,4},{21,5},{22,6},{23,7},{24,8},{25... | collective-permute-start | bytes 196616 | tf_op jit(solution)/shard_map/ppermute | solution.py:478
  18.5 5.1 %collective-permute-start.4 = (f32[128,128]{1,0:T(8,128)S(1)}, f32[128,128]{1,0:T(8,128)S(1)}, u32[]{:S(2)}, u32[]{:S(2)}) collective-permute-start(f32[128,128]{1,0:T(8,128)S(1)} %get-tuple-element.174), channel_id=1, source_target_pairs={{25,0},{24,1},{27,2},{26,3},{29,4},{28,5},{31,6},{30,7},{1,8},{0,9... | collective-permute-start | bytes 196616 | tf_op jit(solution)/shard_map/ppermute | solution.py:478
  20.7 11.1 %copy-start.1 = (bf16[512,1024]{1,0:T(8,128)(2,1)S(1)}, bf16[512,1024]{1,0:T(8,128)(2,1)}, u32[]{:S(2)}) copy-start(bf16[512,1024]{1,0:T(8,128)(2,1)} %refs_2_.4) | copy-start | bytes 3145732
  23.6 5.1 %collective-permute-start.6 = (f32[128,128]{1,0:T(8,128)S(1)}, f32[128,128]{1,0:T(8,128)S(1)}, u32[]{:S(2)}, u32[]{:S(2)}) collective-permute-start(f32[128,128]{1,0:T(8,128)S(1)} %get-tuple-element.184), channel_id=1, source_target_pairs={{4,0},{5,1},{6,2},{7,3},{0,4},{1,5},{2,6},{3,7},{12,8},{13,9},{14,... | collective-permute-start | bytes 196616 | tf_op jit(solution)/shard_map/ppermute | solution.py:478
  25.4 5.0 %collective-permute-start.7 = (f32[128,128]{1,0:T(8,128)S(1)}, f32[128,128]{1,0:T(8,128)S(1)}, u32[]{:S(2)}, u32[]{:S(2)}) collective-permute-start(f32[128,128]{1,0:T(8,128)S(1)} %get-tuple-element.185), channel_id=1, source_target_pairs={{3,0},{2,1},{1,2},{0,3},{7,4},{6,5},{5,6},{4,7},{11,8},{10,9},{9,1... | collective-permute-start | bytes 196616 | tf_op jit(solution)/shard_map/ppermute | solution.py:478
  26.7 4.9 %collective-permute-start.8 = (f32[128,128]{1,0:T(8,128)S(1)}, f32[128,128]{1,0:T(8,128)S(1)}, u32[]{:S(2)}, u32[]{:S(2)}) collective-permute-start(f32[128,128]{1,0:T(8,128)S(1)} %get-tuple-element.186), channel_id=1, source_target_pairs={{7,0},{6,1},{5,2},{4,3},{3,4},{2,5},{1,6},{0,7},{15,8},{14,9},{13,... | collective-permute-start | bytes 196616 | tf_op jit(solution)/shard_map/ppermute | solution.py:478
  31.7 1.6 %collective-permute-start.9 = (f32[512,128]{1,0:T(8,128)S(1)}, f32[512,128]{1,0:T(8,128)S(1)}, u32[]{:S(2)}, u32[]{:S(2)}) collective-permute-start(f32[512,128]{1,0:T(8,128)S(1)} %get-tuple-element.190), channel_id=1, source_target_pairs={{1,0},{0,1},{3,2},{2,3},{5,4},{4,5},{7,6},{6,7},{9,8},{8,9},{11,10... | collective-permute-start | bytes 786440 | tf_op jit(solution)/shard_map/ppermute | solution.py:478
  34.0 3.9 %collective-permute-start.12 = (f32[2,512]{1,0:T(2,128)S(1)}, f32[2,512]{1,0:T(2,128)S(1)}, u32[]{:S(2)}, u32[]{:S(2)}) collective-permute-start(f32[2,512]{1,0:T(2,128)S(1)} %get-tuple-element.206.refs_5_), channel_id=1, source_target_pairs={{0,96},{32,64},{64,32},{96,0},{1,97},{33,65},{65,33},{97,1},{2,98}... | collective-permute-start | bytes 12296 | tf_op jit(solution)/shard_map/ppermute | solution.py:618
  36.6 2.5 %collective-permute-start.11 = (f32[2,512]{1,0:T(2,128)S(1)}, f32[2,512]{1,0:T(2,128)S(1)}, u32[]{:S(2)}, u32[]{:S(2)}) collective-permute-start(f32[2,512]{1,0:T(2,128)S(1)} %get-tuple-element.206.refs_5_), channel_id=1, source_target_pairs={{0,32},{32,0},{64,96},{96,64},{1,33},{33,1},{65,97},{97,65},{2,34}... | collective-permute-start | bytes 12296 | tf_op jit(solution)/shard_map/ppermute | solution.py:618
  36.6 4.0 %collective-permute-start.10 = (f32[2,512]{1,0:T(2,128)S(1)}, f32[2,512]{1,0:T(2,128)S(1)}, u32[]{:S(2)}, u32[]{:S(2)}) collective-permute-start(f32[2,512]{1,0:T(2,128)S(1)} %get-tuple-element.206.refs_5_), channel_id=1, source_target_pairs={{0,64},{32,96},{64,0},{96,32},{1,65},{33,97},{65,1},{97,33},{2,66}... | collective-permute-start | bytes 12296 | tf_op jit(solution)/shard_map/ppermute | solution.py:618
  41.3 3.0 %collective-permute-start.13 = (f32[512,128]{1,0:T(8,128)S(1)}, f32[512,128]{1,0:T(8,128)S(1)}, u32[]{:S(2)}, u32[]{:S(2)}) collective-permute-start(f32[512,128]{1,0:T(8,128)S(1)} %get-tuple-element.207), channel_id=1, source_target_pairs={{1,0},{0,1},{3,2},{2,3},{5,4},{4,5},{7,6},{6,7},{9,8},{8,9},{11,10... | collective-permute-start | bytes 786440 | tf_op jit(solution)/shard_map/ppermute | solution.py:478
  44.4 6.7 %collective-permute-start.14 = (f32[128,128]{1,0:T(8,128)S(1)}, f32[128,128]{1,0:T(8,128)S(1)}, u32[]{:S(2)}, u32[]{:S(2)}) collective-permute-start(f32[128,128]{1,0:T(8,128)S(1)} %get-tuple-element.222), channel_id=1, source_target_pairs={{4,0},{5,1},{6,2},{7,3},{0,4},{1,5},{2,6},{3,7},{12,8},{13,9},{14,... | collective-permute-start | bytes 196616 | tf_op jit(solution)/shard_map/ppermute | solution.py:478
  45.5 5.6 %collective-permute-start.15 = (f32[128,128]{1,0:T(8,128)S(1)}, f32[128,128]{1,0:T(8,128)S(1)}, u32[]{:S(2)}, u32[]{:S(2)}) collective-permute-start(f32[128,128]{1,0:T(8,128)S(1)} %get-tuple-element.223), channel_id=1, source_target_pairs={{3,0},{2,1},{1,2},{0,3},{7,4},{6,5},{5,6},{4,7},{11,8},{10,9},{9,1... | collective-permute-start | bytes 196616 | tf_op jit(solution)/shard_map/ppermute | solution.py:478
  46.7 5.0 %collective-permute-start.16 = (f32[128,128]{1,0:T(8,128)S(1)}, f32[128,128]{1,0:T(8,128)S(1)}, u32[]{:S(2)}, u32[]{:S(2)}) collective-permute-start(f32[128,128]{1,0:T(8,128)S(1)} %get-tuple-element.224), channel_id=1, source_target_pairs={{7,0},{6,1},{5,2},{4,3},{3,4},{2,5},{1,6},{0,7},{15,8},{14,9},{13,... | collective-permute-start | bytes 196616 | tf_op jit(solution)/shard_map/ppermute | solution.py:478
  51.8 5.9 %collective-permute-start.18 = (f32[128,128]{1,0:T(8,128)S(1)}, f32[128,128]{1,0:T(8,128)S(1)}, u32[]{:S(2)}, u32[]{:S(2)}) collective-permute-start(f32[128,128]{1,0:T(8,128)S(1)} %get-tuple-element.246), channel_id=1, source_target_pairs={{16,0},{17,1},{18,2},{19,3},{20,4},{21,5},{22,6},{23,7},{24,8},{25... | collective-permute-start | bytes 196616 | tf_op jit(solution)/shard_map/ppermute | solution.py:478
  52.6 5.0 %collective-permute-start.17 = (f32[128,128]{1,0:T(8,128)S(1)}, f32[128,128]{1,0:T(8,128)S(1)}, u32[]{:S(2)}, u32[]{:S(2)}) collective-permute-start(f32[128,128]{1,0:T(8,128)S(1)} %get-tuple-element.246), channel_id=1, source_target_pairs={{9,0},{8,1},{11,2},{10,3},{13,4},{12,5},{15,6},{14,7},{17,8},{16,9... | collective-permute-start | bytes 196616 | tf_op jit(solution)/shard_map/ppermute | solution.py:478
  57.7 6.4 %collective-permute-start.19 = (f32[128,128]{1,0:T(8,128)S(1)}, f32[128,128]{1,0:T(8,128)S(1)}, u32[]{:S(2)}, u32[]{:S(2)}) collective-permute-start(f32[128,128]{1,0:T(8,128)S(1)} %get-tuple-element.266), channel_id=1, source_target_pairs={{4,0},{5,1},{6,2},{7,3},{0,4},{1,5},{2,6},{3,7},{12,8},{13,9},{14,... | collective-permute-start | bytes 196616 | tf_op jit(solution)/shard_map/ppermute | solution.py:478
  58.5 5.6 %collective-permute-start.20 = (f32[128,128]{1,0:T(8,128)S(1)}, f32[128,128]{1,0:T(8,128)S(1)}, u32[]{:S(2)}, u32[]{:S(2)}) collective-permute-start(f32[128,128]{1,0:T(8,128)S(1)} %get-tuple-element.267), channel_id=1, source_target_pairs={{3,0},{2,1},{1,2},{0,3},{7,4},{6,5},{5,6},{4,7},{11,8},{10,9},{9,1... | collective-permute-start | bytes 196616 | tf_op jit(solution)/shard_map/ppermute | solution.py:478
  60.2 5.0 %collective-permute-start.21 = (f32[128,128]{1,0:T(8,128)S(1)}, f32[128,128]{1,0:T(8,128)S(1)}, u32[]{:S(2)}, u32[]{:S(2)}) collective-permute-start(f32[128,128]{1,0:T(8,128)S(1)} %get-tuple-element.268), channel_id=1, source_target_pairs={{7,0},{6,1},{5,2},{4,3},{3,4},{2,5},{1,6},{0,7},{15,8},{14,9},{13,... | collective-permute-start | bytes 196616 | tf_op jit(solution)/shard_map/ppermute | solution.py:478
  65.3 1.6 %collective-permute-start.22 = (f32[512,128]{1,0:T(8,128)S(1)}, f32[512,128]{1,0:T(8,128)S(1)}, u32[]{:S(2)}, u32[]{:S(2)}) collective-permute-start(f32[512,128]{1,0:T(8,128)S(1)} %get-tuple-element.284), channel_id=1, source_target_pairs={{1,0},{0,1},{3,2},{2,3},{5,4},{4,5},{7,6},{6,7},{9,8},{8,9},{11,10... | collective-permute-start | bytes 786440 | tf_op jit(solution)/shard_map/ppermute | solution.py:478
  (3 other events, 6.5 us)

commit v6 on v5

--- a/solution.py
+++ b/solution.py
@@ -345,12 +345,17 @@
         upper_ref[rows_of(k), :] = dot(query_ref[:, cols] * mask, grad_mixed, TN)
 
 
-def normed_kernel(own_ref, other_ref, inverse_ref, gain_ref, out_ref):
+def normed_kernel(mixed_ref, inverse_ref, gain_ref, *refs, own):
+    out_ref, buf, sems = refs[1 if own else 0 :]
     inverse = inverse_ref[...]
-    for own, mixed_ref in ((True, own_ref), (False, other_ref)):
-        for k in range(COLUMNS):
-            cols = column(k, own)
-            out_ref[:, cols] = (mixed_ref[:, head(k)] * inverse * gain_ref[:, cols]).astype(BF16)
+    copies = []
+    for k in range(COLUMNS):
+        cols = column(k, own)
+        buf[:, head(k)] = (mixed_ref[:, head(k)] * inverse * gain_ref[:, cols]).astype(BF16)
+        copies.append(pltpu.make_async_copy(buf.at[:, head(k)], out_ref.at[:, cols], sems.at[k]))
+        copies[-1].start()
+    for copy in copies:
+        copy.wait()
 
 
 def back_kernel(
@@ -629,10 +634,25 @@
     made = {}
     query_parts, pieces = [], []
 
+    def normed(own, args):
+        return call(
+            normed_kernel,
+            "normed",
+            args,
+            [wide_bf16],
+            wide_f32.size,
+            [pltpu.VMEM((rows_here, COLUMNS * HEAD_DIM), BF16), pltpu.SemaphoreType.DMA((COLUMNS,))],
+            ins=[vmem] * 3 + [hbm] * len(args[3:]),
+            outs=[hbm],
+            alias={3: 0} if own else {},
+            own=own,
+        )
+
     def own_grad(args):
         grad_own, own = call(grad_kernel, "own_grad", args, [side_bf16, half], 4 * product, own=True)
         made[True] = grad_own
-        return [own, grad_own]
+        made[False] = normed(False, (mixed_other, inverse, gain))[0]
+        return [own, grad_own, made[False]]
 
     def back(own, g, args):
         first = g * BACK_HEADS
@@ -655,9 +675,9 @@
     def first_back():
         def run(args):
             done = back(True, 0, args[:7])
-            return [*done, *call(normed_kernel, "normed", args[7:], [wide_bf16], 2 * wide_f32.size)]
-
-        whole = (mixed_own, mixed_other, inverse, gain)
+            return [*done, *normed(True, args[7:])]
+
+        whole = (mixed_own, inverse, gain, made[False])
         return (*back_args, made[True], states_own, *whole), run
 
     def second_back():

time: 68.7 us -> 69.2 us (level)
    pallas_call x25 -> x26, Pallas kernels: 20.6 us -> 21.2 us  [call(): pl.pallas_call(lambda *refs: body(*refs, **fixed), name=name, in_specs=in...]
  transfers between devices with their start and end apart: 23 -> 23, of which waited for: 14 -> 13; matrix products, arithmetic and copies ran while one was open for 0% -> 0% of each run, Pallas kernels for 22% -> 23%
where the time goes in v6:
time: 69.2 us; the launch traced here: 69.1 us
  starting transfers between devices  30 us (43%)
  Pallas kernels  21.2 us (31%)
  waiting for transfers between devices  15.5 us (22%)
  local copies, waits for them, and re-layouts  1.24 us (2%)
  between operations  1.11 us (2%)
    ppermute x20, starting transfers between devices, move(): return lax.ppermute(values, 'ctx', [(source(i), i) for i in range(devices)])  26.1 us
    pallas_call x26, Pallas kernels, call(): pl.pallas_call(lambda *refs: body(*refs, **fixed), name=name, in_specs=in...  21.2 us
    ppermute x20, waiting for transfers between devices, move(): return lax.ppermute(values, 'ctx', [(source(i), i) for i in range(devices)])  12.9 us
    ppermute x3, starting transfers between devices, on_device(): lax.ppermute(sums, 'head', [(i, i ^ flip) for i in range(lax.axis_size('h...  3.94 us
    ppermute x3, waiting for transfers between devices, on_device(): lax.ppermute(sums, 'head', [(i, i ^ flip) for i in range(lax.axis_size('h...  2.58 us
  transfers between devices with their start and end apart: 23, of which 13 were waited for; matrix products, arithmetic and copies ran while one was open for 0% of the time, Pallas kernels for 23%

profile of v6, /device:TPU:1, one launch (start us, length us, event | category | flops | bytes accessed | tf_op | source)
XLA Modules:
  0.0 69.1 jit_solution(1321381000718891643)
XLA Ops:
  1.3 1.8 %states.1 = (f32[512,128]{1,0:T(8,128)S(1)}, f32[40,128]{1,0:T(8,128)S(1)}, bf16[512,1024]{1,0:T(8,128)(2,1)S(1)}, bf16[512,1024]{1,0:T(8,128)(2,1)S(1)}) custom-call(s32[8]{0:T(128)S(1)} %copy-done.3, bf16[512,1024]{1,0:T(8,128)(2,1)} %refs_1_.3, bf16[512,1024]{1,0:T(8,128)(2,1)} %refs_2_.2), custom_call_target="tpu_custom_call" | custom-call | flops 67108864 | bytes 4476960 | tf_op jit(solution)/shard_map/states/pallas_call | solution.py:468
  3.1 1.5 %collective-permute-start = (f32[512,128]{1,0:T(8,128)S(1)}, f32[512,128]{1,0:T(8,128)S(1)}, u32[]{:S(2)}, u32[]{:S(2)}) collective-permute-start(f32[512,128]{1,0:T(8,128)S(1)} %get-tuple-element.155), channel_id=1, source_target_pairs={{1,0},{0,1},{3,2},{2,3},{5,4},{4,5},{7,6},{6,7},{9,8},{8,9},{11,10... | collective-permute-start | bytes 786440 | tf_op jit(solution)/shard_map/ppermute | solution.py:483
  5.8 3.1 %collective-permute-start.1 = (f32[128,128]{1,0:T(8,128)S(1)}, f32[128,128]{1,0:T(8,128)S(1)}, u32[]{:S(2)}, u32[]{:S(2)}) collective-permute-start(f32[128,128]{1,0:T(8,128)S(1)} %get-tuple-element.164), channel_id=1, source_target_pairs={{4,0},{5,1},{6,2},{7,3},{0,4},{1,5},{2,6},{3,7},{12,8},{13,9},{14,... | collective-permute-start | bytes 196616 | tf_op jit(solution)/shard_map/ppermute | solution.py:483
  10.3 1.5 %local_mix.2.refs_2_ = f32[512,512]{1,0:T(8,128)S(1)} custom-call(bf16[512,1024]{1,0:T(8,128)(2,1)S(1)} %copy-done, bf16[512,1024]{1,0:T(8,128)(2,1)S(1)} %get-tuple-element.287.refs_1_.refs_2_, bf16[512,1024]{1,0:T(8,128)(2,1)S(1)} %get-tuple-element.288.refs_2_.refs_3_, bf16[512,512]{1,0:T(8,128)(2,1)S(1)} %pair_mask.1.refs_3_.refs_4_), custom_call_target="tpu_custom_call" | custom-call | flops 402653184 | bytes 4718592 | tf_op jit(solution)/shard_map/local_mix/pallas_call | solution.py:468
  11.8 1.8 %collective-permute-done.2.refs_3_ = f32[128,128]{1,0:T(8,128)S(1)} collective-permute-done((f32[128,128]{1,0:T(8,128)S(1)}, f32[128,128]{1,0:T(8,128)S(1)}, u32[]{:S(2)}, u32[]{:S(2)}) %collective-permute-start.2) | collective-permute-done | bytes 65568 | tf_op jit(solution)/shard_map/ppermute | solution.py:483
  14.8 3.7 %collective-permute-start.5 = (f32[128,128]{1,0:T(8,128)S(1)}, f32[128,128]{1,0:T(8,128)S(1)}, u32[]{:S(2)}, u32[]{:S(2)}) collective-permute-start(f32[128,128]{1,0:T(8,128)S(1)} %get-tuple-element.174), channel_id=1, source_target_pairs={{16,0},{17,1},{18,2},{19,3},{20,4},{21,5},{22,6},{23,7},{24,8},{25... | collective-permute-start | bytes 196616 | tf_op jit(solution)/shard_map/ppermute | solution.py:483
  19.2 1.4 %local_mix.3.refs_2_ = f32[512,512]{1,0:T(8,128)S(1)} custom-call(bf16[512,1024]{1,0:T(8,128)(2,1)S(1)} %copy-done, bf16[512,1024]{1,0:T(8,128)(2,1)S(1)} %get-tuple-element.287.refs_1_.refs_2_, bf16[512,1024]{1,0:T(8,128)(2,1)S(1)} %get-tuple-element.288.refs_2_.refs_3_, bf16[512,512]{1,0:T(8,128)(2,1)S(1)} %pair_mask.1.refs_3_.refs_4_), custom_call_target="tpu_custom_call" | custom-call | flops 402653184 | bytes 4718592 | tf_op jit(solution)/shard_map/local_mix/pallas_call | solution.py:468
  21.1 2.4 %collective-permute-done.4.refs_2_ = f32[128,128]{1,0:T(8,128)S(1)} collective-permute-done((f32[128,128]{1,0:T(8,128)S(1)}, f32[128,128]{1,0:T(8,128)S(1)}, u32[]{:S(2)}, u32[]{:S(2)}) %collective-permute-start.4) | collective-permute-done | bytes 65568 | tf_op jit(solution)/shard_map/ppermute | solution.py:483
  23.6 1.8 %collective-permute-start.6 = (f32[128,128]{1,0:T(8,128)S(1)}, f32[128,128]{1,0:T(8,128)S(1)}, u32[]{:S(2)}, u32[]{:S(2)}) collective-permute-start(f32[128,128]{1,0:T(8,128)S(1)} %get-tuple-element.184), channel_id=1, source_target_pairs={{4,0},{5,1},{6,2},{7,3},{0,4},{1,5},{2,6},{3,7},{12,8},{13,9},{14,... | collective-permute-start | bytes 196616 | tf_op jit(solution)/shard_map/ppermute | solution.py:483
  27.2 1.5 %collective-permute-done.6.refs_4_ = f32[128,128]{1,0:T(8,128)S(1)} collective-permute-done((f32[128,128]{1,0:T(8,128)S(1)}, f32[128,128]{1,0:T(8,128)S(1)}, u32[]{:S(2)}, u32[]{:S(2)}) %collective-permute-start.6) | collective-permute-done | bytes 65568 | tf_op jit(solution)/shard_map/ppermute | solution.py:483
  28.7 1.7 %collective-permute-done.7.refs_5_ = f32[128,128]{1,0:T(8,128)S(1)} collective-permute-done((f32[128,128]{1,0:T(8,128)S(1)}, f32[128,128]{1,0:T(8,128)S(1)}, u32[]{:S(2)}, u32[]{:S(2)}) %collective-permute-start.7) | collective-permute-done | bytes 65568 | tf_op jit(solution)/shard_map/ppermute | solution.py:483
  34.0 2.6 %collective-permute-start.12 = (f32[2,512]{1,0:T(2,128)S(1)}, f32[2,512]{1,0:T(2,128)S(1)}, u32[]{:S(2)}, u32[]{:S(2)}) collective-permute-start(f32[2,512]{1,0:T(2,128)S(1)} %get-tuple-element.206.refs_5_), channel_id=1, source_target_pairs={{0,96},{32,64},{64,32},{96,0},{1,97},{33,65},{65,33},{97,1},{2,98}... | collective-permute-start | bytes 12296 | tf_op jit(solution)/shard_map/ppermute | solution.py:623
  39.0 1.5 %collective-permute-done.10.refs_6_ = f32[2,512]{1,0:T(2,128)S(1)} collective-permute-done((f32[2,512]{1,0:T(2,128)S(1)}, f32[2,512]{1,0:T(2,128)S(1)}, u32[]{:S(2)}, u32[]{:S(2)}) %collective-permute-start.10) | collective-permute-done | bytes 4128 | tf_op jit(solution)/shard_map/ppermute | solution.py:623
  41.3 1.9 %collective-permute-start.13 = (f32[512,128]{1,0:T(8,128)S(1)}, f32[512,128]{1,0:T(8,128)S(1)}, u32[]{:S(2)}, u32[]{:S(2)}) collective-permute-start(f32[512,128]{1,0:T(8,128)S(1)} %get-tuple-element.207), channel_id=1, source_target_pairs={{1,0},{0,1},{3,2},{2,3},{5,4},{4,5},{7,6},{6,7},{9,8},{8,9},{11,10... | collective-permute-start | bytes 786440 | tf_op jit(solution)/shard_map/ppermute | solution.py:483
  46.8 1.7 %collective-permute-start.16 = (f32[128,128]{1,0:T(8,128)S(1)}, f32[128,128]{1,0:T(8,128)S(1)}, u32[]{:S(2)}, u32[]{:S(2)}) collective-permute-start(f32[128,128]{1,0:T(8,128)S(1)} %get-tuple-element.224), channel_id=1, source_target_pairs={{7,0},{6,1},{5,2},{4,3},{3,4},{2,5},{1,6},{0,7},{15,8},{14,9},{13,... | collective-permute-start | bytes 196616 | tf_op jit(solution)/shard_map/ppermute | solution.py:483
  49.4 1.8 %local_back.4 = (bf16[512,256]{1,0:T(8,128)(2,1)S(1)}, f32[512,256]{1,0:T(8,128)S(1)}, f32[512,256]{1,0:T(8,128)S(1)}) custom-call(f32[40,128]{1,0:T(8,128)S(1)} %get-tuple-element.286.refs_0_, bf16[512,1024]{1,0:T(8,128)(2,1)S(1)} %copy-done, bf16[512,1024]{1,0:T(8,128)(2,1)S(1)} %get-tuple-element.287.refs_1_.refs_2_, ...), custom_call_target="tpu_custom_call" | custom-call | flops 570425344 | bytes 5787648 | tf_op jit(solution)/shard_map/local_back/pallas_call | solution.py:468
  52.9 1.9 %collective-permute-start.17 = (f32[128,128]{1,0:T(8,128)S(1)}, f32[128,128]{1,0:T(8,128)S(1)}, u32[]{:S(2)}, u32[]{:S(2)}) collective-permute-start(f32[128,128]{1,0:T(8,128)S(1)} %get-tuple-element.246), channel_id=1, source_target_pairs={{9,0},{8,1},{11,2},{10,3},{13,4},{12,5},{15,6},{14,7},{17,8},{16,9... | collective-permute-start | bytes 196616 | tf_op jit(solution)/shard_map/ppermute | solution.py:483
  54.8 1.8 %local_back.5 = (bf16[512,256]{1,0:T(8,128)(2,1)S(1)}, f32[512,256]{1,0:T(8,128)S(1)}, f32[512,256]{1,0:T(8,128)S(1)}) custom-call(f32[40,128]{1,0:T(8,128)S(1)} %get-tuple-element.286.refs_0_, bf16[512,1024]{1,0:T(8,128)(2,1)S(1)} %copy-done, bf16[512,1024]{1,0:T(8,128)(2,1)S(1)} %get-tuple-element.287.refs_1_.refs_2_, ...), custom_call_target="tpu_custom_call" | custom-call | flops 570425344 | bytes 5787648 | tf_op jit(solution)/shard_map/local_back/pallas_call | solution.py:468
  56.6 1.8 %local_back.6 = (bf16[512,256]{1,0:T(8,128)(2,1)S(1)}, f32[512,256]{1,0:T(8,128)S(1)}, f32[512,256]{1,0:T(8,128)S(1)}) custom-call(f32[40,128]{1,0:T(8,128)S(1)} %get-tuple-element.286.refs_0_, bf16[512,1024]{1,0:T(8,128)(2,1)S(1)} %copy-done, bf16[512,1024]{1,0:T(8,128)(2,1)S(1)} %get-tuple-element.287.refs_1_.refs_2_, ...), custom_call_target="tpu_custom_call" | custom-call | flops 570425344 | bytes 5787648 | tf_op jit(solution)/shard_map/local_back/pallas_call | solution.py:468
  59.1 1.6 %collective-permute-start.20 = (f32[128,128]{1,0:T(8,128)S(1)}, f32[128,128]{1,0:T(8,128)S(1)}, u32[]{:S(2)}, u32[]{:S(2)}) collective-permute-start(f32[128,128]{1,0:T(8,128)S(1)} %get-tuple-element.267), channel_id=1, source_target_pairs={{3,0},{2,1},{1,2},{0,3},{7,4},{6,5},{5,6},{4,7},{11,8},{10,9},{9,1... | collective-permute-start | bytes 196616 | tf_op jit(solution)/shard_map/ppermute | solution.py:483
  60.6 1.4 %collective-permute-start.21 = (f32[128,128]{1,0:T(8,128)S(1)}, f32[128,128]{1,0:T(8,128)S(1)}, u32[]{:S(2)}, u32[]{:S(2)}) collective-permute-start(f32[128,128]{1,0:T(8,128)S(1)} %get-tuple-element.268), channel_id=1, source_target_pairs={{7,0},{6,1},{5,2},{4,3},{3,4},{2,5},{1,6},{0,7},{15,8},{14,9},{13,... | collective-permute-start | bytes 196616 | tf_op jit(solution)/shard_map/ppermute | solution.py:483
  62.0 1.8 %local_back.7 = (bf16[512,256]{1,0:T(8,128)(2,1)S(1)}, f32[512,256]{1,0:T(8,128)S(1)}, f32[512,256]{1,0:T(8,128)S(1)}) custom-call(f32[40,128]{1,0:T(8,128)S(1)} %get-tuple-element.286.refs_0_, bf16[512,1024]{1,0:T(8,128)(2,1)S(1)} %copy-done, bf16[512,1024]{1,0:T(8,128)(2,1)S(1)} %get-tuple-element.287.refs_1_.refs_2_, ...), custom_call_target="tpu_custom_call" | custom-call | flops 570425344 | bytes 5787648 | tf_op jit(solution)/shard_map/local_back/pallas_call | solution.py:468
  65.9 1.5 %own_final.1 = (bf16[512,1024]{1,0:T(8,128)(2,1)}, bf16[512,1024]{1,0:T(8,128)(2,1)}) custom-call(f32[40,128]{1,0:T(8,128)S(1)} %get-tuple-element.286.refs_0_, bf16[512,1024]{1,0:T(8,128)(2,1)S(1)} %get-tuple-element.287.refs_1_.refs_2_, bf16[512,1024]{1,0:T(8,128)(2,1)S(1)} %get-tuple-element.288.refs_2_.refs_3_, ...), custom_call_target="tpu_custom_call" | custom-call | flops 268435456 | bytes 6574080 | tf_op jit(solution)/shard_map/own_final/pallas_call | solution.py:468
  67.4 1.5 %back_states.1 = (bf16[512,1024]{1,0:T(8,128)(2,1)}, bf16[512,1024]{1,0:T(8,128)(2,1)}) custom-call(f32[40,128]{1,0:T(8,128)S(1)} %get-tuple-element.286.refs_0_, bf16[512,1024]{1,0:T(8,128)(2,1)S(1)} %get-tuple-element.287.refs_1_.refs_2_, bf16[512,1024]{1,0:T(8,128)(2,1)S(1)} %get-tuple-element.288.refs_2_.refs_3_, ...), custom_call_target="tpu_custom_call", output_to_operand_aliasing={{0}: (8, {}), {1}: (9, {})} | custom-call | flops 268435456 | bytes 8671232 | tf_op jit(solution)/shard_map/back_states/pallas_call | solution.py:468
  (56 shorter events, 23.2 us)
Async XLA Ops:
  3.1 2.7 %collective-permute-start = (f32[512,128]{1,0:T(8,128)S(1)}, f32[512,128]{1,0:T(8,128)S(1)}, u32[]{:S(2)}, u32[]{:S(2)}) collective-permute-start(f32[512,128]{1,0:T(8,128)S(1)} %get-tuple-element.155), channel_id=1, source_target_pairs={{1,0},{0,1},{3,2},{2,3},{5,4},{4,5},{7,6},{6,7},{9,8},{8,9},{11,10... | collective-permute-start | bytes 786440 | tf_op jit(solution)/shard_map/ppermute | solution.py:483
  5.8 5.9 %collective-permute-start.1 = (f32[128,128]{1,0:T(8,128)S(1)}, f32[128,128]{1,0:T(8,128)S(1)}, u32[]{:S(2)}, u32[]{:S(2)}) collective-permute-start(f32[128,128]{1,0:T(8,128)S(1)} %get-tuple-element.164), channel_id=1, source_target_pairs={{4,0},{5,1},{6,2},{7,3},{0,4},{1,5},{2,6},{3,7},{12,8},{13,9},{14,... | collective-permute-start | bytes 196616 | tf_op jit(solution)/shard_map/ppermute | solution.py:483
  8.9 4.7 %collective-permute-start.2 = (f32[128,128]{1,0:T(8,128)S(1)}, f32[128,128]{1,0:T(8,128)S(1)}, u32[]{:S(2)}, u32[]{:S(2)}) collective-permute-start(f32[128,128]{1,0:T(8,128)S(1)} %get-tuple-element.165), channel_id=1, source_target_pairs={{3,0},{2,1},{1,2},{0,3},{7,4},{6,5},{5,6},{4,7},{11,8},{10,9},{9,1... | collective-permute-start | bytes 196616 | tf_op jit(solution)/shard_map/ppermute | solution.py:483
  9.8 4.9 %collective-permute-start.3 = (f32[128,128]{1,0:T(8,128)S(1)}, f32[128,128]{1,0:T(8,128)S(1)}, u32[]{:S(2)}, u32[]{:S(2)}) collective-permute-start(f32[128,128]{1,0:T(8,128)S(1)} %get-tuple-element.166), channel_id=1, source_target_pairs={{7,0},{6,1},{5,2},{4,3},{3,4},{2,5},{1,6},{0,7},{15,8},{14,9},{13,... | collective-permute-start | bytes 196616 | tf_op jit(solution)/shard_map/ppermute | solution.py:483
  14.8 6.3 %collective-permute-start.5 = (f32[128,128]{1,0:T(8,128)S(1)}, f32[128,128]{1,0:T(8,128)S(1)}, u32[]{:S(2)}, u32[]{:S(2)}) collective-permute-start(f32[128,128]{1,0:T(8,128)S(1)} %get-tuple-element.174), channel_id=1, source_target_pairs={{16,0},{17,1},{18,2},{19,3},{20,4},{21,5},{22,6},{23,7},{24,8},{25... | collective-permute-start | bytes 196616 | tf_op jit(solution)/shard_map/ppermute | solution.py:483
  18.5 5.1 %collective-permute-start.4 = (f32[128,128]{1,0:T(8,128)S(1)}, f32[128,128]{1,0:T(8,128)S(1)}, u32[]{:S(2)}, u32[]{:S(2)}) collective-permute-start(f32[128,128]{1,0:T(8,128)S(1)} %get-tuple-element.174), channel_id=1, source_target_pairs={{25,0},{24,1},{27,2},{26,3},{29,4},{28,5},{31,6},{30,7},{1,8},{0,9... | collective-permute-start | bytes 196616 | tf_op jit(solution)/shard_map/ppermute | solution.py:483
  20.7 11.1 %copy-start.1 = (bf16[512,1024]{1,0:T(8,128)(2,1)S(1)}, bf16[512,1024]{1,0:T(8,128)(2,1)}, u32[]{:S(2)}) copy-start(bf16[512,1024]{1,0:T(8,128)(2,1)} %refs_2_.4) | copy-start | bytes 3145732
  23.6 5.1 %collective-permute-start.6 = (f32[128,128]{1,0:T(8,128)S(1)}, f32[128,128]{1,0:T(8,128)S(1)}, u32[]{:S(2)}, u32[]{:S(2)}) collective-permute-start(f32[128,128]{1,0:T(8,128)S(1)} %get-tuple-element.184), channel_id=1, source_target_pairs={{4,0},{5,1},{6,2},{7,3},{0,4},{1,5},{2,6},{3,7},{12,8},{13,9},{14,... | collective-permute-start | bytes 196616 | tf_op jit(solution)/shard_map/ppermute | solution.py:483
  25.4 5.0 %collective-permute-start.7 = (f32[128,128]{1,0:T(8,128)S(1)}, f32[128,128]{1,0:T(8,128)S(1)}, u32[]{:S(2)}, u32[]{:S(2)}) collective-permute-start(f32[128,128]{1,0:T(8,128)S(1)} %get-tuple-element.185), channel_id=1, source_target_pairs={{3,0},{2,1},{1,2},{0,3},{7,4},{6,5},{5,6},{4,7},{11,8},{10,9},{9,1... | collective-permute-start | bytes 196616 | tf_op jit(solution)/shard_map/ppermute | solution.py:483
  26.7 4.9 %collective-permute-start.8 = (f32[128,128]{1,0:T(8,128)S(1)}, f32[128,128]{1,0:T(8,128)S(1)}, u32[]{:S(2)}, u32[]{:S(2)}) collective-permute-start(f32[128,128]{1,0:T(8,128)S(1)} %get-tuple-element.186), channel_id=1, source_target_pairs={{7,0},{6,1},{5,2},{4,3},{3,4},{2,5},{1,6},{0,7},{15,8},{14,9},{13,... | collective-permute-start | bytes 196616 | tf_op jit(solution)/shard_map/ppermute | solution.py:483
  31.7 1.6 %collective-permute-start.9 = (f32[512,128]{1,0:T(8,128)S(1)}, f32[512,128]{1,0:T(8,128)S(1)}, u32[]{:S(2)}, u32[]{:S(2)}) collective-permute-start(f32[512,128]{1,0:T(8,128)S(1)} %get-tuple-element.190), channel_id=1, source_target_pairs={{1,0},{0,1},{3,2},{2,3},{5,4},{4,5},{7,6},{6,7},{9,8},{8,9},{11,10... | collective-permute-start | bytes 786440 | tf_op jit(solution)/shard_map/ppermute | solution.py:483
  34.0 3.9 %collective-permute-start.12 = (f32[2,512]{1,0:T(2,128)S(1)}, f32[2,512]{1,0:T(2,128)S(1)}, u32[]{:S(2)}, u32[]{:S(2)}) collective-permute-start(f32[2,512]{1,0:T(2,128)S(1)} %get-tuple-element.206.refs_5_), channel_id=1, source_target_pairs={{0,96},{32,64},{64,32},{96,0},{1,97},{33,65},{65,33},{97,1},{2,98}... | collective-permute-start | bytes 12296 | tf_op jit(solution)/shard_map/ppermute | solution.py:623
  36.6 2.5 %collective-permute-start.11 = (f32[2,512]{1,0:T(2,128)S(1)}, f32[2,512]{1,0:T(2,128)S(1)}, u32[]{:S(2)}, u32[]{:S(2)}) collective-permute-start(f32[2,512]{1,0:T(2,128)S(1)} %get-tuple-element.206.refs_5_), channel_id=1, source_target_pairs={{0,32},{32,0},{64,96},{96,64},{1,33},{33,1},{65,97},{97,65},{2,34}... | collective-permute-start | bytes 12296 | tf_op jit(solution)/shard_map/ppermute | solution.py:623
  36.6 4.0 %collective-permute-start.10 = (f32[2,512]{1,0:T(2,128)S(1)}, f32[2,512]{1,0:T(2,128)S(1)}, u32[]{:S(2)}, u32[]{:S(2)}) collective-permute-start(f32[2,512]{1,0:T(2,128)S(1)} %get-tuple-element.206.refs_5_), channel_id=1, source_target_pairs={{0,64},{32,96},{64,0},{96,32},{1,65},{33,97},{65,1},{97,33},{2,66}... | collective-permute-start | bytes 12296 | tf_op jit(solution)/shard_map/ppermute | solution.py:623
  41.3 3.5 %collective-permute-start.13 = (f32[512,128]{1,0:T(8,128)S(1)}, f32[512,128]{1,0:T(8,128)S(1)}, u32[]{:S(2)}, u32[]{:S(2)}) collective-permute-start(f32[512,128]{1,0:T(8,128)S(1)} %get-tuple-element.207), channel_id=1, source_target_pairs={{1,0},{0,1},{3,2},{2,3},{5,4},{4,5},{7,6},{6,7},{9,8},{8,9},{11,10... | collective-permute-start | bytes 786440 | tf_op jit(solution)/shard_map/ppermute | solution.py:483
  44.9 6.3 %collective-permute-start.14 = (f32[128,128]{1,0:T(8,128)S(1)}, f32[128,128]{1,0:T(8,128)S(1)}, u32[]{:S(2)}, u32[]{:S(2)}) collective-permute-start(f32[128,128]{1,0:T(8,128)S(1)} %get-tuple-element.222), channel_id=1, source_target_pairs={{4,0},{5,1},{6,2},{7,3},{0,4},{1,5},{2,6},{3,7},{12,8},{13,9},{14,... | collective-permute-start | bytes 196616 | tf_op jit(solution)/shard_map/ppermute | solution.py:483
  46.0 5.2 %collective-permute-start.15 = (f32[128,128]{1,0:T(8,128)S(1)}, f32[128,128]{1,0:T(8,128)S(1)}, u32[]{:S(2)}, u32[]{:S(2)}) collective-permute-start(f32[128,128]{1,0:T(8,128)S(1)} %get-tuple-element.223), channel_id=1, source_target_pairs={{3,0},{2,1},{1,2},{0,3},{7,4},{6,5},{5,6},{4,7},{11,8},{10,9},{9,1... | collective-permute-start | bytes 196616 | tf_op jit(solution)/shard_map/ppermute | solution.py:483
  46.8 5.2 %collective-permute-start.16 = (f32[128,128]{1,0:T(8,128)S(1)}, f32[128,128]{1,0:T(8,128)S(1)}, u32[]{:S(2)}, u32[]{:S(2)}) collective-permute-start(f32[128,128]{1,0:T(8,128)S(1)} %get-tuple-element.224), channel_id=1, source_target_pairs={{7,0},{6,1},{5,2},{4,3},{3,4},{2,5},{1,6},{0,7},{15,8},{14,9},{13,... | collective-permute-start | bytes 196616 | tf_op jit(solution)/shard_map/ppermute | solution.py:483
  52.1 6.3 %collective-permute-start.18 = (f32[128,128]{1,0:T(8,128)S(1)}, f32[128,128]{1,0:T(8,128)S(1)}, u32[]{:S(2)}, u32[]{:S(2)}) collective-permute-start(f32[128,128]{1,0:T(8,128)S(1)} %get-tuple-element.246), channel_id=1, source_target_pairs={{16,0},{17,1},{18,2},{19,3},{20,4},{21,5},{22,6},{23,7},{24,8},{25... | collective-permute-start | bytes 196616 | tf_op jit(solution)/shard_map/ppermute | solution.py:483
  52.9 5.4 %collective-permute-start.17 = (f32[128,128]{1,0:T(8,128)S(1)}, f32[128,128]{1,0:T(8,128)S(1)}, u32[]{:S(2)}, u32[]{:S(2)}) collective-permute-start(f32[128,128]{1,0:T(8,128)S(1)} %get-tuple-element.246), channel_id=1, source_target_pairs={{9,0},{8,1},{11,2},{10,3},{13,4},{12,5},{15,6},{14,7},{17,8},{16,9... | collective-permute-start | bytes 196616 | tf_op jit(solution)/shard_map/ppermute | solution.py:483
  58.4 6.4 %collective-permute-start.19 = (f32[128,128]{1,0:T(8,128)S(1)}, f32[128,128]{1,0:T(8,128)S(1)}, u32[]{:S(2)}, u32[]{:S(2)}) collective-permute-start(f32[128,128]{1,0:T(8,128)S(1)} %get-tuple-element.266), channel_id=1, source_target_pairs={{4,0},{5,1},{6,2},{7,3},{0,4},{1,5},{2,6},{3,7},{12,8},{13,9},{14,... | collective-permute-start | bytes 196616 | tf_op jit(solution)/shard_map/ppermute | solution.py:483
  59.1 5.8 %collective-permute-start.20 = (f32[128,128]{1,0:T(8,128)S(1)}, f32[128,128]{1,0:T(8,128)S(1)}, u32[]{:S(2)}, u32[]{:S(2)}) collective-permute-start(f32[128,128]{1,0:T(8,128)S(1)} %get-tuple-element.267), channel_id=1, source_target_pairs={{3,0},{2,1},{1,2},{0,3},{7,4},{6,5},{5,6},{4,7},{11,8},{10,9},{9,1... | collective-permute-start | bytes 196616 | tf_op jit(solution)/shard_map/ppermute | solution.py:483
  60.6 5.0 %collective-permute-start.21 = (f32[128,128]{1,0:T(8,128)S(1)}, f32[128,128]{1,0:T(8,128)S(1)}, u32[]{:S(2)}, u32[]{:S(2)}) collective-permute-start(f32[128,128]{1,0:T(8,128)S(1)} %get-tuple-element.268), channel_id=1, source_target_pairs={{7,0},{6,1},{5,2},{4,3},{3,4},{2,5},{1,6},{0,7},{15,8},{14,9},{13,... | collective-permute-start | bytes 196616 | tf_op jit(solution)/shard_map/ppermute | solution.py:483
  65.7 1.7 %collective-permute-start.22 = (f32[512,128]{1,0:T(8,128)S(1)}, f32[512,128]{1,0:T(8,128)S(1)}, u32[]{:S(2)}, u32[]{:S(2)}) collective-permute-start(f32[512,128]{1,0:T(8,128)S(1)} %get-tuple-element.284), channel_id=1, source_target_pairs={{1,0},{0,1},{3,2},{2,3},{5,4},{4,5},{7,6},{6,7},{9,8},{8,9},{11,10... | collective-permute-start | bytes 786440 | tf_op jit(solution)/shard_map/ppermute | solution.py:483
  (3 other events, 6.5 us)

commit v7 on v5

--- a/solution.py
+++ b/solution.py
@@ -616,7 +616,7 @@
     )
     others = [
         lax.ppermute(sums, "head", [(i, i ^ flip) for i in range(lax.axis_size("head"))])
-        for flip in FLIPS
+        for flip in FLIPS[::-1]
     ]
     grad_other, other, inverse, dots = call(
         grad_kernel,

time: 68.7 us -> 69.1 us (level)
  transfers between devices with their start and end apart: 23 -> 23, of which waited for: 14 -> 15; matrix products, arithmetic and copies ran while one was open for 0% -> 0% of each run, Pallas kernels for 22% -> 22%
where the time goes in v7:
time: 69.1 us; the launch traced here: 68.9 us
  starting transfers between devices  29.4 us (43%)
  Pallas kernels  20.6 us (30%)
  waiting for transfers between devices  16.6 us (24%)
  local copies, waits for them, and re-layouts  1.24 us (2%)
  between operations  1.08 us (2%)
    ppermute x20, starting transfers between devices, move(): return lax.ppermute(values, 'ctx', [(source(i), i) for i in range(devices)])  25.7 us
    pallas_call x25, Pallas kernels, call(): pl.pallas_call(lambda *refs: body(*refs, **fixed), name=name, in_specs=in...  20.6 us
    ppermute x20, waiting for transfers between devices, move(): return lax.ppermute(values, 'ctx', [(source(i), i) for i in range(devices)])  13.5 us
    ppermute x3, starting transfers between devices, on_device(): lax.ppermute(sums, 'head', [(i, i ^ flip) for i in range(lax.axis_size('h...  3.68 us
    ppermute x3, waiting for transfers between devices, on_device(): lax.ppermute(sums, 'head', [(i, i ^ flip) for i in range(lax.axis_size('h...  3.11 us
  transfers between devices with their start and end apart: 23, of which 15 were waited for; matrix products, arithmetic and copies ran while one was open for 0% of the time, Pallas kernels for 22%

profile of v7, /device:TPU:1, one launch (start us, length us, event | category | flops | bytes accessed | tf_op | source)
XLA Modules:
  0.0 68.9 jit_solution(2043650500556221046)
XLA Ops:
  1.3 1.8 %states.1 = (f32[512,128]{1,0:T(8,128)S(1)}, f32[40,128]{1,0:T(8,128)S(1)}, bf16[512,1024]{1,0:T(8,128)(2,1)S(1)}, bf16[512,1024]{1,0:T(8,128)(2,1)S(1)}) custom-call(s32[8]{0:T(128)S(1)} %copy-done.3, bf16[512,1024]{1,0:T(8,128)(2,1)} %refs_1_.3, bf16[512,1024]{1,0:T(8,128)(2,1)} %refs_2_.2), custom_call_target="tpu_custom_call" | custom-call | flops 67108864 | bytes 4476960 | tf_op jit(solution)/shard_map/states/pallas_call | solution.py:463
  3.1 1.5 %collective-permute-start = (f32[512,128]{1,0:T(8,128)S(1)}, f32[512,128]{1,0:T(8,128)S(1)}, u32[]{:S(2)}, u32[]{:S(2)}) collective-permute-start(f32[512,128]{1,0:T(8,128)S(1)} %get-tuple-element.155), channel_id=1, source_target_pairs={{1,0},{0,1},{3,2},{2,3},{5,4},{4,5},{7,6},{6,7},{9,8},{8,9},{11,10... | collective-permute-start | bytes 786440 | tf_op jit(solution)/shard_map/ppermute | solution.py:478
  5.8 3.1 %collective-permute-start.1 = (f32[128,128]{1,0:T(8,128)S(1)}, f32[128,128]{1,0:T(8,128)S(1)}, u32[]{:S(2)}, u32[]{:S(2)}) collective-permute-start(f32[128,128]{1,0:T(8,128)S(1)} %get-tuple-element.164), channel_id=1, source_target_pairs={{4,0},{5,1},{6,2},{7,3},{0,4},{1,5},{2,6},{3,7},{12,8},{13,9},{14,... | collective-permute-start | bytes 196616 | tf_op jit(solution)/shard_map/ppermute | solution.py:478
  10.3 1.5 %local_mix.2.refs_2_ = f32[512,512]{1,0:T(8,128)S(1)} custom-call(bf16[512,1024]{1,0:T(8,128)(2,1)S(1)} %copy-done, bf16[512,1024]{1,0:T(8,128)(2,1)S(1)} %get-tuple-element.287.refs_1_.refs_2_, bf16[512,1024]{1,0:T(8,128)(2,1)S(1)} %get-tuple-element.288.refs_2_.refs_3_, bf16[512,512]{1,0:T(8,128)(2,1)S(1)} %pair_mask.1.refs_3_.refs_4_), custom_call_target="tpu_custom_call" | custom-call | flops 402653184 | bytes 4718592 | tf_op jit(solution)/shard_map/local_mix/pallas_call | solution.py:463
  11.8 1.8 %collective-permute-done.2.refs_3_ = f32[128,128]{1,0:T(8,128)S(1)} collective-permute-done((f32[128,128]{1,0:T(8,128)S(1)}, f32[128,128]{1,0:T(8,128)S(1)}, u32[]{:S(2)}, u32[]{:S(2)}) %collective-permute-start.2) | collective-permute-done | bytes 65568 | tf_op jit(solution)/shard_map/ppermute | solution.py:478
  14.8 3.7 %collective-permute-start.5 = (f32[128,128]{1,0:T(8,128)S(1)}, f32[128,128]{1,0:T(8,128)S(1)}, u32[]{:S(2)}, u32[]{:S(2)}) collective-permute-start(f32[128,128]{1,0:T(8,128)S(1)} %get-tuple-element.174), channel_id=1, source_target_pairs={{16,0},{17,1},{18,2},{19,3},{20,4},{21,5},{22,6},{23,7},{24,8},{25... | collective-permute-start | bytes 196616 | tf_op jit(solution)/shard_map/ppermute | solution.py:478
  19.2 1.4 %local_mix.3.refs_2_ = f32[512,512]{1,0:T(8,128)S(1)} custom-call(bf16[512,1024]{1,0:T(8,128)(2,1)S(1)} %copy-done, bf16[512,1024]{1,0:T(8,128)(2,1)S(1)} %get-tuple-element.287.refs_1_.refs_2_, bf16[512,1024]{1,0:T(8,128)(2,1)S(1)} %get-tuple-element.288.refs_2_.refs_3_, bf16[512,512]{1,0:T(8,128)(2,1)S(1)} %pair_mask.1.refs_3_.refs_4_), custom_call_target="tpu_custom_call" | custom-call | flops 402653184 | bytes 4718592 | tf_op jit(solution)/shard_map/local_mix/pallas_call | solution.py:463
  21.1 2.4 %collective-permute-done.4.refs_2_ = f32[128,128]{1,0:T(8,128)S(1)} collective-permute-done((f32[128,128]{1,0:T(8,128)S(1)}, f32[128,128]{1,0:T(8,128)S(1)}, u32[]{:S(2)}, u32[]{:S(2)}) %collective-permute-start.4) | collective-permute-done | bytes 65568 | tf_op jit(solution)/shard_map/ppermute | solution.py:478
  23.6 1.8 %collective-permute-start.6 = (f32[128,128]{1,0:T(8,128)S(1)}, f32[128,128]{1,0:T(8,128)S(1)}, u32[]{:S(2)}, u32[]{:S(2)}) collective-permute-start(f32[128,128]{1,0:T(8,128)S(1)} %get-tuple-element.184), channel_id=1, source_target_pairs={{4,0},{5,1},{6,2},{7,3},{0,4},{1,5},{2,6},{3,7},{12,8},{13,9},{14,... | collective-permute-start | bytes 196616 | tf_op jit(solution)/shard_map/ppermute | solution.py:478
  25.4 1.3 %collective-permute-start.7 = (f32[128,128]{1,0:T(8,128)S(1)}, f32[128,128]{1,0:T(8,128)S(1)}, u32[]{:S(2)}, u32[]{:S(2)}) collective-permute-start(f32[128,128]{1,0:T(8,128)S(1)} %get-tuple-element.185), channel_id=1, source_target_pairs={{3,0},{2,1},{1,2},{0,3},{7,4},{6,5},{5,6},{4,7},{11,8},{10,9},{9,1... | collective-permute-start | bytes 196616 | tf_op jit(solution)/shard_map/ppermute | solution.py:478
  27.2 1.5 %collective-permute-done.6.refs_4_ = f32[128,128]{1,0:T(8,128)S(1)} collective-permute-done((f32[128,128]{1,0:T(8,128)S(1)}, f32[128,128]{1,0:T(8,128)S(1)}, u32[]{:S(2)}, u32[]{:S(2)}) %collective-permute-start.6) | collective-permute-done | bytes 65568 | tf_op jit(solution)/shard_map/ppermute | solution.py:478
  28.7 1.7 %collective-permute-done.7.refs_5_ = f32[128,128]{1,0:T(8,128)S(1)} collective-permute-done((f32[128,128]{1,0:T(8,128)S(1)}, f32[128,128]{1,0:T(8,128)S(1)}, u32[]{:S(2)}, u32[]{:S(2)}) %collective-permute-start.7) | collective-permute-done | bytes 65568 | tf_op jit(solution)/shard_map/ppermute | solution.py:478
  34.0 2.8 %collective-permute-start.12 = (f32[2,512]{1,0:T(2,128)S(1)}, f32[2,512]{1,0:T(2,128)S(1)}, u32[]{:S(2)}, u32[]{:S(2)}) collective-permute-start(f32[2,512]{1,0:T(2,128)S(1)} %get-tuple-element.206.refs_5_), channel_id=1, source_target_pairs={{0,64},{32,96},{64,0},{96,32},{1,65},{33,97},{65,1},{97,33},{2,66}... | collective-permute-start | bytes 12296 | tf_op jit(solution)/shard_map/ppermute | solution.py:618
  39.3 1.5 %collective-permute-done.10.refs_6_ = f32[2,512]{1,0:T(2,128)S(1)} collective-permute-done((f32[2,512]{1,0:T(2,128)S(1)}, f32[2,512]{1,0:T(2,128)S(1)}, u32[]{:S(2)}, u32[]{:S(2)}) %collective-permute-start.10) | collective-permute-done | bytes 4128 | tf_op jit(solution)/shard_map/ppermute | solution.py:618
  41.6 1.9 %collective-permute-start.13 = (f32[512,128]{1,0:T(8,128)S(1)}, f32[512,128]{1,0:T(8,128)S(1)}, u32[]{:S(2)}, u32[]{:S(2)}) collective-permute-start(f32[512,128]{1,0:T(8,128)S(1)} %get-tuple-element.207), channel_id=1, source_target_pairs={{1,0},{0,1},{3,2},{2,3},{5,4},{4,5},{7,6},{6,7},{9,8},{8,9},{11,10... | collective-permute-start | bytes 786440 | tf_op jit(solution)/shard_map/ppermute | solution.py:478
  47.0 1.3 %collective-permute-start.16 = (f32[128,128]{1,0:T(8,128)S(1)}, f32[128,128]{1,0:T(8,128)S(1)}, u32[]{:S(2)}, u32[]{:S(2)}) collective-permute-start(f32[128,128]{1,0:T(8,128)S(1)} %get-tuple-element.224), channel_id=1, source_target_pairs={{7,0},{6,1},{5,2},{4,3},{3,4},{2,5},{1,6},{0,7},{15,8},{14,9},{13,... | collective-permute-start | bytes 196616 | tf_op jit(solution)/shard_map/ppermute | solution.py:478
  49.7 1.8 %local_back.4 = (bf16[512,256]{1,0:T(8,128)(2,1)S(1)}, f32[512,256]{1,0:T(8,128)S(1)}, f32[512,256]{1,0:T(8,128)S(1)}) custom-call(f32[40,128]{1,0:T(8,128)S(1)} %get-tuple-element.286.refs_0_, bf16[512,1024]{1,0:T(8,128)(2,1)S(1)} %copy-done, bf16[512,1024]{1,0:T(8,128)(2,1)S(1)} %get-tuple-element.287.refs_1_.refs_2_, ...), custom_call_target="tpu_custom_call" | custom-call | flops 570425344 | bytes 5787648 | tf_op jit(solution)/shard_map/local_back/pallas_call | solution.py:463
  53.0 1.5 %collective-permute-start.17 = (f32[128,128]{1,0:T(8,128)S(1)}, f32[128,128]{1,0:T(8,128)S(1)}, u32[]{:S(2)}, u32[]{:S(2)}) collective-permute-start(f32[128,128]{1,0:T(8,128)S(1)} %get-tuple-element.246), channel_id=1, source_target_pairs={{9,0},{8,1},{11,2},{10,3},{13,4},{12,5},{15,6},{14,7},{17,8},{16,9... | collective-permute-start | bytes 196616 | tf_op jit(solution)/shard_map/ppermute | solution.py:478
  54.5 1.8 %local_back.5 = (bf16[512,256]{1,0:T(8,128)(2,1)S(1)}, f32[512,256]{1,0:T(8,128)S(1)}, f32[512,256]{1,0:T(8,128)S(1)}) custom-call(f32[40,128]{1,0:T(8,128)S(1)} %get-tuple-element.286.refs_0_, bf16[512,1024]{1,0:T(8,128)(2,1)S(1)} %copy-done, bf16[512,1024]{1,0:T(8,128)(2,1)S(1)} %get-tuple-element.287.refs_1_.refs_2_, ...), custom_call_target="tpu_custom_call" | custom-call | flops 570425344 | bytes 5787648 | tf_op jit(solution)/shard_map/local_back/pallas_call | solution.py:463
  56.2 1.8 %local_back.6 = (bf16[512,256]{1,0:T(8,128)(2,1)S(1)}, f32[512,256]{1,0:T(8,128)S(1)}, f32[512,256]{1,0:T(8,128)S(1)}) custom-call(f32[40,128]{1,0:T(8,128)S(1)} %get-tuple-element.286.refs_0_, bf16[512,1024]{1,0:T(8,128)(2,1)S(1)} %copy-done, bf16[512,1024]{1,0:T(8,128)(2,1)S(1)} %get-tuple-element.287.refs_1_.refs_2_, ...), custom_call_target="tpu_custom_call" | custom-call | flops 570425344 | bytes 5787648 | tf_op jit(solution)/shard_map/local_back/pallas_call | solution.py:463
  58.9 1.7 %collective-permute-start.20 = (f32[128,128]{1,0:T(8,128)S(1)}, f32[128,128]{1,0:T(8,128)S(1)}, u32[]{:S(2)}, u32[]{:S(2)}) collective-permute-start(f32[128,128]{1,0:T(8,128)S(1)} %get-tuple-element.267), channel_id=1, source_target_pairs={{3,0},{2,1},{1,2},{0,3},{7,4},{6,5},{5,6},{4,7},{11,8},{10,9},{9,1... | collective-permute-start | bytes 196616 | tf_op jit(solution)/shard_map/ppermute | solution.py:478
  61.7 1.8 %local_back.7 = (bf16[512,256]{1,0:T(8,128)(2,1)S(1)}, f32[512,256]{1,0:T(8,128)S(1)}, f32[512,256]{1,0:T(8,128)S(1)}) custom-call(f32[40,128]{1,0:T(8,128)S(1)} %get-tuple-element.286.refs_0_, bf16[512,1024]{1,0:T(8,128)(2,1)S(1)} %copy-done, bf16[512,1024]{1,0:T(8,128)(2,1)S(1)} %get-tuple-element.287.refs_1_.refs_2_, ...), custom_call_target="tpu_custom_call" | custom-call | flops 570425344 | bytes 5787648 | tf_op jit(solution)/shard_map/local_back/pallas_call | solution.py:463
  65.8 1.5 %own_final.1 = (bf16[512,1024]{1,0:T(8,128)(2,1)}, bf16[512,1024]{1,0:T(8,128)(2,1)}) custom-call(f32[40,128]{1,0:T(8,128)S(1)} %get-tuple-element.286.refs_0_, bf16[512,1024]{1,0:T(8,128)(2,1)S(1)} %get-tuple-element.287.refs_1_.refs_2_, bf16[512,1024]{1,0:T(8,128)(2,1)S(1)} %get-tuple-element.288.refs_2_.refs_3_, ...), custom_call_target="tpu_custom_call" | custom-call | flops 268435456 | bytes 6574080 | tf_op jit(solution)/shard_map/own_final/pallas_call | solution.py:463
  67.3 1.5 %back_states.1 = (bf16[512,1024]{1,0:T(8,128)(2,1)}, bf16[512,1024]{1,0:T(8,128)(2,1)}) custom-call(f32[40,128]{1,0:T(8,128)S(1)} %get-tuple-element.286.refs_0_, bf16[512,1024]{1,0:T(8,128)(2,1)S(1)} %get-tuple-element.287.refs_1_.refs_2_, bf16[512,1024]{1,0:T(8,128)(2,1)S(1)} %get-tuple-element.288.refs_2_.refs_3_, ...), custom_call_target="tpu_custom_call", output_to_operand_aliasing={{0}: (8, {}), {1}: (9, {})} | custom-call | flops 268435456 | bytes 8671232 | tf_op jit(solution)/shard_map/back_states/pallas_call | solution.py:463
  (55 shorter events, 23.5 us)
Async XLA Ops:
  3.1 2.7 %collective-permute-start = (f32[512,128]{1,0:T(8,128)S(1)}, f32[512,128]{1,0:T(8,128)S(1)}, u32[]{:S(2)}, u32[]{:S(2)}) collective-permute-start(f32[512,128]{1,0:T(8,128)S(1)} %get-tuple-element.155), channel_id=1, source_target_pairs={{1,0},{0,1},{3,2},{2,3},{5,4},{4,5},{7,6},{6,7},{9,8},{8,9},{11,10... | collective-permute-start | bytes 786440 | tf_op jit(solution)/shard_map/ppermute | solution.py:478
  5.8 5.9 %collective-permute-start.1 = (f32[128,128]{1,0:T(8,128)S(1)}, f32[128,128]{1,0:T(8,128)S(1)}, u32[]{:S(2)}, u32[]{:S(2)}) collective-permute-start(f32[128,128]{1,0:T(8,128)S(1)} %get-tuple-element.164), channel_id=1, source_target_pairs={{4,0},{5,1},{6,2},{7,3},{0,4},{1,5},{2,6},{3,7},{12,8},{13,9},{14,... | collective-permute-start | bytes 196616 | tf_op jit(solution)/shard_map/ppermute | solution.py:478
  8.9 4.7 %collective-permute-start.2 = (f32[128,128]{1,0:T(8,128)S(1)}, f32[128,128]{1,0:T(8,128)S(1)}, u32[]{:S(2)}, u32[]{:S(2)}) collective-permute-start(f32[128,128]{1,0:T(8,128)S(1)} %get-tuple-element.165), channel_id=1, source_target_pairs={{3,0},{2,1},{1,2},{0,3},{7,4},{6,5},{5,6},{4,7},{11,8},{10,9},{9,1... | collective-permute-start | bytes 196616 | tf_op jit(solution)/shard_map/ppermute | solution.py:478
  9.8 4.9 %collective-permute-start.3 = (f32[128,128]{1,0:T(8,128)S(1)}, f32[128,128]{1,0:T(8,128)S(1)}, u32[]{:S(2)}, u32[]{:S(2)}) collective-permute-start(f32[128,128]{1,0:T(8,128)S(1)} %get-tuple-element.166), channel_id=1, source_target_pairs={{7,0},{6,1},{5,2},{4,3},{3,4},{2,5},{1,6},{0,7},{15,8},{14,9},{13,... | collective-permute-start | bytes 196616 | tf_op jit(solution)/shard_map/ppermute | solution.py:478
  14.8 6.3 %collective-permute-start.5 = (f32[128,128]{1,0:T(8,128)S(1)}, f32[128,128]{1,0:T(8,128)S(1)}, u32[]{:S(2)}, u32[]{:S(2)}) collective-permute-start(f32[128,128]{1,0:T(8,128)S(1)} %get-tuple-element.174), channel_id=1, source_target_pairs={{16,0},{17,1},{18,2},{19,3},{20,4},{21,5},{22,6},{23,7},{24,8},{25... | collective-permute-start | bytes 196616 | tf_op jit(solution)/shard_map/ppermute | solution.py:478
  18.5 5.1 %collective-permute-start.4 = (f32[128,128]{1,0:T(8,128)S(1)}, f32[128,128]{1,0:T(8,128)S(1)}, u32[]{:S(2)}, u32[]{:S(2)}) collective-permute-start(f32[128,128]{1,0:T(8,128)S(1)} %get-tuple-element.174), channel_id=1, source_target_pairs={{25,0},{24,1},{27,2},{26,3},{29,4},{28,5},{31,6},{30,7},{1,8},{0,9... | collective-permute-start | bytes 196616 | tf_op jit(solution)/shard_map/ppermute | solution.py:478
  20.7 11.1 %copy-start.1 = (bf16[512,1024]{1,0:T(8,128)(2,1)S(1)}, bf16[512,1024]{1,0:T(8,128)(2,1)}, u32[]{:S(2)}) copy-start(bf16[512,1024]{1,0:T(8,128)(2,1)} %refs_2_.4) | copy-start | bytes 3145732
  23.6 5.1 %collective-permute-start.6 = (f32[128,128]{1,0:T(8,128)S(1)}, f32[128,128]{1,0:T(8,128)S(1)}, u32[]{:S(2)}, u32[]{:S(2)}) collective-permute-start(f32[128,128]{1,0:T(8,128)S(1)} %get-tuple-element.184), channel_id=1, source_target_pairs={{4,0},{5,1},{6,2},{7,3},{0,4},{1,5},{2,6},{3,7},{12,8},{13,9},{14,... | collective-permute-start | bytes 196616 | tf_op jit(solution)/shard_map/ppermute | solution.py:478
  25.4 5.0 %collective-permute-start.7 = (f32[128,128]{1,0:T(8,128)S(1)}, f32[128,128]{1,0:T(8,128)S(1)}, u32[]{:S(2)}, u32[]{:S(2)}) collective-permute-start(f32[128,128]{1,0:T(8,128)S(1)} %get-tuple-element.185), channel_id=1, source_target_pairs={{3,0},{2,1},{1,2},{0,3},{7,4},{6,5},{5,6},{4,7},{11,8},{10,9},{9,1... | collective-permute-start | bytes 196616 | tf_op jit(solution)/shard_map/ppermute | solution.py:478
  26.7 4.9 %collective-permute-start.8 = (f32[128,128]{1,0:T(8,128)S(1)}, f32[128,128]{1,0:T(8,128)S(1)}, u32[]{:S(2)}, u32[]{:S(2)}) collective-permute-start(f32[128,128]{1,0:T(8,128)S(1)} %get-tuple-element.186), channel_id=1, source_target_pairs={{7,0},{6,1},{5,2},{4,3},{3,4},{2,5},{1,6},{0,7},{15,8},{14,9},{13,... | collective-permute-start | bytes 196616 | tf_op jit(solution)/shard_map/ppermute | solution.py:478
  31.7 1.6 %collective-permute-start.9 = (f32[512,128]{1,0:T(8,128)S(1)}, f32[512,128]{1,0:T(8,128)S(1)}, u32[]{:S(2)}, u32[]{:S(2)}) collective-permute-start(f32[512,128]{1,0:T(8,128)S(1)} %get-tuple-element.190), channel_id=1, source_target_pairs={{1,0},{0,1},{3,2},{2,3},{5,4},{4,5},{7,6},{6,7},{9,8},{8,9},{11,10... | collective-permute-start | bytes 786440 | tf_op jit(solution)/shard_map/ppermute | solution.py:478
  34.0 4.0 %collective-permute-start.12 = (f32[2,512]{1,0:T(2,128)S(1)}, f32[2,512]{1,0:T(2,128)S(1)}, u32[]{:S(2)}, u32[]{:S(2)}) collective-permute-start(f32[2,512]{1,0:T(2,128)S(1)} %get-tuple-element.206.refs_5_), channel_id=1, source_target_pairs={{0,64},{32,96},{64,0},{96,32},{1,65},{33,97},{65,1},{97,33},{2,66}... | collective-permute-start | bytes 12296 | tf_op jit(solution)/shard_map/ppermute | solution.py:618
  36.8 2.5 %collective-permute-start.11 = (f32[2,512]{1,0:T(2,128)S(1)}, f32[2,512]{1,0:T(2,128)S(1)}, u32[]{:S(2)}, u32[]{:S(2)}) collective-permute-start(f32[2,512]{1,0:T(2,128)S(1)} %get-tuple-element.206.refs_5_), channel_id=1, source_target_pairs={{0,32},{32,0},{64,96},{96,64},{1,33},{33,1},{65,97},{97,65},{2,34}... | collective-permute-start | bytes 12296 | tf_op jit(solution)/shard_map/ppermute | solution.py:618
  37.1 3.7 %collective-permute-start.10 = (f32[2,512]{1,0:T(2,128)S(1)}, f32[2,512]{1,0:T(2,128)S(1)}, u32[]{:S(2)}, u32[]{:S(2)}) collective-permute-start(f32[2,512]{1,0:T(2,128)S(1)} %get-tuple-element.206.refs_5_), channel_id=1, source_target_pairs={{0,96},{32,64},{64,32},{96,0},{1,97},{33,65},{65,33},{97,1},{2,98}... | collective-permute-start | bytes 12296 | tf_op jit(solution)/shard_map/ppermute | solution.py:618
  41.6 3.1 %collective-permute-start.13 = (f32[512,128]{1,0:T(8,128)S(1)}, f32[512,128]{1,0:T(8,128)S(1)}, u32[]{:S(2)}, u32[]{:S(2)}) collective-permute-start(f32[512,128]{1,0:T(8,128)S(1)} %get-tuple-element.207), channel_id=1, source_target_pairs={{1,0},{0,1},{3,2},{2,3},{5,4},{4,5},{7,6},{6,7},{9,8},{8,9},{11,10... | collective-permute-start | bytes 786440 | tf_op jit(solution)/shard_map/ppermute | solution.py:478
  44.8 6.7 %collective-permute-start.14 = (f32[128,128]{1,0:T(8,128)S(1)}, f32[128,128]{1,0:T(8,128)S(1)}, u32[]{:S(2)}, u32[]{:S(2)}) collective-permute-start(f32[128,128]{1,0:T(8,128)S(1)} %get-tuple-element.222), channel_id=1, source_target_pairs={{4,0},{5,1},{6,2},{7,3},{0,4},{1,5},{2,6},{3,7},{12,8},{13,9},{14,... | collective-permute-start | bytes 196616 | tf_op jit(solution)/shard_map/ppermute | solution.py:478
  45.9 5.6 %collective-permute-start.15 = (f32[128,128]{1,0:T(8,128)S(1)}, f32[128,128]{1,0:T(8,128)S(1)}, u32[]{:S(2)}, u32[]{:S(2)}) collective-permute-start(f32[128,128]{1,0:T(8,128)S(1)} %get-tuple-element.223), channel_id=1, source_target_pairs={{3,0},{2,1},{1,2},{0,3},{7,4},{6,5},{5,6},{4,7},{11,8},{10,9},{9,1... | collective-permute-start | bytes 196616 | tf_op jit(solution)/shard_map/ppermute | solution.py:478
  47.0 5.1 %collective-permute-start.16 = (f32[128,128]{1,0:T(8,128)S(1)}, f32[128,128]{1,0:T(8,128)S(1)}, u32[]{:S(2)}, u32[]{:S(2)}) collective-permute-start(f32[128,128]{1,0:T(8,128)S(1)} %get-tuple-element.224), channel_id=1, source_target_pairs={{7,0},{6,1},{5,2},{4,3},{3,4},{2,5},{1,6},{0,7},{15,8},{14,9},{13,... | collective-permute-start | bytes 196616 | tf_op jit(solution)/shard_map/ppermute | solution.py:478
  52.2 5.9 %collective-permute-start.18 = (f32[128,128]{1,0:T(8,128)S(1)}, f32[128,128]{1,0:T(8,128)S(1)}, u32[]{:S(2)}, u32[]{:S(2)}) collective-permute-start(f32[128,128]{1,0:T(8,128)S(1)} %get-tuple-element.246), channel_id=1, source_target_pairs={{16,0},{17,1},{18,2},{19,3},{20,4},{21,5},{22,6},{23,7},{24,8},{25... | collective-permute-start | bytes 196616 | tf_op jit(solution)/shard_map/ppermute | solution.py:478
  53.0 5.1 %collective-permute-start.17 = (f32[128,128]{1,0:T(8,128)S(1)}, f32[128,128]{1,0:T(8,128)S(1)}, u32[]{:S(2)}, u32[]{:S(2)}) collective-permute-start(f32[128,128]{1,0:T(8,128)S(1)} %get-tuple-element.246), channel_id=1, source_target_pairs={{9,0},{8,1},{11,2},{10,3},{13,4},{12,5},{15,6},{14,7},{17,8},{16,9... | collective-permute-start | bytes 196616 | tf_op jit(solution)/shard_map/ppermute | solution.py:478
  58.1 6.4 %collective-permute-start.19 = (f32[128,128]{1,0:T(8,128)S(1)}, f32[128,128]{1,0:T(8,128)S(1)}, u32[]{:S(2)}, u32[]{:S(2)}) collective-permute-start(f32[128,128]{1,0:T(8,128)S(1)} %get-tuple-element.266), channel_id=1, source_target_pairs={{4,0},{5,1},{6,2},{7,3},{0,4},{1,5},{2,6},{3,7},{12,8},{13,9},{14,... | collective-permute-start | bytes 196616 | tf_op jit(solution)/shard_map/ppermute | solution.py:478
  58.9 5.6 %collective-permute-start.20 = (f32[128,128]{1,0:T(8,128)S(1)}, f32[128,128]{1,0:T(8,128)S(1)}, u32[]{:S(2)}, u32[]{:S(2)}) collective-permute-start(f32[128,128]{1,0:T(8,128)S(1)} %get-tuple-element.267), channel_id=1, source_target_pairs={{3,0},{2,1},{1,2},{0,3},{7,4},{6,5},{5,6},{4,7},{11,8},{10,9},{9,1... | collective-permute-start | bytes 196616 | tf_op jit(solution)/shard_map/ppermute | solution.py:478
  60.6 5.0 %collective-permute-start.21 = (f32[128,128]{1,0:T(8,128)S(1)}, f32[128,128]{1,0:T(8,128)S(1)}, u32[]{:S(2)}, u32[]{:S(2)}) collective-permute-start(f32[128,128]{1,0:T(8,128)S(1)} %get-tuple-element.268), channel_id=1, source_target_pairs={{7,0},{6,1},{5,2},{4,3},{3,4},{2,5},{1,6},{0,7},{15,8},{14,9},{13,... | collective-permute-start | bytes 196616 | tf_op jit(solution)/shard_map/ppermute | solution.py:478
  65.6 1.7 %collective-permute-start.22 = (f32[512,128]{1,0:T(8,128)S(1)}, f32[512,128]{1,0:T(8,128)S(1)}, u32[]{:S(2)}, u32[]{:S(2)}) collective-permute-start(f32[512,128]{1,0:T(8,128)S(1)} %get-tuple-element.284), channel_id=1, source_target_pairs={{1,0},{0,1},{3,2},{2,3},{5,4},{4,5},{7,6},{6,7},{9,8},{8,9},{11,10... | collective-permute-start | bytes 786440 | tf_op jit(solution)/shard_map/ppermute | solution.py:478
  (3 other events, 6.5 us)
